TPU v7x, 32 devices: a whole 2x2x4 slice. The times are simulated.
32 devices in a mesh: seq: 4 (over x, core), fsdp: 8 (over z, y).
Axes of the slice: x: 2, y: 2, z: 4, core: 2. Of those that a mesh axis runs over, the one named last changes fastest.
Arguments:
- tokens: bfloat16 [8, 2048, 768], P('fsdp', 'seq'), may hold values from -6 to 6
- encoder: bfloat16 [8, 512, 768], P('fsdp', 'seq'), may hold values from -6 to 6
- cotangent: bfloat16 [8, 2048, 768], P('fsdp', 'seq'), may hold values from -6 to 6
- lengths: int32 [8], P('fsdp'), may hold values from 512 to 2048, as said below
- gains: float32 [3, 768], P(None, ('seq', 'fsdp')), may hold values from 0.5 to 1.5
- self_query: float32 [768, 768], P(('seq', 'fsdp')), may hold values from -0.0546875 to 0.0546875
- self_key: float32 [768, 768], P(('seq', 'fsdp')), may hold values from -0.21875 to 0.21875
- self_value: float32 [768, 768], P(('seq', 'fsdp')), may hold values from -0.21875 to 0.21875
- self_output: float32 [768, 768], P(('seq', 'fsdp')), may hold values from -0.875 to 0.875
- cross_query: float32 [768, 768], P(('seq', 'fsdp')), may hold values from -0.0546875 to 0.0546875
- cross_key: float32 [768, 768], P(('seq', 'fsdp')), may hold values from -0.21875 to 0.21875
- cross_value: float32 [768, 768], P(('seq', 'fsdp')), may hold values from -0.21875 to 0.21875
- cross_output: float32 [768, 768], P(('seq', 'fsdp')), may hold values from -0.875 to 0.875
- ffn_gate: float32 [768, 2048], P(('seq', 'fsdp')), may hold values from -0.21875 to 0.21875
- ffn_up: float32 [768, 2048], P(('seq', 'fsdp')), may hold values from -0.21875 to 0.21875
- ffn_down: float32 [2048, 768], P(('seq', 'fsdp')), may hold values from -0.125 to 0.125
- rel_bias: float32 [32, 12], P(None, 'seq'), may hold values from -4 to 4
Outputs:
- output: bfloat16 [8, 2048, 768], P('fsdp', 'seq')
- input_grad: float32 [8, 2048, 768], P('fsdp', 'seq')
- encoder_grad: float32 [8, 512, 768], P('fsdp', 'seq')
- gains_grad: float32 [3, 768], P(None, ('seq', 'fsdp'))
- self_query_grad: float32 [768, 768], P(('seq', 'fsdp'))
- self_key_grad: float32 [768, 768], P(('seq', 'fsdp'))
- self_value_grad: float32 [768, 768], P(('seq', 'fsdp'))
- self_output_grad: float32 [768, 768], P(('seq', 'fsdp'))
- cross_query_grad: float32 [768, 768], P(('seq', 'fsdp'))
- cross_key_grad: float32 [768, 768], P(('seq', 'fsdp'))
- cross_value_grad: float32 [768, 768], P(('seq', 'fsdp'))
- cross_output_grad: float32 [768, 768], P(('seq', 'fsdp'))
- ffn_gate_grad: float32 [768, 2048], P(('seq', 'fsdp'))
- ffn_up_grad: float32 [768, 2048], P(('seq', 'fsdp'))
- ffn_down_grad: float32 [2048, 768], P(('seq', 'fsdp'))
- rel_bias_grad: float32 [32, 12], P(None, 'seq')
Inputs may be any that keep to these rules, and one draw needn't show every extreme that they name: Slot s holds one sequence in its first lengths[s] positions; the rest is padding. Some slot is full.
All inputs are finite; a program needn't handle non-finite values.
Results may differ from a plain program's by a relative error of at most 0.025.
The roundings to bfloat16 on the way count: a program that leaves them out, or rounds other values in their place, can miss the bound.
Values may be sent and summed in bfloat16 or wider, within the bound.
A program may use at most 192 MiB of HBM per device.

v0:
```python
import jax
import jax.numpy as jnp
import numpy as np
from jax import lax
from jax.sharding import PartitionSpec as P

HEAD = 64


epsilon = 1e-06
negative = -1e30
highest = lax.Precision.HIGHEST
bounds = np.ceil(16.0 * 8.0 ** (np.arange(1, 16) / 16.0)).astype(np.int32)
band_width = 128


def buckets(distance):
    far = 16 + jnp.sum((distance[..., None] >= jnp.asarray(bounds)).astype(jnp.int32), axis=-1)
    return jnp.where(distance < 16, distance, far)


def matmul(left, right):
    return jnp.dot(left, right, preferred_element_type=jnp.float32)


def matmul_t(left, right):
    return lax.dot_general(
        left, right, (((1,), (1,)), ((), ())), preferred_element_type=jnp.float32
    )


def inner_rows(left, right):
    return lax.dot_general(
        left, right, (((0,), (0,)), ((), ())), preferred_element_type=jnp.float32
    )


def rms_norm(values, gain):
    scale = lax.rsqrt(jnp.mean(values * values, axis=-1, keepdims=True) + epsilon)
    return values * scale * gain


def rms_back(values, gain, grad_normed):
    scale = lax.rsqrt(jnp.mean(values * values, axis=-1, keepdims=True) + epsilon)
    unit = values * scale
    grad_unit = grad_normed * gain
    grad_gain = jnp.sum(grad_normed * unit, axis=0)
    grad_values = scale * (grad_unit - unit * jnp.mean(grad_unit * unit, axis=-1, keepdims=True))
    return (grad_values, grad_gain)


def activate(gate, upper):
    return jax.nn.gelu(gate, approximate=True) * upper


def bucket_table(count, width):
    return (
        buckets(jnp.arange(count, dtype=jnp.int32))[:, None]
        == jnp.arange(width, dtype=jnp.int32)[None, :]
    ).astype(jnp.float32)


def band_window(table, block):
    width = block + band_width
    period = width + block
    places = jnp.arange(period, dtype=jnp.int32)
    shifts = jnp.where(places < width, places, places - period)
    distance = jnp.maximum(band_width - shifts, 0)
    onehot = (
        buckets(distance)[:, None] == jnp.arange(table.shape[0], dtype=jnp.int32)[None, :]
    ).astype(jnp.float32)
    values = jnp.dot(onehot, table, precision=highest).T
    heads = table.shape[1]
    tiled = jnp.tile(values, (1, block))[:, : block * (period - 1)]
    return tiled.reshape(heads, block, period - 1)[:, :, :width]


def block_scores(query_block, key_heads, start, position_bias):
    raw = jnp.einsum("qhd,khd->hqk", query_block, key_heads, preferred_element_type=jnp.float32)
    if position_bias is None:
        return raw
    window, far_bias, length = position_bias
    heads = raw.shape[0]
    block = query_block.shape[0]
    key_count = key_heads.shape[0]
    bias_base = jnp.broadcast_to(far_bias[:, None, None], (heads, block, key_count + band_width))
    bias_full = lax.dynamic_update_slice(bias_base, window, (0, 0, start))[:, :, band_width:]
    query_pos = start + jnp.arange(block, dtype=jnp.int32)
    key_pos = jnp.arange(key_count, dtype=jnp.int32)
    distance = query_pos[:, None] - key_pos[None, :]
    valid = (distance >= 0) & (key_pos[None, :] < length)
    return jnp.where(valid[None], raw + bias_full, negative)


def attend_forward(queries, key_rows, value_rows, position_bias):
    rows = queries.shape[0]
    heads = queries.shape[1] // HEAD
    block = min(512, rows)
    key_heads = key_rows.reshape(key_rows.shape[0], heads, HEAD)
    value_heads = value_rows.reshape(value_rows.shape[0], heads, HEAD)

    def one_block(number):
        start = number * block
        query_block = lax.dynamic_slice_in_dim(queries, start, block, 0).reshape(block, heads, HEAD)
        scores = block_scores(query_block, key_heads, start, position_bias)
        largest = jnp.max(scores, axis=-1, keepdims=True)
        expos = jnp.exp(scores - largest)
        totals = jnp.sum(expos, axis=-1, keepdims=True)
        weights = (expos / totals).astype(jnp.bfloat16)
        mixed = jnp.einsum("hqk,khd->qhd", weights, value_heads, preferred_element_type=jnp.float32)
        return (
            mixed.reshape(block, heads * HEAD).astype(jnp.bfloat16),
            (largest + jnp.log(totals))[..., 0],
        )

    mixed, logsum = lax.map(one_block, jnp.arange(rows // block))
    return (mixed.reshape(rows, heads * HEAD), logsum)


def attend_backward(queries, key_rows, value_rows, grad_mixed, logsum, position_bias, bucket_count):
    rows = queries.shape[0]
    heads = queries.shape[1] // HEAD
    block = min(512, rows)
    width = block + band_width
    key_count = key_rows.shape[0]
    key_heads = key_rows.reshape(key_count, heads, HEAD)
    value_heads = value_rows.reshape(key_count, heads, HEAD)
    near_map = bucket_table(band_width, bucket_count)
    last_row = (jnp.arange(bucket_count, dtype=jnp.int32) == bucket_count - 1).astype(jnp.float32)

    def one_block(carry, number):
        grad_keys, grad_values, grad_bias = carry
        start = number * block
        query_block = lax.dynamic_slice_in_dim(queries, start, block, 0).reshape(block, heads, HEAD)
        grad_block = lax.dynamic_slice_in_dim(grad_mixed, start, block, 0).reshape(
            block, heads, HEAD
        )
        scores = block_scores(query_block, key_heads, start, position_bias)
        weights = jnp.exp(scores - logsum[number][..., None])
        grad_weights = jnp.einsum(
            "qhd,khd->hqk", grad_block, value_heads, preferred_element_type=jnp.float32
        )
        grad_scores = weights * (
            grad_weights - jnp.sum(weights * grad_weights, axis=-1, keepdims=True)
        )
        if position_bias is not None:
            grad_padded = jnp.pad(grad_scores, ((0, 0), (0, 0), (band_width, 0)))
            grad_window = lax.dynamic_slice(grad_padded, (0, 0, start), (heads, block, width))
            skewed = jnp.pad(
                grad_window.reshape(heads, block * width), ((0, 0), (0, block))
            ).reshape(heads, block, width + 1)
            band_sums = jnp.sum(skewed[:, :, 1 : band_width + 1], axis=1)[:, ::-1]
            remote = jnp.sum(grad_scores, axis=(1, 2)) - jnp.sum(band_sums, axis=1)
            grad_bias = (
                grad_bias
                + jnp.dot(near_map.T, band_sums.T, precision=highest)
                + last_row[:, None] * remote[None, :]
            )
        low_scores = grad_scores.astype(jnp.bfloat16)
        grad_query = jnp.einsum(
            "hqk,khd->qhd", low_scores, key_heads, preferred_element_type=jnp.float32
        )
        grad_keys = grad_keys + jnp.einsum(
            "hqk,qhd->khd", low_scores, query_block, preferred_element_type=jnp.float32
        )
        grad_values = grad_values + jnp.einsum(
            "hqk,qhd->khd",
            weights.astype(jnp.bfloat16),
            grad_block,
            preferred_element_type=jnp.float32,
        )
        return (
            (grad_keys, grad_values, grad_bias),
            grad_query.reshape(block, heads * HEAD).astype(jnp.bfloat16),
        )

    start_carry = (
        jnp.zeros((key_count, heads, HEAD), jnp.float32),
        jnp.zeros((key_count, heads, HEAD), jnp.float32),
        jnp.zeros((bucket_count, heads), jnp.float32),
    )
    (grad_keys, grad_values, grad_bias), grad_query = lax.scan(
        one_block, start_carry, jnp.arange(rows // block)
    )
    return (
        grad_query.reshape(rows, heads * HEAD),
        grad_keys.reshape(key_count, heads * HEAD).astype(jnp.bfloat16),
        grad_values.reshape(key_count, heads * HEAD).astype(jnp.bfloat16),
        grad_bias,
    )


def per_device(
    tokens,
    encoder,
    cotangent,
    lengths,
    gains,
    self_query,
    self_key,
    self_value,
    self_output,
    cross_query,
    cross_key,
    cross_value,
    cross_output,
    ffn_gate,
    ffn_up,
    ffn_down,
    rel_bias,
):
    rounded = (
        lax.all_gather(gains.astype(jnp.bfloat16), ("seq", "fsdp"), axis=1, tiled=True),
        lax.all_gather(self_query.astype(jnp.bfloat16), ("seq", "fsdp"), axis=0, tiled=True),
        lax.all_gather(self_key.astype(jnp.bfloat16), ("seq", "fsdp"), axis=0, tiled=True),
        lax.all_gather(self_value.astype(jnp.bfloat16), ("seq", "fsdp"), axis=0, tiled=True),
        lax.all_gather(self_output.astype(jnp.bfloat16), ("seq", "fsdp"), axis=0, tiled=True),
        lax.all_gather(cross_query.astype(jnp.bfloat16), ("seq", "fsdp"), axis=0, tiled=True),
        lax.all_gather(cross_key.astype(jnp.bfloat16), ("seq", "fsdp"), axis=0, tiled=True),
        lax.all_gather(cross_value.astype(jnp.bfloat16), ("seq", "fsdp"), axis=0, tiled=True),
        lax.all_gather(cross_output.astype(jnp.bfloat16), ("seq", "fsdp"), axis=0, tiled=True),
        lax.all_gather(ffn_gate.astype(jnp.bfloat16), ("seq", "fsdp"), axis=0, tiled=True),
        lax.all_gather(ffn_up.astype(jnp.bfloat16), ("seq", "fsdp"), axis=0, tiled=True),
        lax.all_gather(ffn_down.astype(jnp.bfloat16), ("seq", "fsdp"), axis=0, tiled=True),
    )
    (
        gain_rows,
        w_query,
        w_key,
        w_value,
        w_output,
        c_query,
        c_key,
        c_value,
        c_output,
        w_gate,
        w_up,
        w_down,
    ) = rounded
    gain_float = gain_rows.astype(jnp.float32)
    length = lengths[0]
    inputs = tokens[0]
    encoded = encoder[0]
    rows = inputs.shape[0]
    values_in = inputs.astype(jnp.float32)
    bucket_count = rel_bias.shape[0]
    normed = rms_norm(values_in, gain_float[0]).astype(jnp.bfloat16)
    queries = matmul(normed, w_query).astype(jnp.bfloat16)
    key_rows = matmul(normed, w_key).astype(jnp.bfloat16)
    value_rows = matmul(normed, w_value).astype(jnp.bfloat16)
    cross_keys = matmul(encoded, c_key).astype(jnp.bfloat16)
    cross_values = matmul(encoded, c_value).astype(jnp.bfloat16)
    head_queries, head_keys, head_values, head_ckeys, head_cvalues = (
        lax.all_to_all(queries, "seq", split_axis=1, concat_axis=0, tiled=True),
        lax.all_to_all(key_rows, "seq", split_axis=1, concat_axis=0, tiled=True),
        lax.all_to_all(value_rows, "seq", split_axis=1, concat_axis=0, tiled=True),
        lax.all_to_all(cross_keys, "seq", split_axis=1, concat_axis=0, tiled=True),
        lax.all_to_all(cross_values, "seq", split_axis=1, concat_axis=0, tiled=True),
    )
    slot_rows = head_queries.shape[0]
    window = band_window(rel_bias, min(512, slot_rows))
    position_bias = (window, rel_bias[bucket_count - 1], length)
    self_mixed, self_logsum = attend_forward(head_queries, head_keys, head_values, position_bias)
    mixed = lax.all_to_all(self_mixed, "seq", split_axis=0, concat_axis=1, tiled=True)
    attended = values_in + matmul(mixed, w_output)
    normed_two = rms_norm(attended, gain_float[1]).astype(jnp.bfloat16)
    cross_queries = matmul(normed_two, c_query).astype(jnp.bfloat16)
    head_cqueries = lax.all_to_all(cross_queries, "seq", split_axis=1, concat_axis=0, tiled=True)
    cross_head_mixed, cross_logsum = attend_forward(head_cqueries, head_ckeys, head_cvalues, None)
    cross_mixed = lax.all_to_all(cross_head_mixed, "seq", split_axis=0, concat_axis=1, tiled=True)
    crossed = attended + matmul(cross_mixed, c_output)
    normed_three = rms_norm(crossed, gain_float[2]).astype(jnp.bfloat16)
    gate = matmul(normed_three, w_gate)
    upper = matmul(normed_three, w_up)
    hidden = activate(gate, upper).astype(jnp.bfloat16)
    result = crossed + matmul(hidden, w_down)
    again = (
        lax.all_gather(gains.astype(jnp.bfloat16), ("seq", "fsdp"), axis=1, tiled=True),
        lax.all_gather(self_query.astype(jnp.bfloat16), ("seq", "fsdp"), axis=0, tiled=True),
        lax.all_gather(self_key.astype(jnp.bfloat16), ("seq", "fsdp"), axis=0, tiled=True),
        lax.all_gather(self_value.astype(jnp.bfloat16), ("seq", "fsdp"), axis=0, tiled=True),
        lax.all_gather(self_output.astype(jnp.bfloat16), ("seq", "fsdp"), axis=0, tiled=True),
        lax.all_gather(cross_query.astype(jnp.bfloat16), ("seq", "fsdp"), axis=0, tiled=True),
        lax.all_gather(cross_key.astype(jnp.bfloat16), ("seq", "fsdp"), axis=0, tiled=True),
        lax.all_gather(cross_value.astype(jnp.bfloat16), ("seq", "fsdp"), axis=0, tiled=True),
        lax.all_gather(cross_output.astype(jnp.bfloat16), ("seq", "fsdp"), axis=0, tiled=True),
        lax.all_gather(ffn_gate.astype(jnp.bfloat16), ("seq", "fsdp"), axis=0, tiled=True),
        lax.all_gather(ffn_up.astype(jnp.bfloat16), ("seq", "fsdp"), axis=0, tiled=True),
        lax.all_gather(ffn_down.astype(jnp.bfloat16), ("seq", "fsdp"), axis=0, tiled=True),
    )
    (
        back_gains,
        b_query,
        b_key,
        b_value,
        b_output,
        bc_query,
        bc_key,
        bc_value,
        bc_output,
        b_gate,
        b_up,
        b_down,
    ) = again
    back_gain = back_gains.astype(jnp.float32)
    positions = lax.axis_index("seq") * rows + jnp.arange(rows, dtype=jnp.int32)
    grad_out = cotangent[0].astype(jnp.float32) * (positions < length).astype(jnp.float32)[:, None]
    grad_ffn = grad_out.astype(jnp.bfloat16)
    grad_down = inner_rows(hidden, grad_ffn)
    grad_hidden = matmul_t(grad_ffn, b_down)
    _, pullback = jax.vjp(activate, gate, upper)
    grad_gate_f, grad_upper_f = pullback(grad_hidden)
    grad_gate = grad_gate_f.astype(jnp.bfloat16)
    grad_upper = grad_upper_f.astype(jnp.bfloat16)
    grad_wgate = inner_rows(normed_three, grad_gate)
    grad_wup = inner_rows(normed_three, grad_upper)
    grad_normed_three = matmul_t(grad_gate, b_gate) + matmul_t(grad_upper, b_up)
    norm_part, grad_gain_two = rms_back(crossed, back_gain[2], grad_normed_three)
    grad_crossed = grad_out + norm_part
    grad_branch = grad_crossed.astype(jnp.bfloat16)
    grad_coutput = inner_rows(cross_mixed, grad_branch)
    grad_cmixed = matmul_t(grad_branch, bc_output).astype(jnp.bfloat16)
    head_grad_cmixed = lax.all_to_all(grad_cmixed, "seq", split_axis=1, concat_axis=0, tiled=True)
    head_dcq, head_dck, head_dcv, _ = attend_backward(
        head_cqueries, head_ckeys, head_cvalues, head_grad_cmixed, cross_logsum, None, bucket_count
    )
    grad_cq, grad_ck, grad_cv = (
        lax.all_to_all(head_dcq, "seq", split_axis=0, concat_axis=1, tiled=True),
        lax.all_to_all(head_dck, "seq", split_axis=0, concat_axis=1, tiled=True),
        lax.all_to_all(head_dcv, "seq", split_axis=0, concat_axis=1, tiled=True),
    )
    grad_cquery = inner_rows(normed_two, grad_cq)
    grad_ckey = inner_rows(encoded, grad_ck)
    grad_cvalue = inner_rows(encoded, grad_cv)
    grad_encoded = matmul_t(grad_ck, bc_key) + matmul_t(grad_cv, bc_value)
    norm_part, grad_gain_one = rms_back(attended, back_gain[1], matmul_t(grad_cq, bc_query))
    grad_attended = grad_crossed + norm_part
    grad_self_branch = grad_attended.astype(jnp.bfloat16)
    grad_output = inner_rows(mixed, grad_self_branch)
    grad_mixed = matmul_t(grad_self_branch, b_output).astype(jnp.bfloat16)
    head_grad_mixed = lax.all_to_all(grad_mixed, "seq", split_axis=1, concat_axis=0, tiled=True)
    head_dq, head_dk, head_dv, grad_table = attend_backward(
        head_queries,
        head_keys,
        head_values,
        head_grad_mixed,
        self_logsum,
        position_bias,
        bucket_count,
    )
    grad_q, grad_k, grad_v = (
        lax.all_to_all(head_dq, "seq", split_axis=0, concat_axis=1, tiled=True),
        lax.all_to_all(head_dk, "seq", split_axis=0, concat_axis=1, tiled=True),
        lax.all_to_all(head_dv, "seq", split_axis=0, concat_axis=1, tiled=True),
    )
    grad_query = inner_rows(normed, grad_q)
    grad_key = inner_rows(normed, grad_k)
    grad_value = inner_rows(normed, grad_v)
    grad_normed = matmul_t(grad_q, b_query) + matmul_t(grad_k, b_key) + matmul_t(grad_v, b_value)
    norm_part, grad_gain_zero = rms_back(values_in, back_gain[0], grad_normed)
    grad_input = grad_attended + norm_part
    grad_gains = jnp.stack([grad_gain_zero, grad_gain_one, grad_gain_two])
    shares = (
        lax.psum_scatter(grad_gains, ("seq", "fsdp"), scatter_dimension=1, tiled=True),
        lax.psum_scatter(grad_query, ("seq", "fsdp"), scatter_dimension=0, tiled=True),
        lax.psum_scatter(grad_key, ("seq", "fsdp"), scatter_dimension=0, tiled=True),
        lax.psum_scatter(grad_value, ("seq", "fsdp"), scatter_dimension=0, tiled=True),
        lax.psum_scatter(grad_output, ("seq", "fsdp"), scatter_dimension=0, tiled=True),
        lax.psum_scatter(grad_cquery, ("seq", "fsdp"), scatter_dimension=0, tiled=True),
        lax.psum_scatter(grad_ckey, ("seq", "fsdp"), scatter_dimension=0, tiled=True),
        lax.psum_scatter(grad_cvalue, ("seq", "fsdp"), scatter_dimension=0, tiled=True),
        lax.psum_scatter(grad_coutput, ("seq", "fsdp"), scatter_dimension=0, tiled=True),
        lax.psum_scatter(grad_wgate, ("seq", "fsdp"), scatter_dimension=0, tiled=True),
        lax.psum_scatter(grad_wup, ("seq", "fsdp"), scatter_dimension=0, tiled=True),
        lax.psum_scatter(grad_down, ("seq", "fsdp"), scatter_dimension=0, tiled=True),
    )
    table_grad = lax.psum(grad_table, "fsdp")
    return (
        result.astype(jnp.bfloat16)[None],
        grad_input[None],
        grad_encoded[None],
        shares[0],
        shares[1],
        shares[2],
        shares[3],
        shares[4],
        shares[5],
        shares[6],
        shares[7],
        shares[8],
        shares[9],
        shares[10],
        shares[11],
        table_grad,
    )


def solution(mesh):
    placed = (
        P("fsdp", "seq", None),
        P("fsdp", "seq", None),
        P("fsdp", "seq", None),
        P("fsdp"),
        P(None, ("seq", "fsdp")),
        P(("seq", "fsdp"), None),
        P(("seq", "fsdp"), None),
        P(("seq", "fsdp"), None),
        P(("seq", "fsdp"), None),
        P(("seq", "fsdp"), None),
        P(("seq", "fsdp"), None),
        P(("seq", "fsdp"), None),
        P(("seq", "fsdp"), None),
        P(("seq", "fsdp"), None),
        P(("seq", "fsdp"), None),
        P(("seq", "fsdp"), None),
        P(None, "seq"),
    )
    return jax.shard_map(
        per_device,
        mesh=mesh,
        in_specs=placed,
        out_specs=(
            P("fsdp", "seq", None),
            P("fsdp", "seq", None),
            P("fsdp", "seq", None),
            P(None, ("seq", "fsdp")),
            P(("seq", "fsdp"), None),
            P(("seq", "fsdp"), None),
            P(("seq", "fsdp"), None),
            P(("seq", "fsdp"), None),
            P(("seq", "fsdp"), None),
            P(("seq", "fsdp"), None),
            P(("seq", "fsdp"), None),
            P(("seq", "fsdp"), None),
            P(("seq", "fsdp"), None),
            P(("seq", "fsdp"), None),
            P(("seq", "fsdp"), None),
            P(None, "seq"),
        ),
        check_vma=False,
    )
```

profile of v0, /device:TPU:0, one launch (start us, length us, event | category | flops | bytes accessed | tf_op | source)
XLA Modules:
  0.0 1882.2 jit_solution(754934044320028863)
XLA Ops:
  21.6 69.9 %all-gather = bf16[32,24,3]{1,2,0:T(4,128)(2,1)S(1)} all-gather(bf16[1,24,3]{1,2,0:T(4,128)(2,1)S(1)} %convert_bitcast_fusion.1), channel_id=1, replica_groups=mesh['seq'=4,'fsdp'=8] {'seq','fsdp'}, dimensions={0}, use_global_device_ids=true | all-gather | bytes 4752 | tf_op jit(solution)/shard_map/all_gather | solution.py:213
  100.3 25.3 %all-gather.15.cloned.1.call-done = bf16[768,768]{1,0:T(8,128)(2,1)} async-done(((bf16[24,768]{1,0:T(8,128)(2,1)}), bf16[768,768]{1,0:T(8,128)(2,1)}) %all-gather.15.cloned.1.call-update) | async-done | bytes 1179664 | tf_op jit(solution)/shard_map/all_gather | solution.py:215
  133.1 49.0 %all-gather.13.cloned.1.call-done = bf16[768,768]{1,0:T(8,128)(2,1)} async-done(((bf16[24,768]{1,0:T(8,128)(2,1)}), bf16[768,768]{1,0:T(8,128)(2,1)}) %all-gather.13.cloned.1.call-update) | async-done | bytes 1179664 | tf_op jit(solution)/shard_map/all_gather | solution.py:214
  192.3 11.5 copy.194
  213.9 16.4 reshape.484
  240.3 93.8 %while.58 = (s32[]{:T(128)}, bf16[4,512,192]{1,2,0:T(8,128)(2,1)S(1)}, f32[4,3,512]{2,1,0:T(4,128)}, s32[4]{0:T(128)S(1)}, s32[]{:T(128)}, /*index=5*/bf16[2048,...) while((s32[]{:T(128)}, ...), condition=%wide.region_5.6_spmd, body=%wide.region_2.5_spmd.sunk | while | flops 833717248 | bytes 142534992 | solution.py:116
  362.4 47.0 %all-gather.21.cloned.1.call-done = bf16[768,768]{1,0:T(8,128)(2,1)} async-done(((bf16[24,768]{1,0:T(8,128)(2,1)}), bf16[768,768]{1,0:T(8,128)(2,1)}) %all-gather.21.cloned.1.call-update) | async-done | bytes 1179664 | tf_op jit(solution)/shard_map/all_gather | solution.py:218
  430.4 18.6 while.59
  454.2 12.2 all-gather.27.cloned.1.call-done
  471.1 57.4 %all-gather.31.cloned.1.call-done = bf16[768,2048]{1,0:T(8,128)(2,1)} async-done(((bf16[24,2048]{1,0:T(8,128)(2,1)}), bf16[768,2048]{1,0:T(8,128)(2,1)}) %all-gather.31.cloned.1.call-update) | async-done | bytes 3145744 | tf_op jit(solution)/shard_map/all_gather | solution.py:223
  534.4 55.3 %all-gather.29.cloned.1.call-done = bf16[768,2048]{1,0:T(8,128)(2,1)} async-done(((bf16[24,2048]{1,0:T(8,128)(2,1)}), bf16[768,2048]{1,0:T(8,128)(2,1)}) %all-gather.29.cloned.1.call-update) | async-done | bytes 3145744 | tf_op jit(solution)/shard_map/all_gather | solution.py:222
  595.6 55.5 %all-gather.33.cloned.1.call-done = bf16[2048,768]{1,0:T(8,128)(2,1)} async-done(((bf16[64,768]{1,0:T(8,128)(2,1)}), bf16[2048,768]{1,0:T(8,128)(2,1)}) %all-gather.33.cloned.1.call-update) | async-done | bytes 3145744 | tf_op jit(solution)/shard_map/all_gather | solution.py:224
  691.9 39.7 %while.60 = (s32[]{:T(128)}, f32[512,3,64]{0,2,1:T(8,128)S(1)}, f32[512,3,64]{0,2,1:T(8,128)S(1)}, bf16[4,512,192]{1,2,0:T(8,128)(2,1)}, s32[4]{0:T(128)S(1)}, /...) while((s32[]{:T(128)}, f32[512,3,64]{0,2,1:T(8,128)S(1)}, ...), condition=%wide.region_15.16_spmd.clone, body=%wide.region_13.15_spmd.clone.sunk | while | flops 510884352 | bytes 28748064 | solution.py:182
  758.8 15.6 all_to_all.270
  805.0 279.2 %while.61 = (s32[]{:T(128)}, f32[2048,3,64]{0,2,1:T(8,128)}, f32[2048,3,64]{0,2,1:T(8,128)}, f32[32,3]{0,1:T(4,128)S(1)}, bf16[4,512,192]{1,2,0:T(8,128)(2,1)}, ...) while((s32[]{:T(128)}, f32[2048,3,64]{0,2,1:T(8,128)}, ...), condition=%wide.region_23.24_spmd.clone, body=%wide.region_18.23_spmd.clone.sunk | while | flops 2053039488 | bytes 358221568 | solution.py:182
  836.5 11.2 fusion.281
  861.7 11.0 reshape.509
  905.9 11.4 fusion.281
  975.7 11.2 fusion.281
  1000.7 11.1 reshape.509
  1045.4 11.2 fusion.281
  1086.5 14.2 all_to_all.271
  1108.0 14.0 all_to_all.272
  1126.4 14.0 all_to_all.273
  1173.0 21.8 %psum.7 = f32[32,3]{0,1:T(4,128)} all-reduce(f32[32,3]{0,1:T(4,128)S(1)} %get-tuple-element.371), channel_id=1, replica_groups=mesh['seq'=4,'fsdp'=8] {'fsdp'}, use_global_device_ids=true, to_apply=%region_40.41 | all-reduce | flops 96 | bytes 768 | tf_op jit(solution)/shard_map/psum | solution.py:377
  1200.7 37.0 %all-reduce.2 = f32[3,768]{1,0:T(4,128)S(1)} all-reduce(f32[3,768]{1,0:T(4,128)S(1)} %pad_maximum_fusion), channel_id=2, replica_groups=mesh['seq'=4,'fsdp'=8] {'seq','fsdp'}, use_global_device_ids=true, to_apply=%region_28.29.clone | all-reduce | flops 2304 | bytes 18432
  1241.4 64.5 %reduce-scatter.21.cloned.1.call-done = f32[24,768]{1,0:T(8,128)} async-done(((f32[768,768]{1,0:T(8,128)}), f32[24,768]{1,0:T(8,128)}) %reduce-scatter.21.cloned.1.call-update) | async-done | bytes 73744 | tf_op jit(solution)/shard_map/reduce_scatter | solution.py:367
  1306.0 104.3 %reduce-scatter.19.cloned.1.call-done = f32[24,768]{1,0:T(8,128)} async-done(((f32[768,768]{1,0:T(8,128)}), f32[24,768]{1,0:T(8,128)}) %reduce-scatter.19.cloned.1.call-update) | async-done | bytes 73744 | tf_op jit(solution)/shard_map/reduce_scatter | solution.py:366
  1410.3 104.5 %reduce-scatter.17.cloned.1.call-done = f32[24,768]{1,0:T(8,128)} async-done(((f32[768,768]{1,0:T(8,128)}), f32[24,768]{1,0:T(8,128)}) %reduce-scatter.17.cloned.1.call-update) | async-done | bytes 73744 | tf_op jit(solution)/shard_map/reduce_scatter | solution.py:365
  1514.8 120.1 %reduce-scatter.33.cloned.1.call-done = f32[64,768]{1,0:T(8,128)} async-done(((f32[2048,768]{1,0:T(8,128)}), f32[64,768]{1,0:T(8,128)}) %reduce-scatter.33.cloned.1.call-update) | async-done | bytes 196624 | tf_op jit(solution)/shard_map/reduce_scatter | solution.py:375
  1634.9 120.2 %reduce-scatter.31.cloned.1.call-done = f32[24,2048]{1,0:T(8,128)} async-done(((f32[768,2048]{1,0:T(8,128)}), f32[24,2048]{1,0:T(8,128)}) %reduce-scatter.31.cloned.1.call-update) | async-done | bytes 196624 | tf_op jit(solution)/shard_map/reduce_scatter | solution.py:374
  1755.0 120.1 %reduce-scatter.29.cloned.1.call-done = f32[24,2048]{1,0:T(8,128)} async-done(((f32[768,2048]{1,0:T(8,128)}), f32[24,2048]{1,0:T(8,128)}) %reduce-scatter.29.cloned.1.call-update) | async-done | bytes 196624 | tf_op jit(solution)/shard_map/reduce_scatter | solution.py:373
  (653 shorter events, 620.7 us)
Async XLA Ops:
  7.2 85.4 %all-gather.17.cloned.1.call-start = ((), (), s32[]{:S(2)}) async-start(), calls=%async_computation.29 | async-start | bytes 1216512 | tf_op jit(solution)/shard_map/all_gather | solution.py:216
  8.9 116.7 %all-gather.15.cloned.1.call-start = ((), (), s32[]{:S(2)}) async-start(), calls=%async_computation.28 | async-start | bytes 1216512 | tf_op jit(solution)/shard_map/all_gather | solution.py:215
  10.5 171.7 %all-gather.13.cloned.1.call-start = ((), (), s32[]{:S(2)}) async-start(), calls=%async_computation.27 | async-start | bytes 1216512 | tf_op jit(solution)/shard_map/all_gather | solution.py:214
  12.0 326.4 %all-gather.25.cloned.1.call-start = ((), (), s32[]{:S(2)}) async-start(), calls=%async_computation.33 | async-start | bytes 1216512 | tf_op jit(solution)/shard_map/all_gather | solution.py:220
  13.6 327.3 %all-gather.23.cloned.1.call-start = ((), (), s32[]{:S(2)}) async-start(), calls=%async_computation.32 | async-start | bytes 1216512 | tf_op jit(solution)/shard_map/all_gather | solution.py:219
  15.2 338.5 %all-gather.19.cloned.1.call-start = ((), (), s32[]{:S(2)}) async-start(), calls=%async_computation.30 | async-start | bytes 1216512 | tf_op jit(solution)/shard_map/all_gather | solution.py:217
  16.8 392.5 %all-gather.21.cloned.1.call-start = ((), (), s32[]{:S(2)}) async-start(), calls=%async_computation.31 | async-start | bytes 1216512 | tf_op jit(solution)/shard_map/all_gather | solution.py:218
  18.4 448.0 %all-gather.27.cloned.1.call-start = ((), (), s32[]{:S(2)}) async-start(), calls=%async_computation.34 | async-start | bytes 1216512 | tf_op jit(solution)/shard_map/all_gather | solution.py:221
  19.9 508.5 %all-gather.31.cloned.1.call-start = ((), (), s32[]{:S(2)}) async-start(), calls=%async_computation.36 | async-start | bytes 3244032 | tf_op jit(solution)/shard_map/all_gather | solution.py:223
  96.0 32.9 %all-to-all-start.2 = ((bf16[512,4,192]{0,2,1:T(8,128)(2,1)}), bf16[512,4,192]{0,2,1:T(8,128)(2,1)S(1)}, u32[]{:S(2)}, u32[]{:S(2)}) async-start(bf16[512,4,192]{0,2,1:T(8,128)(2,1)} %bitcast.21), calls=%async_computation.2 | async-start | bytes 1572864 | tf_op jit(solution)/shard_map/all_to_all | solution.py:256
  99.5 490.2 %all-gather.29.cloned.1.call-start = ((), (), s32[]{:S(2)}) async-start(), calls=%async_computation.35 | async-start | bytes 3244032 | tf_op jit(solution)/shard_map/all_gather | solution.py:222
  128.9 56.5 %all-to-all-start.1 = ((bf16[512,4,192]{0,2,1:T(8,128)(2,1)}), bf16[512,4,192]{0,2,1:T(8,128)(2,1)S(1)}, u32[]{:S(2)}, u32[]{:S(2)}) async-start(bf16[512,4,192]{0,2,1:T(8,128)(2,1)} %bitcast.18), calls=%async_computation.1 | async-start | bytes 1572864 | tf_op jit(solution)/shard_map/all_to_all | solution.py:255
  185.4 54.0 %all-to-all-start = ((bf16[512,4,192]{0,2,1:T(8,128)(2,1)}), bf16[512,4,192]{0,2,1:T(8,128)(2,1)S(1)}, u32[]{:S(2)}, u32[]{:S(2)}) async-start(bf16[512,4,192]{0,2,1:T(8,128)(2,1)} %bitcast.16), calls=%async_computation | async-start | bytes 1572864 | tf_op jit(solution)/shard_map/all_to_all | solution.py:254
  334.9 15.4 all-to-all-start.3
  350.3 8.6 all-to-all-start.6
  359.0 54.1 %all-to-all-start.5 = ((bf16[128,4,192]{0,2,1:T(8,128)(2,1)}), bf16[128,4,192]{0,2,1:T(8,128)(2,1)S(1)}, u32[]{:S(2)}, u32[]{:S(2)}) async-start(bf16[128,4,192]{0,2,1:T(8,128)(2,1)} %bitcast.28), calls=%async_computation.5 | async-start | bytes 393216 | tf_op jit(solution)/shard_map/all_to_all | solution.py:257
  413.1 15.4 all-to-all-start.4
  416.6 234.5 %all-gather.33.cloned.1.call-start = ((), (), s32[]{:S(2)}) async-start(), calls=%async_computation.37 | async-start | bytes 3244032 | tf_op jit(solution)/shard_map/all_gather | solution.py:224
  449.0 17.4 all-to-all-start.7
  672.9 15.9 all-to-all-start.8
  677.1 564.3 %reduce-scatter.27.cloned.1.call-start = ((), (), s32[]{:S(2)}) async-start(), calls=%async_computation.43 | async-start | bytes 2433024 | tf_op jit(solution)/shard_map/reduce_scatter | solution.py:372
  681.1 560.3 %reduce-scatter.37.cloned.1.call-start = ((), (), s32[]{:S(2)}) async-start(), calls=%async_computation.48 | async-start | bytes 2433024
  746.0 495.4 %reduce-scatter.35.cloned.1.call-start = ((), (), s32[]{:S(2)}) async-start(), calls=%async_computation.47 | async-start | bytes 2433024
  758.7 482.7 %reduce-scatter.25.cloned.1.call-start = ((), (), s32[]{:S(2)}) async-start(), calls=%async_computation.42 | async-start | bytes 2433024 | tf_op jit(solution)/shard_map/reduce_scatter | solution.py:369
  786.9 15.9 all-to-all-start.10
  791.1 450.4 %reduce-scatter.23.cloned.1.call-start = ((), (), s32[]{:S(2)}) async-start(), calls=%async_computation.41 | async-start | bytes 2433024 | tf_op jit(solution)/shard_map/reduce_scatter | solution.py:368
  793.4 512.5 %reduce-scatter.21.cloned.1.call-start = ((), (), s32[]{:S(2)}) async-start(), calls=%async_computation.40 | async-start | bytes 2433024 | tf_op jit(solution)/shard_map/reduce_scatter | solution.py:367
  1103.1 307.2 %reduce-scatter.19.cloned.1.call-start = ((), (), s32[]{:S(2)}) async-start(), calls=%async_computation.39 | async-start | bytes 2433024 | tf_op jit(solution)/shard_map/reduce_scatter | solution.py:366
  1125.3 389.5 %reduce-scatter.17.cloned.1.call-start = ((), (), s32[]{:S(2)}) async-start(), calls=%async_computation.38 | async-start | bytes 2433024 | tf_op jit(solution)/shard_map/reduce_scatter | solution.py:365
  1142.9 492.0 %reduce-scatter.33.cloned.1.call-start = ((), (), s32[]{:S(2)}) async-start(), calls=%async_computation.46 | async-start | bytes 6488064 | tf_op jit(solution)/shard_map/reduce_scatter | solution.py:375
  1150.2 604.8 %reduce-scatter.31.cloned.1.call-start = ((), (), s32[]{:S(2)}) async-start(), calls=%async_computation.45 | async-start | bytes 6488064 | tf_op jit(solution)/shard_map/reduce_scatter | solution.py:374
  1157.4 717.7 %reduce-scatter.29.cloned.1.call-start = ((), (), s32[]{:S(2)}) async-start(), calls=%async_computation.44 | async-start | bytes 6488064 | tf_op jit(solution)/shard_map/reduce_scatter | solution.py:373
  (121 other events, 2193.8 us)
Sparse Core Ops, SparseCore 0:
  11.5 56.7 all-gather.16
  71.8 53.8 all-gather.14
  129.1 52.9 all-gather.12
  185.5 52.9 all-gather.24
  241.8 53.0 all-gather.22
  298.3 54.0 all-gather.18
  355.8 53.4 all-gather.20
  412.8 53.4 all-gather.26
  469.8 58.5 all-gather.30
  531.7 57.9 all-gather.28
  593.2 57.9 all-gather.32
  683.5 100.3 reduce-scatter.26
  789.7 98.7 reduce-scatter.36
  894.2 98.6 reduce-scatter.34
  998.6 98.6 reduce-scatter.24
  1103.0 98.5 reduce-scatter.22
  1207.3 98.6 reduce-scatter.20
  1311.7 98.5 reduce-scatter.18
  1416.2 98.5 reduce-scatter.16
  1520.8 114.0 reduce-scatter.32
  1641.1 113.8 reduce-scatter.30
  1761.2 113.8 reduce-scatter.28
where the time goes:
time: 1890 us; the launch traced here: 1880 us
  waiting for transfers between devices  972 us (51%)
  local copies, waits for them, and re-layouts  273 us (14%)
  matrix products  225 us (12%)
  blocking collectives  202 us (11%)
  other arithmetic  127 us (7%)
  starting transfers between devices  38.2 us (2%)
  loops' own time  28.4 us (2%)
    reduce_scatter x1, waiting for transfers between devices, per_device(): lax.psum_scatter(grad_wup, ('seq', 'fsdp'), scatter_dimension=0, tiled=True)  120 us
    reduce_scatter x1, waiting for transfers between devices, per_device(): lax.psum_scatter(grad_down, ('seq', 'fsdp'), scatter_dimension=0, tiled=T...  120 us
    reduce_scatter x1, waiting for transfers between devices, per_device(): lax.psum_scatter(grad_wgate, ('seq', 'fsdp'), scatter_dimension=0, tiled=...  120 us
    reduce_scatter x1, waiting for transfers between devices, per_device(): lax.psum_scatter(grad_query, ('seq', 'fsdp'), scatter_dimension=0, tiled=...  104 us
    reduce_scatter x1, waiting for transfers between devices, per_device(): lax.psum_scatter(grad_key, ('seq', 'fsdp'), scatter_dimension=0, tiled=True)  104 us
    dot_general x16, matrix products, block_scores(): jnp.einsum('qhd,khd->hqk', query_block, key_heads, preferred_element_type...  71.4 us
    all_gather x1, blocking collectives, per_device(): lax.all_gather(gains.astype(jnp.bfloat16), ('seq', 'fsdp'), axis=1, tiled...  69.9 us
    reduce_scatter x1, waiting for transfers between devices, per_device(): lax.psum_scatter(grad_value, ('seq', 'fsdp'), scatter_dimension=0, tiled=...  64.5 us
  transfers between devices with their start and end apart: 32, of which 18 were waited for; matrix products, arithmetic and copies ran while one was open for 30% of the time, Pallas kernels for 0%

commit v1 on v0

v1 whole, which is shorter than its diff:
```python
import functools
import jax
import jax.numpy as jnp
import numpy as np
from jax import lax
from jax.experimental import pallas as pl
from jax.experimental.pallas import tpu as pltpu
from jax.sharding import PartitionSpec as P

LANES = 128
BLOCK = 512
negative = -1e30
epsilon = 1e-06
highest = lax.Precision.HIGHEST
HEAD = 64


def nt(left, right):
    return lax.dot_general(left, right, (((1,), (1,)), ((), ())), preferred_element_type=jnp.float32)


def nn(left, right):
    return jnp.dot(left, right, preferred_element_type=jnp.float32)


def half_mask(head, head_size):
    lane = lax.broadcasted_iota(jnp.int32, (1, LANES), 1)
    per_tile = LANES // head_size
    return (lane // head_size) == (head % per_tile)


def attend_forward_kernel(*refs, causal, head_size):
    if causal:
        length_ref, q_ref, k_ref, v_ref, base_ref, o_ref, lse_ref, s_scr, p_scr, t_scr = refs
        length = length_ref[0]
    else:
        q_ref, k_ref, v_ref, o_ref, lse_ref, s_scr, p_scr = refs
    head = pl.program_id(0)
    first = (head % (LANES // head_size)) == 0
    mask = half_mask(head, head_size)
    rows, keys = q_ref.shape[0], k_ref.shape[0]
    block = min(BLOCK, rows)
    if causal:
        wide = jnp.broadcast_to(base_ref[0], (LANES, 3 * LANES))
        t_scr[...] = pltpu.roll(wide, 0, 1, stride=1, stride_axis=0)[:, : 2 * LANES]
    for number in range(rows // block):
        start = number * block
        queries = jnp.where(mask, q_ref[start : start + block, :], 0)
        total = start + block if causal else keys
        for low in range(0, total, BLOCK):
            high = min(low + BLOCK, total)
            s_scr[:, low:high] = nt(queries, k_ref[low:high, :])
        if causal:
            for part in range(block // LANES):
                at = slice(part * LANES, (part + 1) * LANES)
                column = start + part * LANES
                if column > 0:
                    s_scr[at, column - LANES : column + LANES] += t_scr[...]
                else:
                    s_scr[at, :LANES] += t_scr[:, LANES:]
            for low in range(0, total, BLOCK):
                high = min(low + BLOCK, total)

                @pl.when(length < high)
                def _(low=low, high=high):
                    place = low + lax.broadcasted_iota(jnp.int32, (block, high - low), 1)
                    s_scr[:, low:high] = jnp.where(place < length, s_scr[:, low:high], negative)

        sums = []
        for part in range(block // LANES):
            at = slice(part * LANES, (part + 1) * LANES)
            width = start + (part + 1) * LANES if causal else keys
            scores = s_scr[at, :width]
            largest = jnp.max(scores, axis=1, keepdims=True)
            expos = jnp.exp(scores - largest)
            totals = jnp.sum(expos, axis=1, keepdims=True)
            p_scr[at, :width] = expos.astype(jnp.bfloat16)
            if width < total:
                p_scr[at, width:total] = jnp.zeros((LANES, total - width), jnp.bfloat16)
            logsum = jnp.broadcast_to(largest + jnp.log(totals), (LANES, LANES))
            lse_ref[0, :, start + part * LANES : start + (part + 1) * LANES] = logsum.T[:8]
            sums.append(totals)
        mixed = nn(p_scr[:, :total], v_ref[:total, :])
        mixed = mixed / jnp.concatenate(sums, axis=0)
        before = jnp.where(first, jnp.zeros_like(mixed), o_ref[start : start + block, :].astype(jnp.float32))
        o_ref[start : start + block, :] = jnp.where(mask, mixed, before).astype(jnp.bfloat16)


def attend_forward(queries, keys, values, heads, head_size, padded=0, bias=None, length=None):
    causal = bias is not None
    rows, width = queries.shape
    count = keys.shape[0]
    per_tile = LANES // head_size
    block = min(BLOCK, rows)
    width = padded or width
    tile = lambda h: (0, h // per_tile)
    row_spec = pl.BlockSpec((rows, LANES), tile)
    skip = padded // LANES
    key_specs = [pl.BlockSpec((count, LANES), lambda h, n=n: (0, n * skip + h // per_tile)) for n in (1, 2)]
    in_specs = [row_spec, *key_specs]
    args = [queries, keys, values]
    scratch = [pltpu.VMEM((block, count), jnp.float32), pltpu.VMEM((block, count), jnp.bfloat16)]
    if causal:
        in_specs = [pl.BlockSpec(memory_space=pltpu.SMEM)] + in_specs + [pl.BlockSpec((1, 1, 3 * LANES), lambda h: (h, 0, 0))]
        args = [length] + args + [bias]
        scratch = scratch + [pltpu.VMEM((LANES, 2 * LANES), jnp.float32)]
    return pl.pallas_call(
        functools.partial(attend_forward_kernel, causal=causal, head_size=head_size),
        grid=(heads,),
        in_specs=in_specs,
        out_specs=[row_spec, pl.BlockSpec((1, 8, rows), lambda h: (h, 0, 0))],
        out_shape=[
            jax.ShapeDtypeStruct((rows, width), jnp.bfloat16),
            jax.ShapeDtypeStruct((heads, 8, rows), jnp.float32),
        ],
        scratch_shapes=scratch,
        compiler_params=pltpu.CompilerParams(vmem_limit_bytes=60 * 2**20),
        cost_estimate=pl.CostEstimate(
            flops=4 * heads * LANES * rows * count // (2 if causal else 1),
            bytes_accessed=4 * (rows + count) * width,
            transcendentals=heads * rows * count // (2 if causal else 1),
        ),
        name="self_forward" if causal else "cross_forward",
    )(*args)


def attend_backward_kernel(*refs, causal, head_size, heads):
    if causal:
        (length_ref, q_ref, k_ref, v_ref, do_ref, o_ref, lse_ref, base_ref, dq_ref, dk_ref, dv_ref, near_ref,
         kt_scr, dqt_scr, dk_scr, dv_scr, t_scr, row_scr) = refs
        length = length_ref[0]
    else:
        (q_ref, k_ref, v_ref, do_ref, o_ref, lse_ref, dq_ref, dk_ref, dv_ref,
         kt_scr, dqt_scr, dk_scr, dv_scr, row_scr) = refs
    head = pl.program_id(0)
    per_tile = LANES // head_size
    first = (head % per_tile) == 0
    last = ((head % per_tile) == per_tile - 1) | (head == heads - 1)
    mask = half_mask(head, head_size)
    rows, keys = q_ref.shape[0], k_ref.shape[0]
    block = min(BLOCK, rows)
    key_block = min(BLOCK, keys)

    @pl.when(first)
    def _():
        dqt_scr[...] = jnp.zeros_like(dqt_scr)
        dk_scr[...] = jnp.zeros_like(dk_scr)
        dv_scr[...] = jnp.zeros_like(dv_scr)

    if causal:
        wide = jnp.broadcast_to(base_ref[0], (LANES, 3 * LANES))
        t_scr[...] = pltpu.roll(wide, 0, 1, stride=1, stride_axis=0)[:, : 2 * LANES]
        near_ref[0] = jnp.zeros((LANES, 2 * LANES), jnp.float32)
    for low in range(0, keys, key_block):
        kt_scr[:, low : low + key_block] = jnp.where(mask, k_ref[low : low + key_block, :], 0).T
    for low in range(0, rows, block):
        at = slice(low, low + block)
        product = do_ref[at, :].astype(jnp.float32) * o_ref[at, :].astype(jnp.float32)
        delta = jnp.sum(jnp.where(mask, product, 0.0).T, axis=0, keepdims=True)
        logsum = lse_ref[0, 0:1, at]
        if causal:
            place = low + lax.broadcasted_iota(jnp.int32, (1, block), 1)
            logsum = jnp.where(place < length, logsum, -negative)
        row_scr[0:1, at] = logsum
        row_scr[1:2, at] = delta

    def piece(key_at, row_at, score_fix, near_width):
        queries = jnp.where(mask, q_ref[row_at, :], 0)
        grads = jnp.where(mask, do_ref[row_at, :], 0)
        scores = score_fix(nt(k_ref[key_at, :], queries))
        weights = jnp.exp(scores - row_scr[0:1, row_at])
        grad_weights = nt(v_ref[key_at, :], grads)
        grad_scores = weights * (grad_weights - row_scr[1:2, row_at])
        low_scores = grad_scores.astype(jnp.bfloat16)
        dv_scr[key_at, :] += nn(weights.astype(jnp.bfloat16), grads)
        dk_scr[key_at, :] += nn(low_scores, queries)
        dqt_scr[:, row_at] += nn(kt_scr[:, key_at], low_scores)
        return grad_scores

    if not causal:
        for low in range(0, keys, key_block):
            for at in range(0, rows, block):
                piece(slice(low, low + key_block), slice(at, at + block), lambda s: s, 0)
    else:
        for low in range(0, keys, block):
            for part in range(block // LANES):
                here = low + part * LANES
                width = block - part * LANES
                near = min(2 * LANES, width)

                def fix(scores, near=near):
                    head_part = scores[:, :near] + t_scr[:, :near]
                    if near == scores.shape[1]:
                        return head_part
                    return jnp.concatenate([head_part, scores[:, near:]], axis=1)

                grad = piece(slice(here, here + LANES), slice(here, low + block), fix, near)
                near_ref[0, :, :near] += grad[:, :near]
            for at in range(low + block, rows, block):
                if at == low + block:

                    def fix(scores):
                        top, bottom = scores[: block - LANES], scores[block - LANES :]
                        bottom = jnp.concatenate(
                            [bottom[:, :LANES] + t_scr[:, LANES:], bottom[:, LANES:]], axis=1
                        )
                        return jnp.concatenate([top, bottom], axis=0)
                else:
                    fix = lambda s: s
                grad = piece(slice(low, low + block), slice(at, at + block), fix, 0)
                if at == low + block:
                    near_ref[0, :, LANES:] += grad[block - LANES :, :LANES]

    @pl.when(last)
    def _():
        for low in range(0, rows, block):
            dq_ref[low : low + block, :] = dqt_scr[:, low : low + block].T.astype(jnp.bfloat16)
        dk_ref[...] = dk_scr[...].astype(jnp.bfloat16)
        dv_ref[...] = dv_scr[...].astype(jnp.bfloat16)


def attend_backward(queries, keys, values, grad_mixed, mixed, logsum, heads, head_size, padded=0, bias=None, length=None):
    causal = bias is not None
    rows, width = queries.shape
    count = keys.shape[0]
    per_tile = LANES // head_size
    width = padded or width
    tile = lambda h: (0, h // per_tile)
    row_spec = pl.BlockSpec((rows, LANES), tile)
    key_spec = pl.BlockSpec((count, LANES), tile)
    skip = padded // LANES
    key_specs = [pl.BlockSpec((count, LANES), lambda h, n=n: (0, n * skip + h // per_tile)) for n in (1, 2)]
    in_specs = [row_spec, *key_specs, row_spec, row_spec, pl.BlockSpec((1, 8, rows), lambda h: (h, 0, 0))]
    args = [queries, keys, values, grad_mixed, mixed, logsum]
    out_specs = [row_spec, key_spec, key_spec]
    out_shape = [
        jax.ShapeDtypeStruct((rows, width), jnp.bfloat16),
        jax.ShapeDtypeStruct((count, width), jnp.bfloat16),
        jax.ShapeDtypeStruct((count, width), jnp.bfloat16),
    ]
    scratch = [
        pltpu.VMEM((LANES, count), jnp.bfloat16),
        pltpu.VMEM((LANES, rows), jnp.float32),
        pltpu.VMEM((count, LANES), jnp.float32),
        pltpu.VMEM((count, LANES), jnp.float32),
    ]
    if causal:
        in_specs = [pl.BlockSpec(memory_space=pltpu.SMEM)] + in_specs + [pl.BlockSpec((1, 1, 3 * LANES), lambda h: (h, 0, 0))]
        args = [length] + args + [bias]
        out_specs = out_specs + [pl.BlockSpec((1, LANES, 2 * LANES), lambda h: (h, 0, 0))]
        out_shape = out_shape + [jax.ShapeDtypeStruct((heads, LANES, 2 * LANES), jnp.float32)]
        scratch = scratch + [pltpu.VMEM((LANES, 2 * LANES), jnp.float32)]
    scratch = scratch + [pltpu.VMEM((8, rows), jnp.float32)]
    return pl.pallas_call(
        functools.partial(attend_backward_kernel, causal=causal, head_size=head_size, heads=heads),
        grid=(heads,),
        in_specs=in_specs,
        out_specs=out_specs,
        out_shape=out_shape,
        scratch_shapes=scratch,
        compiler_params=pltpu.CompilerParams(vmem_limit_bytes=60 * 2**20),
        cost_estimate=pl.CostEstimate(
            flops=10 * heads * LANES * rows * count // (2 if causal else 1),
            bytes_accessed=8 * (rows + count) * width,
            transcendentals=heads * rows * count // (2 if causal else 1),
        ),
        name="self_backward" if causal else "cross_backward",
    )(*args)


bounds = np.ceil(16.0 * 8.0 ** (np.arange(1, 16) / 16.0)).astype(np.int32)


def buckets(distance):
    far = 16 + jnp.sum((distance[..., None] >= jnp.asarray(bounds)).astype(jnp.int32), axis=-1)
    return jnp.where(distance < 16, distance, far)


def bias_rows(table):
    count = table.shape[0]
    place = jnp.arange(3 * LANES, dtype=jnp.int32)

    def row(distance, outside):
        onehot = buckets(jnp.clip(distance, 0, 2 * LANES))[None, :] == jnp.arange(count, dtype=jnp.int32)[:, None]
        relative = table - table[count - 1 :]
        values = jnp.sum(jnp.where(onehot[:, None, :], relative[:, :, None], 0.0), axis=0)
        return jnp.where(outside[None], negative, values)[:, None, :]

    forward = row(jnp.where(place < 2 * LANES, LANES - place, 2 * LANES), (place > LANES) & (place < 2 * LANES))
    backward = row(place, place >= 2 * LANES)
    return forward, backward


def matmul_t(left, right):
    return nt(left, right)


def inner_rows(left, right):
    return lax.dot_general(left, right, (((0,), (0,)), ((), ())), preferred_element_type=jnp.float32)


def rms_norm(values, gain):
    scale = lax.rsqrt(jnp.mean(values * values, axis=-1, keepdims=True) + epsilon)
    return values * scale * gain


def rms_back(values, gain, grad_normed):
    scale = lax.rsqrt(jnp.mean(values * values, axis=-1, keepdims=True) + epsilon)
    unit = values * scale
    grad_unit = grad_normed * gain
    grad_gain = jnp.sum(grad_normed * unit, axis=0)
    grad_values = scale * (grad_unit - unit * jnp.mean(grad_unit * unit, axis=-1, keepdims=True))
    return (grad_values, grad_gain)


def activate(gate, upper):
    return jax.nn.gelu(gate, approximate=True) * upper


def per_device(
    tokens, encoder, cotangent, lengths, gains, self_query, self_key, self_value, self_output,
    cross_query, cross_key, cross_value, cross_output, ffn_gate, ffn_up, ffn_down, rel_bias,
):
    both = ("seq", "fsdp")
    seq, fsdp = lax.axis_size("seq"), lax.axis_size("fsdp")
    world = seq * fsdp
    low = jnp.bfloat16
    share = self_query.shape[0]
    width = self_query.shape[1]
    hidden_share = ffn_down.shape[0]
    inner = ffn_gate.shape[1]
    rows = tokens.shape[1]
    group = rel_bias.shape[1]
    group_width = group * HEAD
    padded = -(-group_width // LANES) * LANES
    heads = width // HEAD
    place = lax.axis_index("seq")

    everyone = lax.all_gather(tokens[0], "seq", axis=0, tiled=True)
    encoded = lax.all_gather(encoder[0], "seq", axis=0, tiled=True)

    gain_share = gains.shape[1]
    gain_block = jnp.pad(gains.astype(low).reshape(1, -1), ((0, 7), (0, width - gains.size)))
    pack = jnp.concatenate(
        [w.astype(low) for w in (self_query, self_key, self_value, self_output, cross_query, cross_key, cross_value, cross_output)]
        + [gain_block],
        axis=0,
    )
    packed = lax.all_gather(pack, both, axis=0)
    gate_up = lax.all_gather(jnp.concatenate([ffn_gate.astype(low), ffn_up.astype(low)], axis=1), both, axis=0, tiled=True)
    w_down = lax.all_gather(ffn_down.astype(low), both, axis=0, tiled=True)

    def whole(number):
        return packed[:, number * share : (number + 1) * share].reshape(width, width)

    w_output, c_query, c_key, c_value, c_output = (whole(n) for n in range(3, 8))

    def own(number):
        cut = lax.dynamic_slice_in_dim(whole(number), place * group_width, group_width, 1)
        return jnp.pad(cut, ((0, 0), (0, padded - group_width)))

    w_qkv = jnp.concatenate([own(n) for n in range(3)], axis=1)
    gain_rows = packed[:, 8 * share, : gains.size].reshape(world, 3, gain_share).transpose(1, 0, 2).reshape(3, width).astype(jnp.float32)

    length = lengths[0]
    values_in = tokens[0].astype(jnp.float32)
    normed_all = rms_norm(everyone.astype(jnp.float32), gain_rows[0]).astype(low)
    qkv = nn(normed_all, w_qkv).astype(low)
    base_forward, base_backward = bias_rows(rel_bias)
    own_mixed, own_logsum = attend_forward(qkv, qkv, qkv, group, HEAD, padded, base_forward, lengths)
    mixed = lax.all_to_all(own_mixed[:, :group_width], "seq", split_axis=0, concat_axis=1, tiled=True)
    attended = values_in + nn(mixed, w_output)
    normed_two = rms_norm(attended, gain_rows[1]).astype(low)
    cross_queries = nn(normed_two, c_query).astype(low)
    cross_keys = nn(encoded, c_key).astype(low)
    cross_values = nn(encoded, c_value).astype(low)
    cross_mixed, cross_logsum = attend_forward(cross_queries, cross_keys, cross_values, heads, HEAD)
    crossed = attended + nn(cross_mixed, c_output)
    normed_three = rms_norm(crossed, gain_rows[2]).astype(low)
    both_parts = nn(normed_three, gate_up)
    gate, upper = both_parts[:, :inner], both_parts[:, inner:]
    hidden = activate(gate, upper).astype(low)
    result = crossed + nn(hidden, w_down)

    positions = place * rows + jnp.arange(rows, dtype=jnp.int32)
    grad_out = cotangent[0].astype(jnp.float32) * (positions < length).astype(jnp.float32)[:, None]
    grad_ffn = grad_out.astype(low)
    grad_down = inner_rows(hidden, grad_ffn).astype(low)
    share_down = lax.psum_scatter(grad_down, both, scatter_dimension=0, tiled=True)
    grad_hidden = matmul_t(grad_ffn, w_down)
    _, pullback = jax.vjp(activate, gate, upper)
    grad_gate, grad_upper = pullback(grad_hidden)
    grad_both = jnp.concatenate([grad_gate.astype(low), grad_upper.astype(low)], axis=1)
    grad_gate_up = inner_rows(normed_three, grad_both).astype(low)
    share_gate_up = lax.psum_scatter(grad_gate_up, both, scatter_dimension=0, tiled=True)
    grad_normed_three = matmul_t(grad_both, gate_up)
    norm_part, grad_gain_two = rms_back(crossed, gain_rows[2], grad_normed_three)
    grad_crossed = grad_out + norm_part
    grad_branch = grad_crossed.astype(low)
    grad_coutput = inner_rows(cross_mixed, grad_branch).astype(low)
    grad_cmixed = matmul_t(grad_branch, c_output).astype(low)
    grad_cq, grad_ck, grad_cv = attend_backward(
        cross_queries, cross_keys, cross_values, grad_cmixed, cross_mixed, cross_logsum, heads, HEAD
    )
    grad_cquery = inner_rows(normed_two, grad_cq).astype(low)
    grad_ckey = inner_rows(encoded, grad_ck).astype(low)
    grad_cvalue = inner_rows(encoded, grad_cv).astype(low)
    grad_encoded_part = (matmul_t(grad_ck, c_key) + matmul_t(grad_cv, c_value)).astype(low)
    grad_encoded = lax.psum_scatter(grad_encoded_part, "seq", scatter_dimension=0, tiled=True).astype(jnp.float32)
    norm_part, grad_gain_one = rms_back(attended, gain_rows[1], matmul_t(grad_cq, c_query))
    grad_attended = grad_crossed + norm_part
    grad_self_branch = grad_attended.astype(low)
    grad_output = inner_rows(mixed, grad_self_branch).astype(low)
    grad_mixed = matmul_t(grad_self_branch, w_output).astype(low)
    share_square = lax.psum_scatter(
        jnp.concatenate([grad_output, grad_cquery, grad_ckey, grad_cvalue, grad_coutput], axis=1),
        both, scatter_dimension=0, tiled=True,
    )
    own_grad_mixed = lax.all_to_all(grad_mixed, "seq", split_axis=1, concat_axis=0, tiled=True)
    own_grad_mixed = jnp.pad(own_grad_mixed, ((0, 0), (0, padded - group_width)))
    own_dq, own_dk, own_dv, near = attend_backward(
        qkv, qkv, qkv, own_grad_mixed, own_mixed, own_logsum, group, HEAD, padded, base_backward, lengths
    )
    own_qkv = jnp.concatenate([own_dq, own_dk, own_dv], axis=1)
    grad_normed = lax.psum_scatter(matmul_t(own_qkv, w_qkv).astype(low), "seq", scatter_dimension=0, tiled=True)
    grad_own = inner_rows(normed_all, own_qkv).astype(low)
    grad_own = grad_own.reshape(seq, fsdp, share, 3 * padded).transpose(1, 0, 2, 3)
    grad_own = lax.psum_scatter(grad_own, "fsdp", scatter_dimension=0, tiled=True)[0]
    grad_own = lax.all_to_all(grad_own, "seq", split_axis=0, concat_axis=0, tiled=True)
    grad_own = grad_own.reshape(seq, share, 3, padded)[:, :, :, :group_width].transpose(2, 1, 0, 3).reshape(3, share, width)

    norm_part, grad_gain_zero = rms_back(values_in, gain_rows[0], grad_normed.astype(jnp.float32))
    grad_input = grad_attended + norm_part
    grad_gains = jnp.stack([grad_gain_zero, grad_gain_one, grad_gain_two])
    share_gains = lax.psum_scatter(grad_gains, both, scatter_dimension=1, tiled=True)

    bins = rel_bias.shape[0]
    skew = jnp.pad(near.reshape(group, -1), ((0, 0), (0, LANES))).reshape(group, LANES, 2 * LANES + 1)
    by_distance = jnp.sum(skew[:, :, :LANES], axis=1)
    near_map = (buckets(jnp.arange(LANES, dtype=jnp.int32))[:, None] == jnp.arange(bins - 1, dtype=jnp.int32)[None]).astype(jnp.float32)
    near_sums = jnp.dot(near_map.T, by_distance.T, precision=highest)
    grad_table = jnp.concatenate([near_sums, -jnp.sum(near_sums, axis=0, keepdims=True)], axis=0)
    table_grad = lax.psum(grad_table, "fsdp")

    wide = jnp.float32
    outputs = [share_square[:, n * width : (n + 1) * width].astype(wide) for n in range(5)]
    own_outputs = [grad_own[n].astype(wide) for n in range(3)]
    return (
        result.astype(low)[None], grad_input[None], grad_encoded[None], share_gains,
        *own_outputs, *outputs,
        share_gate_up[:, :inner].astype(wide), share_gate_up[:, inner:].astype(wide), share_down.astype(wide),
        table_grad,
    )


def solution(mesh):
    split = P(("seq", "fsdp"), None)
    rows = P("fsdp", "seq", None)
    gains = P(None, ("seq", "fsdp"))
    return jax.shard_map(
        per_device,
        mesh=mesh,
        in_specs=(rows, rows, rows, P("fsdp"), gains, *([split] * 11), P(None, "seq")),
        out_specs=(rows, rows, rows, gains, *([split] * 11), P(None, "seq")),
        check_vma=False,
    )
```

time: 1890 us -> 854 us (0.45)
  waiting for transfers between devices: 972 us -> 503 us
  local copies, waits for them, and re-layouts: 273 us -> 46.1 us
  matrix products: 225 us -> 88.2 us
  blocking collectives: 202 us -> 74.8 us
  other arithmetic: 127 us -> 25.2 us
  Pallas kernels: 0 us -> 77.8 us
  loops' own time: 28.4 us -> 0 us
  starting transfers between devices: 38.2 us -> 12.2 us
    reduce_scatter x9 -> x5, waiting for transfers between devices: 634 us -> 266 us  [the longest x1 114 us: per_device(): lax.psum_scatter(grad_gate_up, both, scatter_dimension=0, tiled=True)]
    all_gather x11 -> x4, waiting for transfers between devices: 302 us -> 140 us  [the longest x1 83.5 us: per_device(): packed = lax.all_gather(pack, both, axis=0)]
    dot_general x83 -> x17, matrix products: 187 us -> 60.7 us  [the longest x8 30.3 us: nn(): return jnp.dot(left, right, preferred_element_type=jnp.float32)]
    pallas_call x0 -> x4, Pallas kernels: none -> 77.8 us  [the longest x2 40.6 us: attend_backward(): pl.pallas_call(functools.partial(attend_backward_kernel, causal=causal, h...]
    reduce_sum x20 -> x4, other arithmetic: 80.1 us -> 3.97 us  [the longest x1 1.87 us: rms_back(): grad_gain = jnp.sum(grad_normed * unit, axis=0)]
    unnamed x24 -> x11, waiting for transfers between devices: 0.37 us -> 76 us
    all_to_all x6 -> x0, blocking collectives: 73.2 us -> none  [the longest x1 15.6 us: per_device(): lax.all_to_all(head_dcq, 'seq', split_axis=0, concat_axis=1, tiled=True)]
    reshape x9 -> x4, local copies, waits for them, and re-layouts: 63.6 us -> 1.82 us  [the longest x1 1.14 us: per_device(): grad_own.reshape(seq, fsdp, share, 3 * padded).transpose(1, 0, 2, 3)]
  transfers between devices with their start and end apart: 32 -> 13, of which waited for: 18 -> 10; matrix products, arithmetic and copies ran while one was open for 30% -> 14% of each run, Pallas kernels for 0% -> 4%
where the time goes in v1:
time: 854 us; the launch traced here: 844 us
  waiting for transfers between devices  503 us (59%)
  matrix products  88.2 us (10%)
  Pallas kernels  77.8 us (9%)
  blocking collectives  74.8 us (9%)
  local copies, waits for them, and re-layouts  46.1 us (5%)
  other arithmetic  25.2 us (3%)
  between operations  16.2 us (2%)
  starting transfers between devices  12.2 us (1%)
    reduce_scatter x1, waiting for transfers between devices, per_device(): lax.psum_scatter(grad_gate_up, both, scatter_dimension=0, tiled=True)  114 us
    reduce_scatter x1, waiting for transfers between devices, per_device(): lax.psum_scatter(grad_down, both, scatter_dimension=0, tiled=True)  103 us
    all_gather x1, waiting for transfers between devices, per_device(): packed = lax.all_gather(pack, both, axis=0)  83.5 us
    unnamed x11, waiting for transfers between devices  76 us
    all_gather x1, waiting for transfers between devices, per_device(): w_down = lax.all_gather(ffn_down.astype(low), both, axis=0, tiled=True)  45.9 us
    pallas_call x2, Pallas kernels, attend_backward(): pl.pallas_call(functools.partial(attend_backward_kernel, causal=causal, h...  40.6 us
    unnamed x1, blocking collectives  39.5 us
    reduce_scatter x1, waiting for transfers between devices, per_device(): lax.psum_scatter(matmul_t(own_qkv, w_qkv).astype(low), 'seq', scatter_dim...  37.9 us
  transfers between devices with their start and end apart: 13, of which 10 were waited for; matrix products, arithmetic and copies ran while one was open for 14% of the time, Pallas kernels for 4%

profile of v1, /device:TPU:0, one launch (start us, length us, event | category | flops | bytes accessed | tf_op | source)
XLA Modules:
  0.0 843.9 jit_solution(2095984153806196351)
XLA Ops:
  18.5 14.8 %all-gather.2 = bf16[1,512,768]{2,1,0:T(8,128)(2,1)} all-gather(bf16[1,128,768]{2,1,0:T(8,128)(2,1)S(1)} %copy-done.37), channel_id=4, replica_groups=mesh['seq'=4,'fsdp'=8] {'seq'}, dimensions={1}, use_global_device_ids=true | all-gather | bytes 983040 | tf_op jit(solution)/shard_map/all_gather | solution.py:340
  34.6 10.5 %all-gather.12.cloned.1.call-done = bf16[1,2048,768]{2,1,0:T(8,128)(2,1)} async-done(((bf16[1,512,768]{2,1,0:T(8,128)(2,1)}), bf16[1,2048,768]{2,1,0:T(8,128)(2,1)}) %all-gather.12.cloned.1.call-update) | async-done | bytes 3145744 | tf_op jit(solution)/shard_map/all_gather | solution.py:339
  48.3 83.5 %all-gather.14.cloned.1.call-done = bf16[6400,768]{1,0:T(8,128)(2,1)} async-done(((bf16[200,768]{1,0:T(8,128)(2,1)}), bf16[6400,768]{1,0:T(8,128)(2,1)}) %all-gather.14.cloned.1.call-update) | async-done | bytes 9830416 | tf_op jit(solution)/shard_map/all_gather | solution.py:349
  133.5 6.6 fusion.63
  141.6 4.4 convolution_convert_fusion.3.refs_1_.refs_2_.refs_3_
  146.0 21.8 %self_forward.1 = (bf16[2048,256]{1,0:T(8,128)(2,1)}, f32[3,8,2048]{2,1,0:T(8,128)}) custom-call(s32[1]{0:T(128)} %copy.174.refs_0_, bf16[2048,768]{1,0:T(8,128)(2,1)} %convolution_convert_fusion.3.refs_1_.refs_2_.refs_3_, bf16[2048,768]{1,0:T(8,128)(2,1)} %convolution_convert_fusion.3.refs_1_.refs_2_.refs_3_, ...), custom_call_target="tpu_custom_call" | custom-call | flops 3221225472 | bytes 4194304 | tf_op jit(solution)/shard_map/self_forward/pallas_call | solution.py:107
  170.1 3.8 all-to-all-start
  180.2 10.0 %all-to-all-done = bf16[4,512,192]{1,2,0:T(8,128)(2,1)S(1)} async-done(((bf16[4,512,192]{1,2,0:T(8,128)(2,1)}), bf16[4,512,192]{1,2,0:T(8,128)(2,1)S(1)}, u32[]{:S(2)}, u32[]{:S(2)}) %all-to-all-start) | async-done | bytes 786464 | tf_op jit(solution)/shard_map/all_to_all | solution.py:371
  194.5 15.5 %cross_forward.1 = (bf16[512,768]{1,0:T(8,128)(2,1)}, f32[12,8,512]{2,1,0:T(8,128)}) custom-call(bf16[512,768]{1,0:T(8,128)(2,1)} %convolution_convert_fusion.14.refs_0_, bf16[512,768]{1,0:T(8,128)(2,1)} %fusion.34.refs_1_, bf16[512,768]{1,0:T(8,128)(2,1)} %fusion.35.refs_2_), custom_call_target="tpu_custom_call" | custom-call | flops 1610612736 | bytes 3145728 | tf_op jit(solution)/shard_map/cross_forward/pallas_call | solution.py:107
  212.9 8.7 %fusion.60 = f32[512,4096]{1,0:T(8,128)} fusion(bf16[768,4096]{1,0:T(8,128)(2,1)} %all-gather.8.cloned.1.call-done, f32[512,768]{1,0:T(8,128)S(1)} %get-tuple-element.171, f32[768]{0:T(1024)S(1)} %mul.253, f32[512]{0:T(512)S(1)} %add_rsqrt_fusion.2), kind=kOutput, calls=%fused_computation.158 | convolution fusion | flops 3222405120 | bytes 16258048 | tf_op jit(solution)/shard_map/dot_general | solution.py:23
  221.6 45.9 %all-gather.10.cloned.1.call-done = bf16[2048,768]{1,0:T(8,128)(2,1)} async-done(((bf16[64,768]{1,0:T(8,128)(2,1)}), bf16[2048,768]{1,0:T(8,128)(2,1)}) %all-gather.10.cloned.1.call-update) | async-done | bytes 3145744 | tf_op jit(solution)/shard_map/all_gather | solution.py:351
  267.5 8.8 %fusion.9 = (bf16[512,2048]{1,0:T(8,128)(2,1)S(1)}, bf16[512,2048]{1,0:T(8,128)(2,1)S(1)}, bf16[512,2048]{1,0:T(8,128)(2,1)}) fusion(f32[512,4096]{1,0:T(8,128)} %fusion.60, bf16[2048,768]{1,0:T(8,128)(2,1)} %all-gather.10.cloned.1.call-done, bf16[1,512,768]{2,1,0:T(8,128)(2,1)S(1)} %copy-done.24, f32[512]{0:T(512)S(1)} %copy-done.45), kind=kOutput, calls=%fused_computation.14 | convolution fusion | flops 1639055360 | bytes 18614272 | tf_op jit(solution)/shard_map/dot_general | solution.py:19
  276.3 4.2 multiply_reduce_fusion
  283.5 14.4 %cross_backward.1 = (bf16[512,768]{1,0:T(8,128)(2,1)}, bf16[512,768]{1,0:T(8,128)(2,1)}, bf16[512,768]{1,0:T(8,128)(2,1)}) custom-call(bf16[512,768]{1,0:T(8,128)(2,1)} %convolution_convert_fusion.14.refs_0_, bf16[512,768]{1,0:T(8,128)(2,1)} %fusion.34.refs_1_, bf16[512,768]{1,0:T(8,128)(2,1)} %fusion.35.refs_2_, ...), custom_call_target="tpu_custom_call" | custom-call | flops 4026531840 | bytes 6291456 | tf_op jit(solution)/shard_map/cross_backward/pallas_call | solution.py:254
  298.0 3.2 multiply_reduce_fusion.1
  306.6 4.2 all-to-all-start.1
  311.4 11.0 %all-to-all-done.1 = bf16[512,4,192]{0,2,1:T(8,128)(2,1)} async-done(((bf16[512,4,192]{0,2,1:T(8,128)(2,1)}), bf16[512,4,192]{0,2,1:T(8,128)(2,1)}, u32[]{:S(2)}, u32[]{:S(2)}) %all-to-all-start.1) | async-done | bytes 786464 | tf_op jit(solution)/shard_map/all_to_all | solution.py:419
  327.2 26.1 %self_backward.1 = (bf16[2048,256]{1,0:T(8,128)(2,1)}, bf16[2048,256]{1,0:T(8,128)(2,1)}, bf16[2048,256]{1,0:T(8,128)(2,1)}, f32[3,128,256]{2,1,0:T(8,128)}) custom-call(s32[1]{0:T(128)} %copy.174.refs_0_, bf16[2048,768]{1,0:T(8,128)(2,1)} %convolution_convert_fusion.3.refs_1_.refs_2_.refs_3_, ...), custom_call_target="tpu_custom_call" | custom-call | flops 8053063680 | bytes 8388608 | tf_op jit(solution)/shard_map/self_backward/pallas_call | solution.py:254
  365.6 5.5 convolution_convert_fusion.1
  371.2 6.4 convolution_convert_fusion.2
  377.7 3.2 fusion.29
  388.3 8.5 %copy.145 = bf16[768,3840]{1,0:T(8,128)(2,1)} copy(bf16[768,3840]{0,1:T(8,128)(2,1)} %fusion.27) | data formatting | bytes 11796480
  397.2 8.5 %convolution_convert_fusion = bf16[768,4096]{1,0:T(8,128)(2,1)} fusion(bf16[512,2048]{1,0:T(8,128)(2,1)} %copy-done.17, bf16[512,2048]{1,0:T(8,128)(2,1)} %copy-done.16, f32[512,768]{1,0:T(8,128)S(1)} %get-tuple-element.171, f32[768]{0:T(1024)S(1)} %mul.253, f32[512]{0:T(512)S(1)} %add_rsqrt_fusion.2), kind=kOutput, calls=%fused_computation.2 | convolution fusion | flops 3233939456 | bytes 12063744 | tf_op jit(solution)/shard_map/dot_general | solution.py:299
  407.8 5.2 fusion.36
  414.6 20.6 %psum.7 = f32[32,3]{0,1:T(4,128)} all-reduce(f32[32,3]{0,1:T(4,128)S(1)} %pad_maximum_fusion.5), channel_id=1, replica_groups=mesh['seq'=4,'fsdp'=8] {'fsdp'}, use_global_device_ids=true, to_apply=%region_24.25 | all-reduce | flops 96 | bytes 768 | tf_op jit(solution)/shard_map/psum | solution.py:443
  435.2 3.3 all-to-all-start.2
  438.5 10.9 %reduce-scatter.12.cloned.1.call-done = bf16[128,768]{1,0:T(8,128)(2,1)} async-done(((bf16[512,768]{1,0:T(8,128)(2,1)}), bf16[128,768]{1,0:T(8,128)(2,1)}) %reduce-scatter.12.cloned.1.call-update) | async-done | bytes 196624 | tf_op jit(solution)/shard_map/reduce_scatter | solution.py:409
  453.6 103.4 %reduce-scatter.18.cloned.1.call-done = bf16[64,768]{1,0:T(8,128)(2,1)} async-done(((bf16[2048,768]{1,0:T(8,128)(2,1)}), bf16[64,768]{1,0:T(8,128)(2,1)}) %reduce-scatter.18.cloned.1.call-update) | async-done | bytes 98320 | tf_op jit(solution)/shard_map/reduce_scatter | solution.py:389
  558.6 37.9 %reduce-scatter.10.cloned.1.call-done = bf16[512,768]{1,0:T(8,128)(2,1)} async-done(((bf16[2048,768]{1,0:T(8,128)(2,1)}), bf16[512,768]{1,0:T(8,128)(2,1)}) %reduce-scatter.10.cloned.1.call-update) | async-done | bytes 786448 | tf_op jit(solution)/shard_map/reduce_scatter | solution.py:425
  598.4 39.5 %all-reduce.6 = f32[3,768]{1,0:T(4,128)S(1)} all-reduce(f32[3,768]{1,0:T(4,128)S(1)} %pad_maximum_fusion.4), channel_id=7, replica_groups=mesh['seq'=4,'fsdp'=8] {'seq','fsdp'}, use_global_device_ids=true, to_apply=%region_16.17.clone | all-reduce | flops 2304 | bytes 18432
  640.1 75.2 %reduce-scatter.20.cloned.1.call-done = bf16[24,3840]{1,0:T(8,128)(2,1)} async-done(((bf16[768,3840]{1,0:T(8,128)(2,1)}), bf16[24,3840]{1,0:T(8,128)(2,1)}) %reduce-scatter.20.cloned.1.call-update) | async-done | bytes 184336
  720.8 114.1 %reduce-scatter.16.cloned.1.call-done = bf16[24,4096]{1,0:T(8,128)(2,1)} async-done(((bf16[768,4096]{1,0:T(8,128)(2,1)}), bf16[24,4096]{1,0:T(8,128)(2,1)}) %reduce-scatter.16.cloned.1.call-update) | async-done | bytes 196624 | tf_op jit(solution)/shard_map/reduce_scatter | solution.py:395
  (259 shorter events, 88.2 us)
Async XLA Ops:
  7.2 7.9 copy-start.38
  7.2 8.7 %copy-start.34 = (f32[24,2048]{1,0:T(8,128)S(1)}, f32[24,2048]{1,0:T(8,128)}, u32[]{:S(2)}) copy-start(f32[24,2048]{1,0:T(8,128)} %param.31) | copy-start | bytes 589828
  7.2 8.7 %copy-start.35 = (f32[24,2048]{1,0:T(8,128)S(1)}, f32[24,2048]{1,0:T(8,128)}, u32[]{:S(2)}) copy-start(f32[24,2048]{1,0:T(8,128)} %param.32) | copy-start | bytes 589828
  7.2 9.5 %copy-start.36 = (f32[64,768]{1,0:T(8,128)S(1)}, f32[64,768]{1,0:T(8,128)}, u32[]{:S(2)}) copy-start(f32[64,768]{1,0:T(8,128)} %param.33) | copy-start | bytes 589828
  7.2 37.8 %all-gather.12.cloned.1.call-start = ((), (), s32[]{:S(2)}) async-start(), calls=%async_computation.16 | async-start | bytes 3932160 | tf_op jit(solution)/shard_map/all_gather | solution.py:339
  8.0 9.5 %copy-start.55 = (s32[15]{0:T(128)S(1)}, s32[15]{0:T(128)}, u32[]{:S(2)}) copy-start(s32[15]{0:T(128)} %constant.55.clone) | copy-start | bytes 184
  8.0 9.6 %copy-start.50 = (f32[32,3]{0,1:T(4,128)S(1)}, f32[32,3]{0,1:T(4,128)}, u32[]{:S(2)}) copy-start(f32[32,3]{0,1:T(4,128)} %param.34) | copy-start | bytes 1156
  8.0 10.5 %copy-start.37 = (bf16[1,128,768]{2,1,0:T(8,128)(2,1)S(1)}, bf16[1,128,768]{2,1,0:T(8,128)(2,1)}, u32[]{:S(2)}) copy-start(bf16[1,128,768]{2,1,0:T(8,128)(2,1)} %param.19) | copy-start | bytes 589828
  8.0 123.8 %all-gather.14.cloned.1.call-start = ((), (), s32[]{:S(2)}) async-start(), calls=%async_computation.17 | async-start | bytes 10137600 | tf_op jit(solution)/shard_map/all_gather | solution.py:349
  15.8 197.1 %all-gather.8.cloned.1.call-start = ((), (), s32[]{:S(2)}) async-start(), calls=%async_computation.9 | async-start | bytes 6488064 | tf_op jit(solution)/shard_map/all_gather | solution.py:350
  16.7 250.9 %all-gather.10.cloned.1.call-start = ((), (), s32[]{:S(2)}) async-start(), calls=%async_computation.10 | async-start | bytes 3244032 | tf_op jit(solution)/shard_map/all_gather | solution.py:351
  133.5 7.2 copy-start.40
  133.5 8.1 copy-start.14
  167.8 6.7 copy-start.39
  167.8 7.6 copy-start.26
  170.1 20.2 %all-to-all-start = ((bf16[4,512,192]{1,2,0:T(8,128)(2,1)}), bf16[4,512,192]{1,2,0:T(8,128)(2,1)S(1)}, u32[]{:S(2)}, u32[]{:S(2)}) async-start(bf16[4,512,192]{1,2,0:T(8,128)(2,1)} %copy.123), calls=%async_computation | async-start | bytes 1572864 | tf_op jit(solution)/shard_map/all_to_all | solution.py:371
  178.5 11.7 %copy-start.3 = (bf16[1,512,768]{2,1,0:T(8,128)(2,1)S(1)}, bf16[1,512,768]{2,1,0:T(8,128)(2,1)}, u32[]{:S(2)}) copy-start(bf16[1,512,768]{2,1,0:T(8,128)(2,1)} %param.18) | copy-start | bytes 2359300
  212.9 54.6 %copy-start.24 = (bf16[1,512,768]{2,1,0:T(8,128)(2,1)S(1)}, bf16[1,512,768]{2,1,0:T(8,128)(2,1)}, u32[]{:S(2)}) copy-start(bf16[1,512,768]{2,1,0:T(8,128)(2,1)} %param.20) | copy-start | bytes 2359300
  212.9 54.6 %copy-start.45 = (f32[512]{0:T(512)S(1)}, f32[512]{0:T(512)}, u32[]{:S(2)}) copy-start(f32[512]{0:T(512)} %fusion.57) | copy-start | bytes 6148
  267.5 8.8 %copy-start.5 = (bf16[768,4096]{1,0:T(8,128)(2,1)S(1)}, bf16[768,4096]{1,0:T(8,128)(2,1)}, u32[]{:S(2)}) copy-start(bf16[768,4096]{1,0:T(8,128)(2,1)} %all-gather.8.cloned.1.call-done) | copy-start | bytes 18874372
  283.5 14.4 %copy-start.7 = (f32[512,768]{1,0:T(8,128)S(1)}, f32[512,768]{1,0:T(8,128)}, u32[]{:S(2)}) copy-start(f32[512,768]{1,0:T(8,128)} %copy-done.6) | copy-start | bytes 4718596
  283.5 14.4 %copy-start.48 = (f32[512]{0:T(512)S(1)}, f32[512]{0:T(512)}, u32[]{:S(2)}) copy-start(f32[512]{0:T(512)} %copy-done.47) | copy-start | bytes 6148
  306.6 15.9 %all-to-all-start.1 = ((bf16[512,4,192]{0,2,1:T(8,128)(2,1)}), bf16[512,4,192]{0,2,1:T(8,128)(2,1)}, u32[]{:S(2)}, u32[]{:S(2)}) async-start(bf16[512,4,192]{0,2,1:T(8,128)(2,1)} %bitcast.124), calls=%async_computation.1 | async-start | bytes 1572864 | tf_op jit(solution)/shard_map/all_to_all | solution.py:419
  310.7 124.4 %reduce-scatter.14.cloned.1.call-start = ((), (), s32[]{:S(2)}) async-start(), calls=%async_computation.13 | async-start | bytes 1327104 | tf_op jit(solution)/shard_map/reduce_scatter | solution.py:428
  361.1 88.4 %reduce-scatter.12.cloned.1.call-start = ((), (), s32[]{:S(2)}) async-start(), calls=%async_computation.12 | async-start | bytes 983040 | tf_op jit(solution)/shard_map/reduce_scatter | solution.py:409
  365.4 191.7 %reduce-scatter.18.cloned.1.call-start = ((), (), s32[]{:S(2)}) async-start(), calls=%async_computation.15 | async-start | bytes 3244032 | tf_op jit(solution)/shard_map/reduce_scatter | solution.py:389
  371.1 225.4 %reduce-scatter.10.cloned.1.call-start = ((), (), s32[]{:S(2)}) async-start(), calls=%async_computation.11 | async-start | bytes 3932160 | tf_op jit(solution)/shard_map/reduce_scatter | solution.py:425
  377.6 337.7 %reduce-scatter.20.cloned.1.call-start = ((), (), s32[]{:S(2)}) async-start(), calls=%async_computation.18 | async-start | bytes 6082560
  396.9 438.0 %reduce-scatter.16.cloned.1.call-start = ((), (), s32[]{:S(2)}) async-start(), calls=%async_computation.14 | async-start | bytes 6488064 | tf_op jit(solution)/shard_map/reduce_scatter | solution.py:395
  435.2 16.0 %all-to-all-start.2 = ((bf16[4,24,768]{2,1,0:T(8,128)(2,1)}), bf16[4,24,768]{2,1,0:T(8,128)(2,1)S(1)}, u32[]{:S(2)}, u32[]{:S(2)}) async-start(bf16[4,24,768]{2,1,0:T(8,128)(2,1)} %bitcast.142), calls=%async_computation.5 | async-start | bytes 294912 | tf_op jit(solution)/shard_map/all_to_all | solution.py:429
  438.5 158.0 %copy-start.4 = (bf16[1,512,768]{2,1,0:T(8,128)(2,1)S(1)}, bf16[1,512,768]{2,1,0:T(8,128)(2,1)}, u32[]{:S(2)}) copy-start(bf16[1,512,768]{2,1,0:T(8,128)(2,1)} %param.18) | copy-start | bytes 2359300
  596.5 42.0 %copy-start.13 = (bf16[512,768]{1,0:T(8,128)(2,1)S(1)}, bf16[512,768]{1,0:T(8,128)(2,1)}, u32[]{:S(2)}) copy-start(bf16[512,768]{1,0:T(8,128)(2,1)} %reduce-scatter.10.cloned.1.call-done) | copy-start | bytes 2359300
  (42 other events, 103.8 us)
Sparse Core Ops, SparseCore 0:
  9.6 35.4 all-gather.11
  48.5 83.1 all-gather.13
  135.3 70.3 all-gather.7
  208.4 59.0 all-gather.9
  361.2 63.5 reduce-scatter.13
  427.2 22.1 reduce-scatter.11
  454.9 102.1 reduce-scatter.17
  559.6 36.8 reduce-scatter.9
  602.2 113.1 reduce-scatter.19
  720.8 114.0 reduce-scatter.15

commit v2 on v1

--- a/solution.py
+++ b/solution.py
@@ -291,6 +291,327 @@
     return forward, backward
 
 
+MESH = pl.DeviceIdType.MESH
+
+
+def coordinates():
+    place, slot = lax.axis_index("seq"), lax.axis_index("fsdp")
+    return place // 2, lax.rem(place, 2), slot // 2, lax.rem(slot, 2)
+
+
+def device(x, c, z, y):
+    return (x * 2 + c, z * 2 + y)
+
+
+def greet(others):
+    barrier = pltpu.get_barrier_semaphore()
+    for other in others:
+        pl.semaphore_signal(barrier, inc=1, device_id=other, device_id_type=MESH)
+    pl.semaphore_wait(barrier, len(others))
+
+
+class Copies:
+    def __init__(self, send_sem, recv_sem):
+        self.send_sem, self.recv_sem, self.made = send_sem, recv_sem, []
+
+    def send(self, source, target, other):
+        number = len(self.made)
+        copy = pltpu.make_async_remote_copy(
+            src_ref=source, dst_ref=target, send_sem=self.send_sem.at[number], recv_sem=self.recv_sem.at[number],
+            device_id=other, device_id_type=MESH,
+        )
+        copy.start()
+        self.made.append(copy)
+        return copy
+
+    def finish(self):
+        for copy in self.made:
+            copy.wait_send()
+
+
+def gather_kernel(nz, tok, enc, own, squares, gain, everyone, encoded, qkv_out, squares_out, gain_out, send_sem, recv_sem, local_sem):
+    x, c, z, y = coordinates()
+    flat = device(1 - x, c, z, y), device(x, 1 - c, z, y), device(1 - x, 1 - c, z, y)
+    by_x, by_core, diagonal = flat
+    by_y = device(x, c, z, 1 - y)
+    steps = [lax.rem(z + t, nz) for t in range(nz)]
+    backs = [lax.rem(z - t + nz, nz) for t in range(nz)]
+    by_z = [device(x, c, steps[t], y) for t in range(nz)]
+    greet([*flat, by_y, *by_z[1:]])
+    copies = Copies(send_sem, recv_sem)
+    local = [
+        pltpu.make_async_copy(source, target, local_sem.at[n])
+        for n, (source, target) in enumerate(
+            [
+                (own.at[x, c], qkv_out.at[x, c, z, y]),
+                (tok, everyone.at[x, c]),
+                (enc, encoded.at[x, c]),
+                (squares, squares_out.at[:, x, c, z, y]),
+                (gain, gain_out.at[x, c, z, y]),
+            ]
+        )
+    ]
+    for copy in local:
+        copy.start()
+    first = [
+        copies.send(own.at[1 - x, c], qkv_out.at[x, c, z, y], by_x),
+        copies.send(own.at[x, 1 - c], qkv_out.at[x, c, z, y], by_core),
+        copies.send(own.at[1 - x, 1 - c], qkv_out.at[x, c, z, y], diagonal),
+    ]
+    rows_x = [copies.send(enc, encoded.at[x, c], by_x), copies.send(tok, everyone.at[x, c], by_x)]
+    rows_core = [copies.send(enc, encoded.at[x, c], by_core), copies.send(tok, everyone.at[x, c], by_core)]
+
+    def relay(xx, cc, zz, yy, other):
+        return [
+            copies.send(squares_out.at[:, xx, cc, zz, yy], squares_out.at[:, xx, cc, zz, yy], other),
+            copies.send(gain_out.at[xx, cc, zz, yy], gain_out.at[xx, cc, zz, yy], other),
+        ]
+
+    def fresh(other):
+        return [
+            copies.send(squares, squares_out.at[:, x, c, z, y], other),
+            copies.send(gain, gain_out.at[x, c, z, y], other),
+        ]
+
+    def arrive(pair):
+        for copy in pair:
+            copy.wait_recv()
+
+    for copy in local:
+        copy.wait()
+    arrive(first)
+    qkv_z = [None] + [copies.send(qkv_out.at[:, :, z, y], qkv_out.at[:, :, z, y], by_z[t]) for t in range(1, nz)]
+    qkv_y = [copies.send(qkv_out.at[:, :, z, y], qkv_out.at[:, :, z, y], by_y)]
+    squares_z = [None] + [fresh(by_z[t]) for t in range(1, nz)]
+    squares_y, squares_x, squares_core = [fresh(by_y)], [fresh(by_x)], [fresh(by_core)]
+    for t in range(1, nz):
+        qkv_z[t].wait_recv()
+        qkv_y.append(copies.send(qkv_out.at[:, :, backs[t], y], qkv_out.at[:, :, backs[t], y], by_y))
+    for t in range(1, nz):
+        arrive(squares_z[t])
+        squares_y.append(relay(x, c, backs[t], y, by_y))
+        squares_x.append(relay(x, c, backs[t], y, by_x))
+        squares_core.append(relay(x, c, backs[t], y, by_core))
+    for copy, target in zip(rows_x, (encoded, everyone)):
+        copy.wait_recv()
+        rows_core.append(copies.send(target.at[1 - x, c], target.at[1 - x, c], by_core))
+    corner = []
+    for t in range(nz):
+        arrive(squares_x[t])
+        if t % 2 == 0:
+            corner.append(relay(1 - x, c, backs[t], y, by_y))
+        squares_core.append(relay(1 - x, c, backs[t], y, by_core))
+        arrive(squares_y[t])
+        if t % 2 == 1:
+            corner.append(relay(x, c, backs[t], 1 - y, by_x))
+        squares_core.append(relay(x, c, backs[t], 1 - y, by_core))
+    for t in range(nz):
+        arrive(corner[t])
+        squares_core.append(relay(1 - x, c, backs[t], 1 - y, by_core))
+    for copy in qkv_y + rows_core:
+        copy.wait_recv()
+    for pair in squares_core:
+        arrive(pair)
+    copies.finish()
+
+
+def gather(nz, tok, enc, own, squares, gain):
+    count, share, width = squares.shape
+    everywhere = (2, 2, nz, 2)
+    shapes = [
+        jax.ShapeDtypeStruct((2, 2, *tok.shape), tok.dtype),
+        jax.ShapeDtypeStruct((2, 2, *enc.shape), enc.dtype),
+        jax.ShapeDtypeStruct((*everywhere, share, own.shape[-1]), own.dtype),
+        jax.ShapeDtypeStruct((count, *everywhere, share, width), squares.dtype),
+        jax.ShapeDtypeStruct((*everywhere, *gain.shape), gain.dtype),
+    ]
+    total = 3 + 6 + 2 * nz - 1 + 2 * (nz - 1 + 2 * nz + nz + 4 * nz)
+    return pl.pallas_call(
+        functools.partial(gather_kernel, nz),
+        in_specs=[pl.BlockSpec(memory_space=pltpu.VMEM)] * 5,
+        out_specs=[pl.BlockSpec(memory_space=pl.ANY)] * 5,
+        out_shape=shapes,
+        scratch_shapes=[
+            pltpu.SemaphoreType.DMA((total,)), pltpu.SemaphoreType.DMA((total,)), pltpu.SemaphoreType.DMA((5,)),
+        ],
+        compiler_params=pltpu.CompilerParams(collective_id=0, has_side_effects=True, vmem_limit_bytes=8 * 2**20),
+        name="gather",
+    )(tok, enc, own, squares, gain)
+
+
+def add_low(target, left, right):
+    @pl.loop(0, left.shape[0])
+    def _(n):
+        target[n] = (left[n].astype(jnp.float32) + right[n].astype(jnp.float32)).astype(target.dtype)
+
+
+def reduce_kernel(
+    nz, count, *refs
+):
+    squares = refs[:count]
+    own, tok, enc, gain, near = refs[count : count + 5]
+    out_squares, out_own, out_tok, out_enc, out_gain, out_near = refs[count + 5 : count + 11]
+    (sq_a, sq_ra, sq_b, sq_rb, sq_c, sq_rc, sq_rd, own_r, own_a, own_rz, own_f,
+     tok_r, tok_a, tok_rx, enc_r, enc_a, enc_rx, gain_r, near_r, send_sem, recv_sem) = refs[count + 11 :]
+    x, c, z, y = coordinates()
+    flat = device(1 - x, c, z, y), device(x, 1 - c, z, y), device(1 - x, 1 - c, z, y)
+    by_x, by_core, diagonal = flat
+    by_y = device(x, c, z, 1 - y)
+    world = 8 * nz
+    place, slot = lax.axis_index("seq"), lax.axis_index("fsdp")
+    slots = 2 * nz
+    me = place * slots + slot
+    steps = [lax.rem(z + t, nz) for t in range(nz)]
+    by_z = [device(x, c, steps[t], y) for t in range(nz)]
+    barrier = pltpu.get_barrier_semaphore()
+
+    @pl.loop(1, world)
+    def _(t):
+        other = lax.rem(me + t, world)
+        pl.semaphore_signal(barrier, inc=1, device_id=(other // slots, lax.rem(other, slots)), device_id_type=MESH)
+
+    pl.semaphore_wait(barrier, world - 1)
+    copies = Copies(send_sem, recv_sem)
+    tok_core = copies.send(tok.at[:, 1 - c], tok_r, by_core)
+    enc_core = copies.send(enc.at[:, 1 - c], enc_r, by_core)
+    own_y = copies.send(own.at[:, :, :, 1 - y], own_r, by_y)
+    sq_core = [copies.send(squares[n].at[:, 1 - c], sq_ra.at[n], by_core) for n in range(count)]
+    near_all = []
+    for t in range(1, slots):
+        other = lax.rem(slot + t, slots)
+        near_all.append(copies.send(near, near_r.at[t - 1], (place, other)))
+
+    def gain_copy(t):
+        other = lax.rem(me + t, world)
+        return pltpu.make_async_remote_copy(
+            src_ref=gain.at[other], dst_ref=gain_r.at[t - 1], send_sem=send_sem.at[t - 1 + base_gain],
+            recv_sem=recv_sem.at[t - 1 + base_gain],
+            device_id=(other // slots, lax.rem(other, slots)), device_id_type=MESH,
+        )
+
+    base_gain = send_sem.shape[0] - (world - 1)
+
+    @pl.loop(1, world)
+    def _(t):
+        gain_copy(t).start()
+
+    tok_core.wait_recv()
+    for half in range(2):
+        add_low(tok_a.at[half], tok.at[half, c], tok_r.at[half])
+    tok_x = copies.send(tok_a.at[1 - x], tok_rx, by_x)
+    enc_core.wait_recv()
+    for half in range(2):
+        add_low(enc_a.at[half], enc.at[half, c], enc_r.at[half])
+    enc_x = copies.send(enc_a.at[1 - x], enc_rx, by_x)
+
+    sq_y, sq_x, sq_z = [], [], []
+    for n in range(count):
+        sq_core[n].wait_recv()
+
+        for half in range(2):
+            for side in range(2):
+                add_low(sq_a.at[n, half, :, side], squares[n].at[half, c, :, side], sq_ra.at[n, half, :, side])
+        sq_y.append(copies.send(sq_a.at[n, :, :, 1 - y], sq_rb.at[n], by_y))
+
+    own_y.wait_recv()
+    for half in range(2):
+        for core in range(2):
+            add_low(own_a.at[half, core], own.at[half, core, :, y], own_r.at[half, core])
+    own_z = [copies.send(own_a.at[:, :, steps[t]], own_rz.at[t - 1], by_z[t]) for t in range(1, nz)]
+    for n in range(count):
+        sq_y[n].wait_recv()
+        for half in range(2):
+            add_low(sq_b.at[n, half], sq_a.at[n, half, :, y], sq_rb.at[n, half])
+        sq_x.append(copies.send(sq_b.at[n, 1 - x], sq_rc.at[n], by_x))
+    for copy in own_z:
+        copy.wait_recv()
+    for half in range(2):
+        for core in range(2):
+            total = own_a[half, core, z].astype(jnp.float32)
+            for t in range(nz - 1):
+                total += own_rz[t, half, core].astype(jnp.float32)
+            own_f[half, core] = total.astype(own_f.dtype)
+    own_seq = [
+        copies.send(own_f.at[1 - x, c], out_own.at[x, c], by_x),
+        copies.send(own_f.at[x, 1 - c], out_own.at[x, c], by_core),
+        copies.send(own_f.at[1 - x, 1 - c], out_own.at[x, c], diagonal),
+    ]
+    out_own[x, c] = own_f[x, c]
+    for n in range(count):
+        sq_x[n].wait_recv()
+        add_low(sq_c.at[n], sq_b.at[n, x], sq_rc.at[n])
+        sq_z.append([copies.send(sq_c.at[n, steps[t]], sq_rd.at[n, t - 1], by_z[t]) for t in range(1, nz)])
+    tok_x.wait_recv()
+    add_low(out_tok, tok_a.at[x], tok_rx)
+    enc_x.wait_recv()
+    add_low(out_enc, enc_a.at[x], enc_rx)
+    for n in range(count):
+        for copy in sq_z[n]:
+            copy.wait_recv()
+        total = sq_c[n, z].astype(jnp.float32)
+        for t in range(nz - 1):
+            total += sq_rd[n, t].astype(jnp.float32)
+        out_squares[n] = total
+    for copy in near_all:
+        copy.wait_recv()
+    total = near[...]
+    for t in range(slots - 1):
+        total += near_r[t]
+    out_near[...] = total
+    out_gain[...] = gain[me]
+
+    @pl.loop(1, world)
+    def _(t):
+        gain_copy(t).wait_recv()
+        out_gain[...] += gain_r[t - 1]
+
+    for copy in own_seq:
+        copy.wait_recv()
+    copies.finish()
+
+    @pl.loop(1, world)
+    def _(t):
+        gain_copy(t).wait_send()
+
+
+def reduce(nz, squares, own, tok, enc, gain, near):
+    count = len(squares)
+    share, width = squares[0].shape[-2:]
+    low = jnp.bfloat16
+    vmem = lambda *shape: pltpu.VMEM(shape, low)
+    tok_slabs, enc_slabs = tok.shape[2:], enc.shape[2:]
+    world = 8 * nz
+    total = 3 + count + 2 * nz - 1 + 2 + count * 2 + (nz - 1) * (count + 1) + 3 + world - 1
+    wide = own.shape[-1]
+    return pl.pallas_call(
+        functools.partial(reduce_kernel, nz, count),
+        in_specs=[pl.BlockSpec(memory_space=pltpu.VMEM)] * (count + 5),
+        out_specs=[pl.BlockSpec(memory_space=pltpu.VMEM)] * 6,
+        out_shape=[
+            jax.ShapeDtypeStruct((count, share, width), jnp.float32),
+            jax.ShapeDtypeStruct((2, 2, share, wide), low),
+            jax.ShapeDtypeStruct(tok_slabs, jnp.float32),
+            jax.ShapeDtypeStruct(enc_slabs, jnp.float32),
+            jax.ShapeDtypeStruct(gain.shape[1:], jnp.float32),
+            jax.ShapeDtypeStruct(near.shape, jnp.float32),
+        ],
+        scratch_shapes=[
+            vmem(count, 2, nz, 2, share, width), vmem(count, 2, nz, 2, share, width),
+            vmem(count, 2, nz, share, width), vmem(count, 2, nz, share, width),
+            vmem(count, nz, share, width), vmem(count, nz, share, width),
+            vmem(count, nz - 1, share, width),
+            vmem(2, 2, nz, share, wide), vmem(2, 2, nz, share, wide), vmem(nz - 1, 2, 2, share, wide), vmem(2, 2, share, wide),
+            vmem(2, *tok_slabs), vmem(2, *tok_slabs), vmem(*tok_slabs),
+            vmem(2, *enc_slabs), vmem(2, *enc_slabs), vmem(*enc_slabs),
+            pltpu.VMEM((world - 1, *gain.shape[1:]), jnp.float32),
+            pltpu.VMEM((2 * nz - 1, *near.shape), jnp.float32),
+            pltpu.SemaphoreType.DMA((total,)), pltpu.SemaphoreType.DMA((total,)),
+        ],
+        compiler_params=pltpu.CompilerParams(collective_id=1, has_side_effects=True, vmem_limit_bytes=60 * 2**20),
+        name="reduce",
+    )(*squares, own, tok, enc, gain, near)
+
+
 def matmul_t(left, right):
     return nt(left, right)
 
@@ -336,31 +657,35 @@
     heads = width // HEAD
     place = lax.axis_index("seq")
 
-    everyone = lax.all_gather(tokens[0], "seq", axis=0, tiled=True)
-    encoded = lax.all_gather(encoder[0], "seq", axis=0, tiled=True)
-
+    aligned = share % 8 == 0
+    nz = fsdp // 2
     gain_share = gains.shape[1]
-    gain_block = jnp.pad(gains.astype(low).reshape(1, -1), ((0, 7), (0, width - gains.size)))
-    pack = jnp.concatenate(
-        [w.astype(low) for w in (self_query, self_key, self_value, self_output, cross_query, cross_key, cross_value, cross_output)]
-        + [gain_block],
-        axis=0,
-    )
-    packed = lax.all_gather(pack, both, axis=0)
+    masters = (self_output, cross_query, cross_key, cross_value, cross_output)
     gate_up = lax.all_gather(jnp.concatenate([ffn_gate.astype(low), ffn_up.astype(low)], axis=1), both, axis=0, tiled=True)
     w_down = lax.all_gather(ffn_down.astype(low), both, axis=0, tiled=True)
-
-    def whole(number):
-        return packed[:, number * share : (number + 1) * share].reshape(width, width)
-
-    w_output, c_query, c_key, c_value, c_output = (whole(n) for n in range(3, 8))
-
-    def own(number):
-        cut = lax.dynamic_slice_in_dim(whole(number), place * group_width, group_width, 1)
-        return jnp.pad(cut, ((0, 0), (0, padded - group_width)))
-
-    w_qkv = jnp.concatenate([own(n) for n in range(3)], axis=1)
-    gain_rows = packed[:, 8 * share, : gains.size].reshape(world, 3, gain_share).transpose(1, 0, 2).reshape(3, width).astype(jnp.float32)
+    own = jnp.stack([w.astype(low).reshape(share, seq, group_width) for w in (self_query, self_key, self_value)])
+    own = jnp.pad(own, ((0, 0), (0, 0), (0, 0), (0, padded - group_width))).transpose(2, 1, 0, 3).reshape(seq, share, 3 * padded)
+    squares = jnp.stack([w.astype(low) for w in masters])
+    gain_block = gains.astype(low).astype(jnp.float32).reshape(1, -1)
+    gain_block = jnp.pad(gain_block, ((0, 7), (0, LANES - gains.size)))
+    if aligned:
+        everyone, encoded, w_qkv, squares, gain_rows = gather(
+            nz, tokens[0], encoder[0], own.reshape(2, 2, share, 3 * padded), squares, gain_block
+        )
+    else:
+        everyone = lax.all_gather(tokens[0], "seq", axis=0)
+        encoded = lax.all_gather(encoder[0], "seq", axis=0)
+        w_qkv = lax.all_to_all(own, "seq", split_axis=0, concat_axis=0, tiled=True)
+        w_qkv = lax.all_gather(w_qkv, "fsdp", axis=1)
+        squares = jnp.moveaxis(lax.all_gather(squares, both, axis=0), 1, 0)
+        gain_rows = lax.all_gather(gain_block, both, axis=0)
+    everyone = everyone.reshape(seq * rows, width)
+    encoded = encoded.reshape(-1, width)
+    w_qkv = w_qkv.reshape(width, 3 * padded)
+    squares = squares.reshape(5, width, width)
+    w_output, c_query, c_key, c_value, c_output = (squares[n] for n in range(5))
+    gain_rows = gain_rows.reshape(world, 8, LANES)[:, 0, : gains.size]
+    gain_rows = gain_rows.reshape(world, 3, gain_share).transpose(1, 0, 2).reshape(3, width)
 
     length = lengths[0]
     values_in = tokens[0].astype(jnp.float32)
@@ -406,44 +731,63 @@
     grad_ckey = inner_rows(encoded, grad_ck).astype(low)
     grad_cvalue = inner_rows(encoded, grad_cv).astype(low)
     grad_encoded_part = (matmul_t(grad_ck, c_key) + matmul_t(grad_cv, c_value)).astype(low)
-    grad_encoded = lax.psum_scatter(grad_encoded_part, "seq", scatter_dimension=0, tiled=True).astype(jnp.float32)
     norm_part, grad_gain_one = rms_back(attended, gain_rows[1], matmul_t(grad_cq, c_query))
     grad_attended = grad_crossed + norm_part
     grad_self_branch = grad_attended.astype(low)
     grad_output = inner_rows(mixed, grad_self_branch).astype(low)
     grad_mixed = matmul_t(grad_self_branch, w_output).astype(low)
-    share_square = lax.psum_scatter(
-        jnp.concatenate([grad_output, grad_cquery, grad_ckey, grad_cvalue, grad_coutput], axis=1),
-        both, scatter_dimension=0, tiled=True,
-    )
     own_grad_mixed = lax.all_to_all(grad_mixed, "seq", split_axis=1, concat_axis=0, tiled=True)
     own_grad_mixed = jnp.pad(own_grad_mixed, ((0, 0), (0, padded - group_width)))
     own_dq, own_dk, own_dv, near = attend_backward(
         qkv, qkv, qkv, own_grad_mixed, own_mixed, own_logsum, group, HEAD, padded, base_backward, lengths
     )
     own_qkv = jnp.concatenate([own_dq, own_dk, own_dv], axis=1)
-    grad_normed = lax.psum_scatter(matmul_t(own_qkv, w_qkv).astype(low), "seq", scatter_dimension=0, tiled=True)
+    grad_normed_part = matmul_t(own_qkv, w_qkv)
+    values_all = everyone.astype(jnp.float32)
+    units_all = values_all * lax.rsqrt(jnp.mean(values_all * values_all, axis=-1, keepdims=True) + epsilon)
+    grad_gain_zero = jnp.sum(grad_normed_part * units_all, axis=0)
+    grad_normed_part = grad_normed_part.astype(low)
     grad_own = inner_rows(normed_all, own_qkv).astype(low)
-    grad_own = grad_own.reshape(seq, fsdp, share, 3 * padded).transpose(1, 0, 2, 3)
-    grad_own = lax.psum_scatter(grad_own, "fsdp", scatter_dimension=0, tiled=True)[0]
-    grad_own = lax.all_to_all(grad_own, "seq", split_axis=0, concat_axis=0, tiled=True)
+    grad_gains = jnp.stack([grad_gain_zero, grad_gain_one, grad_gain_two])
+    grad_gains = grad_gains.reshape(3, world, gain_share).transpose(1, 0, 2).reshape(world, 1, 3 * gain_share)
+    grad_gains = jnp.pad(grad_gains, ((0, 0), (0, 7), (0, LANES - 3 * gain_share)))
+    skew = jnp.pad(near.reshape(group, -1), ((0, 0), (0, LANES))).reshape(group, LANES, 2 * LANES + 1)
+    by_distance = jnp.pad(jnp.sum(skew[:, :, :LANES], axis=1), ((0, 8 - group), (0, 0)))
+    grad_squares = [grad_output, grad_cquery, grad_ckey, grad_cvalue, grad_coutput]
+    if aligned:
+        slab = 64
+        share_square, grad_own, grad_normed, grad_encoded, share_gains, by_distance = reduce(
+            nz,
+            [g.reshape(2, 2, nz, 2, share, width) for g in grad_squares],
+            grad_own.reshape(2, 2, nz, 2, share, 3 * padded),
+            grad_normed_part.reshape(2, 2, -1, slab, width),
+            grad_encoded_part.reshape(2, 2, -1, slab, width),
+            grad_gains,
+            by_distance,
+        )
+        grad_normed, grad_encoded = grad_normed.reshape(rows, width), grad_encoded.reshape(-1, width)
+        grad_own = grad_own.reshape(seq, share, 3 * padded)
+    else:
+        share_square = lax.psum_scatter(jnp.concatenate(grad_squares, axis=1), both, scatter_dimension=0, tiled=True)
+        share_square = share_square.reshape(share, 5, width).transpose(1, 0, 2)
+        grad_own = grad_own.reshape(seq, fsdp, share, 3 * padded).transpose(1, 0, 2, 3)
+        grad_own = lax.psum_scatter(grad_own, "fsdp", scatter_dimension=0, tiled=True)[0]
+        grad_own = lax.all_to_all(grad_own, "seq", split_axis=0, concat_axis=0, tiled=True)
+        grad_normed = lax.psum_scatter(grad_normed_part, "seq", scatter_dimension=0, tiled=True).astype(jnp.float32)
+        grad_encoded = lax.psum_scatter(grad_encoded_part, "seq", scatter_dimension=0, tiled=True).astype(jnp.float32)
+        share_gains = lax.psum_scatter(grad_gains, both, scatter_dimension=0, tiled=True)[0]
+        by_distance = lax.psum(by_distance, "fsdp")
+    share_gains = share_gains[0, : 3 * gain_share].reshape(3, gain_share)
     grad_own = grad_own.reshape(seq, share, 3, padded)[:, :, :, :group_width].transpose(2, 1, 0, 3).reshape(3, share, width)
-
-    norm_part, grad_gain_zero = rms_back(values_in, gain_rows[0], grad_normed.astype(jnp.float32))
+    norm_part, _ = rms_back(values_in, gain_rows[0], grad_normed)
     grad_input = grad_attended + norm_part
-    grad_gains = jnp.stack([grad_gain_zero, grad_gain_one, grad_gain_two])
-    share_gains = lax.psum_scatter(grad_gains, both, scatter_dimension=1, tiled=True)
-
     bins = rel_bias.shape[0]
-    skew = jnp.pad(near.reshape(group, -1), ((0, 0), (0, LANES))).reshape(group, LANES, 2 * LANES + 1)
-    by_distance = jnp.sum(skew[:, :, :LANES], axis=1)
     near_map = (buckets(jnp.arange(LANES, dtype=jnp.int32))[:, None] == jnp.arange(bins - 1, dtype=jnp.int32)[None]).astype(jnp.float32)
-    near_sums = jnp.dot(near_map.T, by_distance.T, precision=highest)
-    grad_table = jnp.concatenate([near_sums, -jnp.sum(near_sums, axis=0, keepdims=True)], axis=0)
-    table_grad = lax.psum(grad_table, "fsdp")
+    near_sums = jnp.dot(near_map.T, by_distance[:group].T, precision=highest)
+    table_grad = jnp.concatenate([near_sums, -jnp.sum(near_sums, axis=0, keepdims=True)], axis=0)
 
     wide = jnp.float32
-    outputs = [share_square[:, n * width : (n + 1) * width].astype(wide) for n in range(5)]
+    outputs = [share_square[n].astype(wide) for n in range(5)]
     own_outputs = [grad_own[n].astype(wide) for n in range(3)]
     return (
         result.astype(low)[None], grad_input[None], grad_encoded[None], share_gains,

time: 854 us -> 462 us (0.54)
  waiting for transfers between devices: 503 us -> 10.6 us
  Pallas kernels: 77.8 us -> 255 us
  blocking collectives: 74.8 us -> 0 us
  matrix products: 88.2 us -> 98.4 us
    pallas_call x0 -> x2, Pallas kernels: none -> 178 us  [the longest x1 104 us: reduce(): pl.pallas_call(functools.partial(reduce_kernel, nz, count), in_specs=[pl....]
    reduce_scatter x1, waiting for transfers between devices: 114 us -> 8.47 us  [per_device(): lax.psum_scatter(grad_gate_up, both, scatter_dimension=0, tiled=True)]
    reduce_scatter x1, waiting for transfers between devices: 103 us -> 0.01 us  [per_device(): lax.psum_scatter(grad_down, both, scatter_dimension=0, tiled=True)]
    all_gather x2 -> x0, waiting for transfers between devices: 94 us -> none  [the longest x1 83.5 us: per_device(): packed = lax.all_gather(pack, both, axis=0)]
    unnamed x11 -> x4, waiting for transfers between devices: 76 us -> 0.07 us
    reduce_scatter x3 -> x0, waiting for transfers between devices: 48.8 us -> none  [the longest x1 37.9 us: per_device(): lax.psum_scatter(matmul_t(own_qkv, w_qkv).astype(low), 'seq', scatter_dim...]
    all_gather x1, waiting for transfers between devices: 45.9 us -> 0.01 us  [per_device(): w_down = lax.all_gather(ffn_down.astype(low), both, axis=0, tiled=True)]
    unnamed x1 -> x0, blocking collectives: 39.5 us -> none
  transfers between devices with their start and end apart: 13 -> 6, of which waited for: 10 -> 2; matrix products, arithmetic and copies ran while one was open for 14% -> 29% of each run, Pallas kernels for 4% -> 56%
where the time goes in v2:
time: 462 us; the launch traced here: 453 us
  Pallas kernels  255 us (55%)
  matrix products  98.4 us (21%)
  local copies, waits for them, and re-layouts  41.9 us (9%)
  other arithmetic  22.8 us (5%)
  between operations  15.5 us (3%)
  waiting for transfers between devices  10.6 us (2%)
  starting transfers between devices  9.34 us (2%)
    pallas_call x1, Pallas kernels, reduce(): pl.pallas_call(functools.partial(reduce_kernel, nz, count), in_specs=[pl....  104 us
    pallas_call x1, Pallas kernels, gather(): pl.pallas_call(functools.partial(gather_kernel, nz), in_specs=[pl.BlockSp...  73.7 us
    pallas_call x2, Pallas kernels, attend_backward(): pl.pallas_call(functools.partial(attend_backward_kernel, causal=causal, h...  40.8 us
    pallas_call x2, Pallas kernels, attend_forward(): pl.pallas_call(functools.partial(attend_forward_kernel, causal=causal, he...  35.8 us
    dot_general x8, matrix products, nt(): lax.dot_general(left, right, (((1,), (1,)), ((), ())), preferred_element_...  34 us
    dot_general x8, matrix products, nn(): return jnp.dot(left, right, preferred_element_type=jnp.float32)  33.3 us
    dot_general x8, matrix products, inner_rows(): lax.dot_general(left, right, (((0,), (0,)), ((), ())), preferred_element_...  30.2 us
    unnamed x125, local copies, waits for them, and re-layouts  17 us
  transfers between devices with their start and end apart: 6, of which 2 were waited for; matrix products, arithmetic and copies ran while one was open for 29% of the time, Pallas kernels for 56%

profile of v2, /device:TPU:0, one launch (start us, length us, event | category | flops | bytes accessed | tf_op | source)
XLA Modules:
  0.0 453.3 jit_solution(3711188499622599381)
XLA Ops:
  15.3 73.7 %gather.1 = (bf16[2,2,512,768]{3,2,1,0:T(8,128)(2,1)S(1)}, bf16[2,2,128,768]{3,2,1,0:T(8,128)(2,1)S(1)}, bf16[2,2,4,2,24,768]{5,4,3,2,1,0:T(8,128)(2,1)S(1)}, bf...) custom-call(bf16[512,768]{1,0:T(8,128)(2,1)S(1)} %bitcast.134, bf16[128,768]{1,0:T(8,128)(2,1)S(1)} %bitcast.136, ...), custom_call_target="tpu_custom_call" | custom-call | tf_op jit(solution)/shard_map/gather/pallas_call | solution.py:429
  89.0 2.5 copy-done.2
  97.5 3.9 convolution_convert_fusion.2.refs_1_.refs_2_.refs_3_
  101.5 20.3 %self_forward.1 = (bf16[2048,256]{1,0:T(8,128)(2,1)}, f32[3,8,2048]{2,1,0:T(8,128)}) custom-call(s32[1]{0:T(128)} %copy.120.refs_0_, bf16[2048,768]{1,0:T(8,128)(2,1)} %convolution_convert_fusion.2.refs_1_.refs_2_.refs_3_, bf16[2048,768]{1,0:T(8,128)(2,1)} %convolution_convert_fusion.2.refs_1_.refs_2_.refs_3_, ...), custom_call_target="tpu_custom_call" | custom-call | flops 3221225472 | bytes 4194304 | tf_op jit(solution)/shard_map/self_forward/pallas_call | solution.py:107
  121.8 2.2 copy.95
  124.0 4.2 all-to-all-start
  129.9 5.4 %fusion.43 = (bf16[1,2,2,4,2,24,768]{6,5,4,3,2,1,0:T(8,128)(2,1)}, bf16[1,2,2,4,2,24,768]{6,5,4,3,2,1,0:T(8,128)(2,1)}, bf16[1,2,2,4,2,24,768]{6,5,4,3,2,1,0:T(8...) fusion(bf16[5,2,2,4,2,24,768]{6,5,4,3,2,1,0:T(8,128)(2,1)} %copy-done.2), kind=kLoop, calls=%fused_computation.139 | loop fusion | bytes 11796480 | tf_op jit(solution)/shard_map/slice | solution.py:686
  135.6 3.3 convolution_convert_fusion.11.refs_2_
  142.7 2.8 multiply_reduce_fusion.7
  148.3 15.4 %cross_forward.1 = (bf16[512,768]{1,0:T(8,128)(2,1)}, f32[12,8,512]{2,1,0:T(8,128)}) custom-call(bf16[512,768]{1,0:T(8,128)(2,1)} %convolution_convert_fusion.13.refs_0_, bf16[512,768]{1,0:T(8,128)(2,1)} %convolution_convert_fusion.12.refs_1_, bf16[512,768]{1,0:T(8,128)(2,1)} %convolution_convert_fusion.11.refs_2_), custom_call_target="tpu_custom_call" | custom-call | flops 1610612736 | bytes 3145728 | tf_op jit(solution)/shard_map/cross_forward/pallas_call | solution.py:107
  163.8 4.1 multiply_reduce_fusion.6
  167.9 10.0 %fusion.42 = f32[512,4096]{1,0:T(8,128)} fusion(bf16[768,4096]{1,0:T(8,128)(2,1)} %all-gather.3.cloned.1.call-done, f32[512,768]{1,0:T(8,128)} %get-tuple-element.97, f32[768]{0:T(1024)S(1)} %mul.274, f32[512]{0:T(512)S(1)} %add_rsqrt_fusion.2), kind=kOutput, calls=%fused_computation.138 | convolution fusion | flops 3222405120 | bytes 16258048 | tf_op jit(solution)/shard_map/dot_general | solution.py:23
  177.9 9.8 %fusion.6 = (bf16[512,2048]{1,0:T(8,128)(2,1)}, bf16[512,2048]{1,0:T(8,128)(2,1)}, bf16[512,2048]{1,0:T(8,128)(2,1)S(1)}) fusion(f32[512,4096]{1,0:T(8,128)} %fusion.42, bf16[2048,768]{1,0:T(8,128)(2,1)} %all-gather.5.cloned.1.call-done, bf16[1,512,768]{2,1,0:T(8,128)(2,1)} %param.20, f32[512]{0:T(512)S(1)} %fusion.38), kind=kOutput, calls=%fused_computation.14 | convolution fusion | flops 1639055360 | bytes 18614272 | tf_op jit(solution)/shard_map/dot_general | solution.py:19
  189.1 3.6 convolution_convert_fusion.1
  195.4 8.2 %multiply_reduce_fusion.2 = (f32[768]{0:T(1024)S(1)}, f32[512]{0:T(512)S(1)}, f32[512,768]{1,0:T(8,128)S(1)}) fusion(f32[512,768]{1,0:T(8,128)} %get-tuple-element.97, f32[512]{0:T(512)S(1)} %add_rsqrt_fusion.2, f32[768]{0:T(1024)S(1)} %mul.274, bf16[768,4096]{1,0:T(8,128)(2,1)} %all-gather.3.cloned.1.call-done, bf16[512,2048]{1,0:T(8,128)(2,1)} %get-tuple-element.69, ...), kind=kOutput, calls=%fused_computation.38 | convolution fusion | flops 3231972096 | bytes 13641728 | tf_op jit(solution)/shard_map/dot_general | solution.py:19
  206.6 14.4 %cross_backward.1 = (bf16[512,768]{1,0:T(8,128)(2,1)}, bf16[512,768]{1,0:T(8,128)(2,1)}, bf16[512,768]{1,0:T(8,128)(2,1)}) custom-call(bf16[512,768]{1,0:T(8,128)(2,1)} %convolution_convert_fusion.13.refs_0_, bf16[512,768]{1,0:T(8,128)(2,1)} %convolution_convert_fusion.12.refs_1_, bf16[512,768]{1,0:T(8,128)(2,1)} %convolution_convert_fusion.11.refs_2_, ...), custom_call_target="tpu_custom_call" | custom-call | flops 4026531840 | bytes 6291456 | tf_op jit(solution)/shard_map/cross_backward/pallas_call | solution.py:254
  221.1 4.3 multiply_reduce_fusion.3
  225.3 7.8 %convolution_convert_fusion = bf16[768,4096]{1,0:T(8,128)(2,1)} fusion(bf16[512,2048]{1,0:T(8,128)(2,1)} %get-tuple-element.69, bf16[512,2048]{1,0:T(8,128)(2,1)S(1)} %copy-done.21, f32[512,768]{1,0:T(8,128)S(1)} %copy-done.11, f32[768]{0:T(1024)S(1)} %mul.274, f32[512]{0:T(512)S(1)} %add_rsqrt_fusion.2), kind=kOutput, calls=%fused_computation | convolution fusion | flops 3233939456 | bytes 12063744 | tf_op jit(solution)/shard_map/dot_general | solution.py:620
  233.2 2.9 multiply_add_fusion
  239.0 2.3 copy.98
  241.3 4.6 %all-to-all-start.1 = ((bf16[512,4,192]{0,2,1:T(8,128)(2,1)}), bf16[512,4,192]{0,2,1:T(8,128)(2,1)}, u32[]{:S(2)}, u32[]{:S(2)}) async-start(bf16[512,4,192]{0,2,1:T(8,128)(2,1)} %bitcast.149), calls=%async_computation.1 | async-start | bytes 1572864 | tf_op jit(solution)/shard_map/all_to_all | solution.py:739
  245.9 3.5 convolution_convert_fusion.5
  251.2 3.1 convolution_convert_fusion.8
  262.2 5.7 %fusion.18 = bf16[1,512,768]{2,1,0:T(8,128)(2,1)} fusion(f32[512,768]{1,0:T(8,128)} %get-tuple-element.97, bf16[512,2048]{1,0:T(8,128)(2,1)} %copy-done.58, bf16[2048,768]{1,0:T(8,128)(2,1)} %all-gather.5.cloned.1.call-done), kind=kOutput, calls=%fused_computation.61 | convolution fusion | flops 1611399168 | bytes 7602176 | tf_op jit(solution)/shard_map/dot_general | solution.py:23
  267.9 2.3 copy.99
  270.2 2.4 pad.29.refs_4_
  272.5 26.4 %self_backward.1 = (bf16[2048,256]{1,0:T(8,128)(2,1)}, bf16[2048,256]{1,0:T(8,128)(2,1)}, bf16[2048,256]{1,0:T(8,128)(2,1)}, f32[3,128,256]{2,1,0:T(8,128)}) custom-call(s32[1]{0:T(128)} %copy.120.refs_0_, bf16[2048,768]{1,0:T(8,128)(2,1)} %convolution_convert_fusion.2.refs_1_.refs_2_.refs_3_, ...), custom_call_target="tpu_custom_call" | custom-call | flops 8053063680 | bytes 8388608 | tf_op jit(solution)/shard_map/self_backward/pallas_call | solution.py:254
  301.9 5.7 %multiply_reduce_fusion = (f32[768]{0:T(1024)}, bf16[2048,768]{1,0:T(8,128)(2,1)}, bf16[2048,768]{1,0:T(8,128)(2,1)}) fusion(bf16[2,2,512,768]{3,2,1,0:T(8,128)(2,1)S(1)} %get-tuple-element.38, f32[2048]{0:T(1024)S(1)} %bitcast.173, f32[768]{0:T(1024)S(1)} %copy-done.45, bf16[2048,768]{1,0:T(8,128)(2,1)S(1)} %constant_dynamic-update-slice_fusion, ...), kind=kOutput, calls=%fused_computation.2 | convolution fusion | flops 2426928384 | bytes 13776896 | tf_op jit(solution)/shard_map/dot_general | solution.py:19
  311.6 6.6 %convolution_convert_fusion.3 = bf16[768,768]{1,0:T(8,128)(2,1)} fusion(bf16[2048,768]{1,0:T(8,128)(2,1)} %get-tuple-element.78, bf16[2048,768]{1,0:T(8,128)(2,1)} %copy-done.34), kind=kOutput, calls=%fused_computation.49 | convolution fusion | flops 2416508928 | bytes 7471104 | tf_op jit(solution)/shard_map/dot_general | solution.py:620
  318.2 104.5 %reduce.9 = (f32[5,24,768]{2,1,0:T(8,128)}, bf16[2,2,24,768]{3,2,1,0:T(8,128)(2,1)}, f32[8,64,768]{2,1,0:T(8,128)}, f32[2,64,768]{2,1,0:T(8,128)}, f32[8,128]{1,0:T(8,128)}, /*index=5*/f32[8,128]{1,0:T(8,128)}) custom-call(bf16[2,2,4,2,24,768]{5,4,3,2,1,0:T(8,128)(2,1)} %bitcast.145, bf16[2,2,4,2,24,768]{5,4,3,2,1,0:T(8,128)(2,1)} %bitcast.162, ...), custom_call_target="tpu_custom_call" | custom-call | tf_op jit(solution)/shard_map/reduce/pallas_call | solution.py:586
  431.0 3.0 fusion.13
  435.6 8.5 %reduce-scatter.3.cloned.1.call-done = bf16[24,4096]{1,0:T(8,128)(2,1)} async-done(((bf16[768,4096]{1,0:T(8,128)(2,1)}), bf16[24,4096]{1,0:T(8,128)(2,1)}) %reduce-scatter.3.cloned.1.call-update) | async-done | bytes 196624 | tf_op jit(solution)/shard_map/reduce_scatter | solution.py:720
  (236 shorter events, 60.4 us)
Async XLA Ops:
  7.2 4.5 copy-start.36
  7.2 4.5 copy-start.37
  7.2 4.7 %copy-start.38 = (f32[24,768]{1,0:T(8,128)S(1)}, f32[24,768]{1,0:T(8,128)}, u32[]{:S(2)}) copy-start(f32[24,768]{1,0:T(8,128)} %param.24) | copy-start | bytes 221188
  7.2 5.0 %copy-start.39 = (f32[24,768]{1,0:T(8,128)S(1)}, f32[24,768]{1,0:T(8,128)}, u32[]{:S(2)}) copy-start(f32[24,768]{1,0:T(8,128)} %param.25) | copy-start | bytes 221188
  7.2 160.7 %all-gather.3.cloned.1.call-start = ((), (), s32[]{:S(2)}) async-start(), calls=%async_computation.4 | async-start | bytes 6488064 | tf_op jit(solution)/shard_map/all_gather | solution.py:664
  8.3 4.8 %copy-start.52 = (f32[3,24]{1,0:T(4,128)S(1)}, f32[3,24]{1,0:T(4,128)}, u32[]{:S(2)}) copy-start(f32[3,24]{1,0:T(4,128)} %param.22) | copy-start | bytes 868
  8.3 4.9 %copy-start.40 = (f32[24,768]{1,0:T(8,128)S(1)}, f32[24,768]{1,0:T(8,128)}, u32[]{:S(2)}) copy-start(f32[24,768]{1,0:T(8,128)} %param.27) | copy-start | bytes 221188
  10.0 167.9 %all-gather.5.cloned.1.call-start = ((), (), s32[]{:S(2)}) async-start(), calls=%async_computation.5 | async-start | bytes 3244032 | tf_op jit(solution)/shard_map/all_gather | solution.py:665
  12.2 81.4 %copy-start.53 = (s32[15]{0:T(128)S(1)}, s32[15]{0:T(128)}, u32[]{:S(2)}) copy-start(s32[15]{0:T(128)} %constant.52.clone) | copy-start | bytes 184
  12.2 81.5 %copy-start.50 = (f32[32,3]{0,1:T(4,128)S(1)}, f32[32,3]{0,1:T(4,128)}, u32[]{:S(2)}) copy-start(f32[32,3]{0,1:T(4,128)} %param.34) | copy-start | bytes 1156
  124.0 18.7 %all-to-all-start = ((bf16[4,512,192]{1,2,0:T(8,128)(2,1)}), bf16[4,512,192]{1,2,0:T(8,128)(2,1)}, u32[]{:S(2)}, u32[]{:S(2)}) async-start(bf16[4,512,192]{1,2,0:T(8,128)(2,1)} %copy.95), calls=%async_computation | async-start | bytes 1572864 | tf_op jit(solution)/shard_map/all_to_all | solution.py:696
  128.2 305.8 %reduce-scatter.5.cloned.1.call-start = ((), (), s32[]{:S(2)}) async-start(), calls=%async_computation.7 | async-start | bytes 3244032 | tf_op jit(solution)/shard_map/reduce_scatter | solution.py:714
  129.9 63.7 %copy-start.47 = (f32[512]{0:T(512)}, f32[512]{0:T(512)S(1)}, u32[]{:S(2)}) copy-start(f32[512]{0:T(512)S(1)} %add_rsqrt_fusion.1) | copy-start | bytes 6148
  142.7 3.9 copy-start.26
  177.9 11.2 %copy-start.29 = (bf16[1,512,768]{2,1,0:T(8,128)(2,1)S(1)}, bf16[1,512,768]{2,1,0:T(8,128)(2,1)}, u32[]{:S(2)}) copy-start(bf16[1,512,768]{2,1,0:T(8,128)(2,1)} %param.20) | copy-start | bytes 2359300
  192.7 251.3 %reduce-scatter.3.cloned.1.call-start = ((), (), s32[]{:S(2)}) async-start(), calls=%async_computation.6 | async-start | bytes 6488064 | tf_op jit(solution)/shard_map/reduce_scatter | solution.py:720
  195.4 8.2 %copy-start.10 = (f32[512,768]{1,0:T(8,128)S(1)}, f32[512,768]{1,0:T(8,128)}, u32[]{:S(2)}) copy-start(f32[512,768]{1,0:T(8,128)} %get-tuple-element.97) | copy-start | bytes 4718596
  195.4 8.3 %copy-start.30 = (bf16[1,512,768]{2,1,0:T(8,128)(2,1)S(1)}, bf16[1,512,768]{2,1,0:T(8,128)(2,1)}, u32[]{:S(2)}) copy-start(bf16[1,512,768]{2,1,0:T(8,128)(2,1)} %param.20) | copy-start | bytes 2359300
  221.1 4.3 copy-start.11
  221.1 4.3 copy-start.21
  233.2 4.1 copy-start.25
  241.3 26.6 %all-to-all-start.1 = ((bf16[512,4,192]{0,2,1:T(8,128)(2,1)}), bf16[512,4,192]{0,2,1:T(8,128)(2,1)}, u32[]{:S(2)}, u32[]{:S(2)}) async-start(bf16[512,4,192]{0,2,1:T(8,128)(2,1)} %bitcast.149), calls=%async_computation.1 | async-start | bytes 1572864 | tf_op jit(solution)/shard_map/all_to_all | solution.py:739
  301.6 6.1 %copy-start.34 = (bf16[2048,768]{1,0:T(8,128)(2,1)}, bf16[2048,768]{1,0:T(8,128)(2,1)S(1)}, u32[]{:S(2)}) copy-start(bf16[2048,768]{1,0:T(8,128)(2,1)S(1)} %constant_dynamic-update-slice_fusion) | copy-start | bytes 9437188
  301.9 7.4 %copy-start.31 = (f32[3,128,256]{2,1,0:T(8,128)S(1)}, f32[3,128,256]{2,1,0:T(8,128)}, u32[]{:S(2)}) copy-start(f32[3,128,256]{2,1,0:T(8,128)} %get-tuple-element.53) | copy-start | bytes 1179652
  318.1 104.5 %copy-start.54 = (s32[128]{0:T(128)S(1)}, s32[128]{0:T(128)}, u32[]{:S(2)}) copy-start(s32[128]{0:T(128)} %compare_select_fusion.2) | copy-start | bytes 1540
  318.1 105.7 %copy-start.1 = (bf16[1,512,768]{2,1,0:T(8,128)(2,1)S(1)}, bf16[1,512,768]{2,1,0:T(8,128)(2,1)}, u32[]{:S(2)}) copy-start(bf16[1,512,768]{2,1,0:T(8,128)(2,1)} %param.18) | copy-start | bytes 2359300
  318.1 105.7 %copy-start.46 = (f32[768]{0:T(1024)S(1)}, f32[768]{0:T(1024)}, u32[]{:S(2)}) copy-start(f32[768]{0:T(1024)} %copy-done.44) | copy-start | bytes 9220
  318.1 105.7 %copy-start.49 = (f32[8,64]{1,0:T(8,128)S(1)}, f32[8,64]{1,0:T(8,128)}, u32[]{:S(2)}) copy-start(f32[8,64]{1,0:T(8,128)} %rsqrt.48) | copy-start | bytes 6148
  425.7 4.6 %copy-start.33 = (f32[5,24,768]{2,1,0:T(8,128)S(1)}, f32[5,24,768]{2,1,0:T(8,128)}, u32[]{:S(2)}) copy-start(f32[5,24,768]{2,1,0:T(8,128)} %get-tuple-element.58) | copy-start | bytes 1105924
  425.7 5.3 %copy-start.14 = (f32[512,768]{1,0:T(8,128)S(1)}, f32[512,768]{1,0:T(8,128)}, u32[]{:S(2)}) copy-start(f32[512,768]{1,0:T(8,128)} %copy-done.12) | copy-start | bytes 4718596
  425.7 5.3 %copy-start.48 = (f32[512]{0:T(512)S(1)}, f32[512]{0:T(512)}, u32[]{:S(2)}) copy-start(f32[512]{0:T(512)} %copy-done.47) | copy-start | bytes 6148
  431.0 14.8 %copy-start.32 = (f32[2,64,768]{2,1,0:T(8,128)S(1)}, f32[2,64,768]{2,1,0:T(8,128)}, u32[]{:S(2)}) copy-start(f32[2,64,768]{2,1,0:T(8,128)} %get-tuple-element.55) | copy-start | bytes 1179652
  (33 other events, 68.6 us)
Sparse Core Ops, SparseCore 0:
  11.5 91.7 all-gather.2
  106.8 61.4 all-gather.4
  192.9 116.7 reduce-scatter.4
  315.1 128.9 reduce-scatter.2

commit v3 on v1

v3 whole, which is shorter than its diff:
```python
import functools

import jax
import jax.numpy as jnp
import numpy as np
from jax import lax
from jax.experimental import pallas as pl
from jax.experimental.pallas import tpu as pltpu
from jax.sharding import PartitionSpec as P

LANES = 128
BLOCK = 512
HEAD = 64
negative = -1e30
epsilon = 1e-06
highest = lax.Precision.HIGHEST
bounds = np.ceil(16.0 * 8.0 ** (np.arange(1, 16) / 16.0)).astype(np.int32)
low = jnp.bfloat16
MESH = pl.DeviceIdType.MESH


def nt(left, right):
    return lax.dot_general(left, right, (((1,), (1,)), ((), ())), preferred_element_type=jnp.float32)


def nn(left, right):
    return jnp.dot(left, right, preferred_element_type=jnp.float32)


def tn(left, right):
    return lax.dot_general(left, right, (((0,), (0,)), ((), ())), preferred_element_type=jnp.float32)


def buckets(distance):
    far = 16 + jnp.sum((distance[..., None] >= jnp.asarray(bounds)).astype(jnp.int32), axis=-1)
    return jnp.where(distance < 16, distance, far)


def bias_rows(table):
    count = table.shape[0]
    place = jnp.arange(3 * LANES, dtype=jnp.int32)
    onehot = buckets(jnp.clip(place, 0, 2 * LANES))[None, :] == jnp.arange(count, dtype=jnp.int32)[:, None]
    relative = table - table[count - 1 :]
    values = jnp.sum(jnp.where(onehot[:, None, :], relative[:, :, None], 0.0), axis=0)
    return jnp.where((place >= 2 * LANES)[None], negative, values)[:, None, :]


def head_place(heads):
    head = pl.program_id(0)
    per_tile = LANES // HEAD
    side = lax.rem(head, per_tile)
    lane = lax.broadcasted_iota(jnp.int32, (1, LANES), 1)
    return head, side == 0, (side == per_tile - 1) | (head == heads - 1), (lane // HEAD) == side


def bias_tiles(base_ref, t_scr):
    wide = jnp.broadcast_to(base_ref[0], (LANES, 3 * LANES))
    t_scr[...] = pltpu.roll(wide, 0, 1, stride=1, stride_axis=0)[:, : 2 * LANES]


def add_near(scores, t_scr):
    near = min(2 * LANES, scores.shape[1])
    fixed = scores[:, :near] + t_scr[:, :near]
    return fixed if near == scores.shape[1] else jnp.concatenate([fixed, scores[:, near:]], axis=1)


def add_corner(scores, t_scr):
    top, bottom = scores[:-LANES], scores[-LANES:]
    bottom = jnp.concatenate([bottom[:, :LANES] + t_scr[:, LANES:], bottom[:, LANES:]], axis=1)
    return jnp.concatenate([top, bottom], axis=0)


def at_step(head, stages, point, points):
    for due, stage in stages:
        if due >= 0 and due % points == point:
            pl.when(head == due // points)(stage)


def at_end(head, heads, stages):
    for due, stage in stages:
        if due < 0:
            pl.when(head == heads - 1)(stage)


FORWARD_POINTS = 4
BACKWARD_POINTS = 10


def attend_forward_kernel(*refs, causal, heads, plan):
    refs = list(refs)
    take = lambda n: [refs.pop(0) for _ in range(n)]
    if causal:
        (length_ref,) = take(1)
    q_ref, k_ref, v_ref = take(3)
    if causal:
        (base_ref,) = take(1)
    given = take(plan.inputs) if plan else []
    o_ref, lse_ref = take(2)
    made = take(plan.outputs) if plan else []
    s_scr, vt_scr, acc_scr, ot_scr = take(4)
    if causal:
        t_scr, mask_scr = take(2)
    stages = plan.stages(given, made, refs) if plan else []
    head, first, last, mask = head_place(heads)
    rows, keys = q_ref.shape[0], k_ref.shape[0]
    block = min(BLOCK, rows)
    if causal:
        bias_tiles(base_ref, t_scr)

        @pl.when(head == 0)
        def _():
            place = lax.broadcasted_iota(jnp.int32, (keys, LANES), 0)
            mask_scr[...] = jnp.where(place < length_ref[0], 0.0, negative)

    for at in range(0, keys, BLOCK):
        vt_scr[:, at : at + BLOCK] = jnp.where(mask, v_ref[at : at + BLOCK, :], 0).T

    def limit(scores, start):
        if start < BLOCK:
            return scores
        part = mask_scr[start : start + scores.shape[0], :]
        return scores + jnp.concatenate([part] * (scores.shape[1] // LANES), axis=1)

    for number in range(rows // block):
        at_step(head, stages, number, FORWARD_POINTS)
        start = number * block
        queries = jnp.where(mask, q_ref[start : start + block, :], 0)
        pieces = [(at, BLOCK, 0) for at in range(0, start if causal else keys, BLOCK)]
        if causal:
            pieces += [(start + part, LANES, part) for part in range(0, block, LANES)]
        largest = jnp.full((1, block), negative, jnp.float32)
        for at, size, skip in pieces:
            scores = nt(k_ref[at : at + size, :], queries[skip:])
            if causal:
                if size == LANES:
                    scores = add_near(scores, t_scr)
                elif at + size == start:
                    scores = add_corner(scores, t_scr)
                scores = limit(scores, at)
            s_scr[at : at + size, skip:] = scores
            top = jnp.maximum(largest[:, skip:], jnp.max(scores, axis=0, keepdims=True))
            largest = top if skip == 0 else jnp.concatenate([largest[:, :skip], top], axis=1)
        totals = jnp.zeros((1, block), jnp.float32)
        acc_scr[...] = jnp.zeros_like(acc_scr)
        for at, size, skip in pieces:
            expos = jnp.exp(s_scr[at : at + size, skip:] - largest[:, skip:])
            more = totals[:, skip:] + jnp.sum(expos, axis=0, keepdims=True)
            totals = more if skip == 0 else jnp.concatenate([totals[:, :skip], more], axis=1)
            acc_scr[:, skip:] += nn(vt_scr[:, at : at + size], expos.astype(low))
        lse_ref[0, :, start : start + block] = jnp.broadcast_to(largest + jnp.log(totals), (8, block))
        mixed = acc_scr[...] / totals
        ot_scr[:, start : start + block] = mixed + jnp.where(first, 0.0, ot_scr[:, start : start + block])

    @pl.when(last)
    def _():
        for at in range(0, rows, block):
            o_ref[at : at + block, :] = ot_scr[:, at : at + block].T.astype(low)

    at_end(head, heads, stages)


def attend_specs(queries, keys, padded):
    rows = queries.shape[0]
    width = padded or queries.shape[1]
    count = keys.shape[0]
    per_tile = LANES // HEAD
    skip = padded // LANES
    row_spec = pl.BlockSpec((rows, LANES), lambda h: (0, h // per_tile))
    key_spec = pl.BlockSpec((count, LANES), lambda h: (0, h // per_tile))
    key_specs = [pl.BlockSpec((count, LANES), lambda h, n=n: (0, n * skip + h // per_tile)) for n in (1, 2)]
    return rows, width, count, row_spec, key_spec, key_specs


def attend_forward(queries, keys, values, heads, padded=0, bias=None, length=None, plan=None, extra=()):
    causal = bias is not None
    rows, width, count, row_spec, _, key_specs = attend_specs(queries, keys, padded)
    block = min(BLOCK, rows)
    in_specs = [row_spec, *key_specs]
    args = [queries, keys, values]
    scratch = [
        pltpu.VMEM((count, block), jnp.float32), pltpu.VMEM((LANES, count), low),
        pltpu.VMEM((LANES, block), jnp.float32), pltpu.VMEM((LANES, rows), jnp.float32),
    ]
    if causal:
        in_specs = [pl.BlockSpec(memory_space=pltpu.SMEM), *in_specs, pl.BlockSpec((1, 1, 3 * LANES), lambda h: (h, 0, 0))]
        args = [length, *args, bias]
        scratch += [pltpu.VMEM((LANES, 2 * LANES), jnp.float32), pltpu.VMEM((count, LANES), jnp.float32)]
    return pl.pallas_call(
        functools.partial(attend_forward_kernel, causal=causal, heads=heads, plan=plan),
        grid=(heads,),
        in_specs=in_specs + (plan.in_specs() if plan else []),
        out_specs=[row_spec, pl.BlockSpec((1, 8, rows), lambda h: (h, 0, 0))] + (plan.out_specs() if plan else []),
        out_shape=[
            jax.ShapeDtypeStruct((rows, width), low),
            jax.ShapeDtypeStruct((heads, 8, rows), jnp.float32),
        ] + (plan.out_shape() if plan else []),
        scratch_shapes=scratch + (plan.scratch() if plan else []),
        compiler_params=plan.params() if plan else pltpu.CompilerParams(vmem_limit_bytes=60 * 2**20),
        cost_estimate=pl.CostEstimate(
            flops=4 * heads * LANES * rows * count // (2 if causal else 1),
            bytes_accessed=4 * (rows + count) * width,
            transcendentals=heads * rows * count // (2 if causal else 1),
        ),
        name="self_forward" if causal else "cross_forward",
    )(*args, *extra)


def attend_backward_kernel(*refs, causal, heads, plan):
    refs = list(refs)
    take = lambda n: [refs.pop(0) for _ in range(n)]
    if causal:
        (length_ref,) = take(1)
    q_ref, k_ref, v_ref, do_ref, o_ref, lse_ref = take(6)
    if causal:
        (base_ref,) = take(1)
    given = take(plan.inputs) if plan else []
    dq_ref, dk_ref, dv_ref = take(3)
    if causal:
        (distance_ref,) = take(1)
    made = take(plan.outputs) if plan else []
    kt_scr, dqt_scr, dk_scr, dv_scr, row_scr = take(5)
    if causal:
        t_scr, near_scr = take(2)
    stages = plan.stages(given, made, refs) if plan else []
    head, first, last, mask = head_place(heads)
    rows, keys = q_ref.shape[0], k_ref.shape[0]
    block = min(BLOCK, rows)
    key_block = min(BLOCK, keys)

    @pl.when(first)
    def _():
        dqt_scr[...] = jnp.zeros_like(dqt_scr)
        dk_scr[...] = jnp.zeros_like(dk_scr)
        dv_scr[...] = jnp.zeros_like(dv_scr)

    if causal:
        bias_tiles(base_ref, t_scr)
        near_scr[...] = jnp.zeros_like(near_scr)
    for at in range(0, keys, key_block):
        kt_scr[:, at : at + key_block] = jnp.where(mask, k_ref[at : at + key_block, :], 0).T
    for start in range(0, rows, block):
        at = slice(start, start + block)
        product = do_ref[at, :].astype(jnp.float32) * o_ref[at, :].astype(jnp.float32)
        delta = jnp.sum(jnp.where(mask, product, 0.0).T, axis=0, keepdims=True)
        logsum = lse_ref[0, 0:1, at]
        if causal:
            place = start + lax.broadcasted_iota(jnp.int32, (1, block), 1)
            logsum = jnp.where(place < length_ref[0], logsum, -negative)
        row_scr[0:1, at] = logsum
        row_scr[1:2, at] = delta

    def piece(key_at, row_at, fix=None):
        queries = jnp.where(mask, q_ref[row_at, :], 0)
        grads = jnp.where(mask, do_ref[row_at, :], 0)
        scores = nt(k_ref[key_at, :], queries)
        if fix is not None:
            scores = fix(scores, t_scr)
        weights = jnp.exp(scores - row_scr[0:1, row_at])
        grad_weights = nt(v_ref[key_at, :], grads)
        grad_scores = weights * (grad_weights - row_scr[1:2, row_at])
        low_scores = grad_scores.astype(low)
        dv_scr[key_at, :] += nn(weights.astype(low), grads)
        dk_scr[key_at, :] += nn(low_scores, queries)
        dqt_scr[:, row_at] += nn(kt_scr[:, key_at], low_scores)
        return grad_scores

    point = 0
    if not causal:
        for start in range(0, keys, key_block):
            for at in range(0, rows, block):
                piece(slice(start, start + key_block), slice(at, at + block))
    else:
        for start in range(0, keys, block):
            at_step(head, stages, point, BACKWARD_POINTS)
            point += 1
            for here in range(start, start + block, LANES):
                grad = piece(slice(here, here + LANES), slice(here, start + block), add_near)
                near = min(2 * LANES, grad.shape[1])
                near_scr[:, :near] += grad[:, :near]
            for at in range(start + block, rows, block):
                at_step(head, stages, point, BACKWARD_POINTS)
                point += 1
                beside = at == start + block
                grad = piece(slice(start, start + block), slice(at, at + block), add_corner if beside else None)
                if beside:
                    near_scr[:, LANES:] += grad[-LANES:, :LANES]
        flip = lax.broadcasted_iota(jnp.int32, (LANES, LANES), 0) + lax.broadcasted_iota(jnp.int32, (LANES, LANES), 1)
        flip = (flip == LANES - 1).astype(jnp.float32)
        turned = lax.dot_general(
            flip, near_scr[...], (((1,), (0,)), ((), ())), precision=highest, preferred_element_type=jnp.float32
        )
        turned = pltpu.roll(turned, 1, 1, stride=1, stride_axis=0)
        sums = jnp.sum(turned[:, LANES:], axis=0, keepdims=True)
        at_row = lax.broadcasted_iota(jnp.int32, (8, LANES), 0) == head
        before = jnp.where(head == 0, 0.0, distance_ref[...])
        distance_ref[...] = jnp.where(at_row, jnp.broadcast_to(sums, (8, LANES)), before)

    @pl.when(last)
    def _():
        for at in range(0, rows, block):
            dq_ref[at : at + block, :] = dqt_scr[:, at : at + block].T.astype(low)
        dk_ref[...] = dk_scr[...].astype(low)
        dv_ref[...] = dv_scr[...].astype(low)

    at_end(head, heads, stages)


def attend_backward(queries, keys, values, grad_mixed, mixed, logsum, heads, padded=0, bias=None, length=None, plan=None, extra=()):
    causal = bias is not None
    rows, width, count, row_spec, key_spec, key_specs = attend_specs(queries, keys, padded)
    in_specs = [row_spec, *key_specs, row_spec, row_spec, pl.BlockSpec((1, 8, rows), lambda h: (h, 0, 0))]
    args = [queries, keys, values, grad_mixed, mixed, logsum]
    out_specs = [row_spec, key_spec, key_spec]
    out_shape = [jax.ShapeDtypeStruct((n, width), low) for n in (rows, count, count)]
    scratch = [
        pltpu.VMEM((LANES, count), low), pltpu.VMEM((LANES, rows), jnp.float32),
        pltpu.VMEM((count, LANES), jnp.float32), pltpu.VMEM((count, LANES), jnp.float32), pltpu.VMEM((8, rows), jnp.float32),
    ]
    if causal:
        in_specs = [pl.BlockSpec(memory_space=pltpu.SMEM), *in_specs, pl.BlockSpec((1, 1, 3 * LANES), lambda h: (h, 0, 0))]
        args = [length, *args, bias]
        out_specs += [pl.BlockSpec((8, LANES), lambda h: (0, 0))]
        out_shape += [jax.ShapeDtypeStruct((8, LANES), jnp.float32)]
        scratch += [pltpu.VMEM((LANES, 2 * LANES), jnp.float32), pltpu.VMEM((LANES, 2 * LANES), jnp.float32)]
    return pl.pallas_call(
        functools.partial(attend_backward_kernel, causal=causal, heads=heads, plan=plan),
        grid=(heads,),
        in_specs=in_specs + (plan.in_specs() if plan else []),
        out_specs=out_specs + (plan.out_specs() if plan else []),
        out_shape=out_shape + (plan.out_shape() if plan else []),
        scratch_shapes=scratch + (plan.scratch() if plan else []),
        compiler_params=plan.params() if plan else pltpu.CompilerParams(vmem_limit_bytes=60 * 2**20),
        cost_estimate=pl.CostEstimate(
            flops=10 * heads * LANES * rows * count // (2 if causal else 1),
            bytes_accessed=8 * (rows + count) * width,
            transcendentals=heads * rows * count // (2 if causal else 1),
        ),
        name="self_backward" if causal else "cross_backward",
    )(*args, *extra)


def coordinates():
    place, slot = lax.axis_index("seq"), lax.axis_index("fsdp")
    return place // 2, lax.rem(place, 2), slot // 2, lax.rem(slot, 2)


def device(x, c, z, y):
    return (x * 2 + c, z * 2 + y)


class Near:
    def __init__(self, nz):
        self.nz = nz
        x, c, z, y = self.x, self.c, self.z, self.y = coordinates()
        self.by_x, self.by_core, self.by_y = device(1 - x, c, z, y), device(x, 1 - c, z, y), device(x, c, z, 1 - y)
        self.diagonal = device(1 - x, 1 - c, z, y)
        self.steps = [lax.rem(z + t, nz) for t in range(nz)]
        self.backs = [lax.rem(z - t + nz, nz) for t in range(nz)]
        self.by_z = [device(x, c, self.steps[t], y) for t in range(nz)]


def greet(others):
    barrier = pltpu.get_barrier_semaphore()
    for other in others:
        pl.semaphore_signal(barrier, inc=1, device_id=other, device_id_type=MESH)
    pl.semaphore_wait(barrier, len(others))


class Copies:
    def __init__(self, send_sem, recv_sem):
        self.send_sem, self.recv_sem, self.made = send_sem, recv_sem, []

    def add(self, source, target, other):
        self.made.append((source, target, other))
        return len(self.made) - 1

    def copy(self, number):
        source, target, other = self.made[number]
        return pltpu.make_async_remote_copy(
            src_ref=source(), dst_ref=target(), send_sem=self.send_sem.at[number], recv_sem=self.recv_sem.at[number],
            device_id=other, device_id_type=MESH,
        )

    def start(self, *numbers):
        for number in numbers:
            self.copy(number).start()

    def arrive(self, *numbers):
        for number in numbers:
            self.copy(number).wait_recv()

    def finish(self):
        for number in range(len(self.made)):
            self.copy(number).wait_send()


def add_low(target, left, right):
    @pl.loop(0, left.shape[0])
    def _(n):
        target[n] = (left[n].astype(jnp.float32) + right[n].astype(jnp.float32)).astype(target.dtype)


def whole(space=pltpu.VMEM):
    return pl.BlockSpec(memory_space=space)


class GatherPlan:
    inputs, outputs = 1, 1

    def __init__(self, nz, count, share, width):
        self.nz, self.count, self.share, self.width = nz, count, share, width
        self.total = 8 * nz - 1

    def in_specs(self):
        return [whole()]

    def out_specs(self):
        return [whole(pl.ANY)]

    def out_shape(self):
        return [jax.ShapeDtypeStruct((self.count, 2, 2, self.nz, 2, self.share, self.width), low)]

    def scratch(self):
        return [pltpu.SemaphoreType.DMA((self.total,)), pltpu.SemaphoreType.DMA((self.total,)), pltpu.SemaphoreType.DMA((1,))]

    def params(self):
        return pltpu.CompilerParams(collective_id=2, has_side_effects=True, vmem_limit_bytes=60 * 2**20)

    def stages(self, given, made, scratch):
        (src,), (out,), (send_sem, recv_sem, local_sem) = given, made, scratch
        nz, my = self.nz, Near(self.nz)
        x, c, z, y, backs = my.x, my.c, my.z, my.y, my.backs
        copies = Copies(send_sem, recv_sem)
        own = lambda: src
        at = lambda xx, cc, zz, yy: lambda: out.at[:, xx, cc, zz, yy]
        mine = at(x, c, z, y)
        by_z = [None] + [copies.add(own, mine, my.by_z[t]) for t in range(1, nz)]
        held = [mine if t == 0 else at(x, c, backs[t], y) for t in range(nz)]
        source = [own if t == 0 else held[t] for t in range(nz)]
        by_y = [copies.add(source[t], held[t], my.by_y) for t in range(nz)]
        by_x = [copies.add(source[t], held[t], my.by_x) for t in range(nz)]
        by_core = [copies.add(source[t], held[t], my.by_core) for t in range(nz)]
        from_x = [at(1 - x, c, backs[t], y) for t in range(nz)]
        from_y = [at(x, c, backs[t], 1 - y) for t in range(nz)]
        far = [at(1 - x, c, backs[t], 1 - y) for t in range(nz)]
        corner = [
            copies.add(from_x[t], from_x[t], my.by_y) if t % 2 == 0 else copies.add(from_y[t], from_y[t], my.by_x)
            for t in range(nz)
        ]
        core_x = [copies.add(from_x[t], from_x[t], my.by_core) for t in range(nz)]
        core_y = [copies.add(from_y[t], from_y[t], my.by_core) for t in range(nz)]
        core_far = [copies.add(far[t], far[t], my.by_core) for t in range(nz)]
        local = lambda: pltpu.make_async_copy(src, mine(), local_sem.at[0])

        def begin():
            greet([my.by_x, my.by_core, my.by_y, *my.by_z[1:]])
            copies.start(*by_z[1:], by_y[0], by_x[0], by_core[0])
            local().start()

        def line(t):
            copies.arrive(by_z[t])
            copies.start(by_y[t], by_x[t], by_core[t])

        def plane(t):
            copies.arrive(by_x[t])
            copies.start(*([corner[t]] if t % 2 == 0 else []), core_x[t])
            copies.arrive(by_y[t])
            copies.start(*([corner[t]] if t % 2 == 1 else []), core_y[t])

        def turn(t):
            copies.arrive(corner[t])
            copies.start(core_far[t])

        def end():
            local().wait()
            copies.arrive(*by_core, *core_x, *core_y, *core_far)
            copies.finish()

        work = [functools.partial(line, t) for t in range(1, nz)]
        work += [functools.partial(plane, t) for t in range(nz)] + [functools.partial(turn, t) for t in range(nz)]
        points = 3 * FORWARD_POINTS - 1
        stages = [(0, begin)]
        for number, stage in enumerate(work):
            stages.append((1 + number * points // (len(work) + 1), stage))
        return stages + [(-1, end)]


class ReducePlan:
    outputs = 2

    def __init__(self, nz, count, share, width, slabs):
        self.nz, self.count, self.share, self.width, self.slabs = nz, count, share, width, slabs
        self.inputs = count + 1
        self.total = count * (nz + 2) + 2

    def in_specs(self):
        return [whole()] * self.inputs

    def out_specs(self):
        return [whole(), whole()]

    def out_shape(self):
        return [
            jax.ShapeDtypeStruct((self.count, self.share, self.width), jnp.float32),
            jax.ShapeDtypeStruct(self.slabs, jnp.float32),
        ]

    def scratch(self):
        nz, tail = self.nz, (self.share, self.width)
        vmem = lambda *shape: pltpu.VMEM((self.count, *shape, *tail), low)
        slabs = [pltpu.VMEM((*lead, *self.slabs), low) for lead in ((2,), (2,), ())]
        sems = [pltpu.SemaphoreType.DMA((self.total,)), pltpu.SemaphoreType.DMA((self.total,))]
        return [vmem(2, 2, nz), vmem(2, nz, 2), vmem(2, nz), vmem(2, nz), vmem(nz), vmem(nz), vmem(nz - 1), *slabs, *sems]

    def params(self):
        return pltpu.CompilerParams(collective_id=3, has_side_effects=True, vmem_limit_bytes=60 * 2**20)

    def stages(self, given, made, scratch):
        squares, enc = given[:-1], given[-1]
        out, out_enc = made
        a, ra, b, rb, d, rd, re, enc_r, enc_a, enc_rx, send_sem, recv_sem = scratch
        nz, my, count = self.nz, Near(self.nz), self.count
        x, c, z, y = my.x, my.c, my.z, my.y
        copies = Copies(send_sem, recv_sem)
        enc_core = copies.add(lambda: enc.at[:, 1 - c], lambda: enc_r, my.by_core)
        core = [copies.add(lambda n=n: squares[n].at[:, 1 - c], lambda n=n: ra.at[n], my.by_core) for n in range(count)]
        enc_x = copies.add(lambda: enc_a.at[1 - x], lambda: enc_rx, my.by_x)
        one, two, three = [], [], []
        for n in range(count):
            y_first = n % 2 == 0
            if y_first:
                one.append(copies.add(lambda n=n: a.at[n, :, 1 - y], lambda n=n: rb.at[n], my.by_y))
                two.append(copies.add(lambda n=n: b.at[n, 1 - x], lambda n=n: rd.at[n], my.by_x))
            else:
                one.append(copies.add(lambda n=n: a.at[n, 1 - x], lambda n=n: rb.at[n], my.by_x))
                two.append(copies.add(lambda n=n: b.at[n, 1 - y], lambda n=n: rd.at[n], my.by_y))
            three.append([
                copies.add(lambda n=n, t=t: d.at[n, my.steps[t]], lambda n=n, t=t: re.at[n, t - 1], my.by_z[t])
                for t in range(1, nz)
            ])

        def begin():
            greet([my.by_x, my.by_core, my.by_y, *my.by_z[1:]])
            copies.start(*core, enc_core)

        def after_core(n):
            copies.arrive(core[n])
            for half in range(2):
                for side in range(2):
                    add_low(a.at[n, half, side], squares[n].at[half, c, :, side], ra.at[n, half, :, side])
            copies.start(one[n])

        def after_one(n):
            copies.arrive(one[n])
            for side in range(2):
                if n % 2 == 0:
                    add_low(b.at[n, side], a.at[n, side, y], rb.at[n, side])
                else:
                    add_low(b.at[n, side], a.at[n, x, side], rb.at[n, side])
            copies.start(two[n])

        def after_two(n):
            copies.arrive(two[n])
            add_low(d.at[n], b.at[n, x if n % 2 == 0 else y], rd.at[n])
            copies.start(*three[n])

        def after_three(n):
            copies.arrive(*three[n])
            total = d[n, z].astype(jnp.float32)
            for t in range(nz - 1):
                total += re[n, t].astype(jnp.float32)
            out[n] = total

        def encoder():
            copies.arrive(enc_core)
            for half in range(2):
                add_low(enc_a.at[half], enc.at[half, c], enc_r.at[half])
            copies.start(enc_x)

        def end():
            copies.arrive(enc_x)
            add_low(out_enc, enc_a.at[x], enc_rx)
            for n in range(count):
                after_three(n)
            copies.finish()

        part = functools.partial
        work = [part(after_core, n) for n in range(count)] + [encoder]
        work += [part(after_one, n) for n in range(count)] + [part(after_two, n) for n in range(count)]
        points = 3 * BACKWARD_POINTS - 2
        stages = [(0, begin)]
        for number, stage in enumerate(work):
            stages.append((2 + number * (points - 2) // len(work), stage))
        return stages + [(-1, end)]


def gather_kernel(nz, tok, enc, own, everyone, encoded, qkv_out, send_sem, recv_sem, local_sem):
    my = Near(nz)
    x, c, z, y, backs = my.x, my.c, my.z, my.y, my.backs
    greet([my.by_x, my.by_core, my.diagonal, my.by_y, *my.by_z[1:]])
    copies = Copies(send_sem, recv_sem)
    local = [
        pltpu.make_async_copy(source, target, local_sem.at[n])
        for n, (source, target) in enumerate(
            [(own.at[x, c], qkv_out.at[x, c, z, y]), (tok, everyone.at[x, c]), (enc, encoded.at[x, c])]
        )
    ]
    for copy in local:
        copy.start()
    mine = lambda: qkv_out.at[x, c, z, y]
    first = [
        copies.add(lambda: own.at[1 - x, c], mine, my.by_x),
        copies.add(lambda: own.at[x, 1 - c], mine, my.by_core),
        copies.add(lambda: own.at[1 - x, 1 - c], mine, my.diagonal),
    ]
    rows = [(tok, everyone), (enc, encoded)]
    rows_x = [copies.add(lambda s=s: s, lambda t=t: t.at[x, c], my.by_x) for s, t in rows]
    rows_core = [copies.add(lambda s=s: s, lambda t=t: t.at[x, c], my.by_core) for s, t in rows]
    rows_far = [copies.add(lambda t=t: t.at[1 - x, c], lambda t=t: t.at[1 - x, c], my.by_core) for s, t in rows]
    line = [lambda t=t: qkv_out.at[:, :, backs[t], y] for t in range(nz)]
    by_z = [None] + [copies.add(line[0], line[0], my.by_z[t]) for t in range(1, nz)]
    by_y = [copies.add(line[t], line[t], my.by_y) for t in range(nz)]
    copies.start(*first, *rows_x, *rows_core)
    for copy in local:
        copy.wait()
    copies.arrive(*first)
    copies.start(*by_z[1:], by_y[0])
    for t in range(1, nz):
        copies.arrive(by_z[t])
        copies.start(by_y[t])
    for n in range(2):
        copies.arrive(rows_x[n])
        copies.start(rows_far[n])
    copies.arrive(*by_y, *rows_core, *rows_far)
    copies.finish()


def gather(nz, tok, enc, own):
    share, wide = own.shape[-2:]
    shapes = [
        jax.ShapeDtypeStruct((2, 2, *tok.shape), tok.dtype),
        jax.ShapeDtypeStruct((2, 2, *enc.shape), enc.dtype),
        jax.ShapeDtypeStruct((2, 2, nz, 2, share, wide), own.dtype),
    ]
    total = 9 + 2 * nz - 1
    return pl.pallas_call(
        functools.partial(gather_kernel, nz),
        in_specs=[whole()] * 3,
        out_specs=[whole(pl.ANY)] * 3,
        out_shape=shapes,
        scratch_shapes=[
            pltpu.SemaphoreType.DMA((total,)), pltpu.SemaphoreType.DMA((total,)), pltpu.SemaphoreType.DMA((3,)),
        ],
        compiler_params=pltpu.CompilerParams(collective_id=0, has_side_effects=True, vmem_limit_bytes=8 * 2**20),
        name="gather",
    )(tok, enc, own)


def reduce_kernel(nz, group_width, square, own, tok, gain, near, out_square, out_q, out_k, out_v, out_tok, out_gain, out_near, *refs):
    (a, ra, b, rb, d, rd, re, own_r, own_a, own_rz, own_f, own_in, tok_r, tok_a, tok_rx, gain_r, near_r,
     send_sem, recv_sem, gain_send, gain_recv) = refs
    my = Near(nz)
    x, c, z, y = my.x, my.c, my.z, my.y
    world, slots = 8 * nz, 2 * nz
    place, slot = lax.axis_index("seq"), lax.axis_index("fsdp")
    me = place * slots + slot
    barrier = pltpu.get_barrier_semaphore()

    @pl.loop(1, world)
    def _(t):
        other = lax.rem(me + t, world)
        pl.semaphore_signal(barrier, inc=1, device_id=(other // slots, lax.rem(other, slots)), device_id_type=MESH)

    pl.semaphore_wait(barrier, world - 1)
    copies = Copies(send_sem, recv_sem)
    add = copies.add
    tok_core = [add(lambda h=h: tok.at[h, 1 - c], lambda h=h: tok_r.at[h], my.by_core) for h in (1 - x, x)]
    own_y = add(lambda: own.at[:, :, :, 1 - y], lambda: own_r, my.by_y)
    core = add(lambda: square.at[:, 1 - c], lambda: ra, my.by_core)
    near_all = [add(lambda: near, lambda t=t: near_r.at[t - 1], (place, lax.rem(slot + t, slots))) for t in range(1, slots)]
    tok_x = add(lambda: tok_a.at[1 - x], lambda: tok_rx, my.by_x)
    one = add(lambda: a.at[:, 1 - y], lambda: rb, my.by_y)
    two = add(lambda: b.at[1 - x], lambda: rd, my.by_x)
    three = [add(lambda t=t: d.at[my.steps[t]], lambda t=t: re.at[t - 1], my.by_z[t]) for t in range(1, nz)]
    own_z = [
        add(lambda t=t: own_a.at[:, :, my.steps[t]], lambda t=t: own_rz.at[t - 1], my.by_z[t]) for t in range(1, nz)
    ]
    landing = lambda: own_in.at[x, c]
    own_seq = [
        add(lambda: own_f.at[1 - x, c], landing, my.by_x),
        add(lambda: own_f.at[x, 1 - c], landing, my.by_core),
        add(lambda: own_f.at[1 - x, 1 - c], landing, my.diagonal),
    ]

    def gain_copy(t):
        other = lax.rem(me + t, world)
        return pltpu.make_async_remote_copy(
            src_ref=gain.at[other], dst_ref=gain_r.at[t - 1], send_sem=gain_send.at[t - 1], recv_sem=gain_recv.at[t - 1],
            device_id=(other // slots, lax.rem(other, slots)), device_id_type=MESH,
        )

    copies.start(own_y, tok_core[0], core, tok_core[1], *near_all)

    @pl.loop(1, world)
    def _(t):
        gain_copy(t).start()

    copies.arrive(tok_core[0])
    add_low(tok_a.at[1 - x], tok.at[1 - x, c], tok_r.at[1 - x])
    copies.start(tok_x)
    copies.arrive(core)
    for half in range(2):
        for side in range(2):
            add_low(a.at[half, side], square.at[half, c, :, side], ra.at[half, :, side])
    copies.start(one)
    copies.arrive(tok_core[1])
    add_low(tok_a.at[x], tok.at[x, c], tok_r.at[x])
    copies.arrive(own_y)
    for half in range(2):
        for side in range(2):
            add_low(own_a.at[half, side], own.at[half, side, :, y], own_r.at[half, side])
    copies.start(*own_z)
    copies.arrive(one)
    for side in range(2):
        add_low(b.at[side], a.at[side, y], rb.at[side])
    copies.start(two)
    copies.arrive(*own_z)
    for half in range(2):
        for side in range(2):
            total = own_a[half, side, z].astype(jnp.float32)
            for t in range(nz - 1):
                total += own_rz[t, half, side].astype(jnp.float32)
            own_f[half, side] = total.astype(low)
    copies.start(*own_seq)
    own_in[x, c] = own_f[x, c]
    copies.arrive(*near_all)
    total = near[...]
    for t in range(slots - 1):
        total += near_r[t]
    out_near[...] = total
    out_gain[...] = gain[me]

    @pl.loop(1, world)
    def _(t):
        gain_copy(t).wait_recv()
        out_gain[...] += gain_r[t - 1]

    copies.arrive(*own_seq)
    padded = own_in.shape[-1] // 3
    for n, out in enumerate((out_q, out_k, out_v)):
        parts = [own_in[s // 2, s % 2, :, n * padded : n * padded + group_width].astype(jnp.float32) for s in range(4)]
        out[...] = jnp.concatenate(parts, axis=1)
    copies.arrive(two)
    add_low(d, b.at[x], rd)
    copies.start(*three)
    copies.arrive(tok_x)
    add_low(out_tok, tok_a.at[x], tok_rx)
    copies.arrive(*three)
    total = d[z].astype(jnp.float32)
    for t in range(nz - 1):
        total += re[t].astype(jnp.float32)
    out_square[...] = total
    copies.finish()

    @pl.loop(1, world)
    def _(t):
        gain_copy(t).wait_send()


def reduce(nz, group_width, square, own, tok, gain, near):
    share, width = square.shape[-2:]
    wide = own.shape[-1]
    vmem = lambda *shape: pltpu.VMEM(shape, low)
    slabs = tok.shape[2:]
    world = 8 * nz
    total = 4 + 2 * nz - 1 + 3 + 2 * (nz - 1) + 3
    f32 = lambda *shape: jax.ShapeDtypeStruct(shape, jnp.float32)
    return pl.pallas_call(
        functools.partial(reduce_kernel, nz, group_width),
        in_specs=[whole()] * 5,
        out_specs=[whole()] * 7,
        out_shape=[f32(share, width)] * 4 + [f32(*slabs), f32(*gain.shape[1:]), f32(*near.shape)],
        scratch_shapes=[
            vmem(2, 2, nz, share, width), vmem(2, nz, 2, share, width), vmem(2, nz, share, width), vmem(2, nz, share, width),
            vmem(nz, share, width), vmem(nz, share, width), vmem(nz - 1, share, width),
            vmem(2, 2, nz, share, wide), vmem(2, 2, nz, share, wide), vmem(nz - 1, 2, 2, share, wide), vmem(2, 2, share, wide),
            vmem(2, 2, share, wide),
            vmem(2, *slabs), vmem(2, *slabs), vmem(*slabs),
            pltpu.VMEM((world - 1, *gain.shape[1:]), jnp.float32), pltpu.VMEM((2 * nz - 1, *near.shape), jnp.float32),
            pltpu.SemaphoreType.DMA((total,)), pltpu.SemaphoreType.DMA((total,)),
            pltpu.SemaphoreType.DMA((world - 1,)), pltpu.SemaphoreType.DMA((world - 1,)),
        ],
        compiler_params=pltpu.CompilerParams(collective_id=1, has_side_effects=True, vmem_limit_bytes=60 * 2**20),
        name="reduce",
    )(square, own, tok, gain, near)


def rms_norm(values, gain):
    scale = lax.rsqrt(jnp.mean(values * values, axis=-1, keepdims=True) + epsilon)
    return values * scale * gain


def rms_back(values, gain, grad_normed):
    scale = lax.rsqrt(jnp.mean(values * values, axis=-1, keepdims=True) + epsilon)
    unit = values * scale
    grad_unit = grad_normed * gain
    grad_gain = jnp.sum(grad_normed * unit, axis=0)
    grad_values = scale * (grad_unit - unit * jnp.mean(grad_unit * unit, axis=-1, keepdims=True))
    return (grad_values, grad_gain)


def activate(gate, upper):
    return jax.nn.gelu(gate, approximate=True) * upper


def per_device(
    tokens, encoder, cotangent, lengths, gains, self_query, self_key, self_value, self_output,
    cross_query, cross_key, cross_value, cross_output, ffn_gate, ffn_up, ffn_down, rel_bias,
):
    both = ("seq", "fsdp")
    seq, fsdp = lax.axis_size("seq"), lax.axis_size("fsdp")
    world = seq * fsdp
    nz = fsdp // 2
    share, width = self_query.shape
    hidden_share = ffn_down.shape[0]
    inner = ffn_gate.shape[1]
    rows = tokens.shape[1]
    group = rel_bias.shape[1]
    group_width = group * HEAD
    padded = -(-group_width // LANES) * LANES
    spare = padded - group_width
    heads = width // HEAD
    place = lax.axis_index("seq")
    aligned = share % 8 == 0

    gate_up = lax.all_gather(jnp.concatenate([ffn_gate.astype(low), ffn_up.astype(low)], axis=1), both, axis=0, tiled=True)
    w_down = lax.all_gather(ffn_down.astype(low), both, axis=0, tiled=True)
    squares = jnp.stack([w.astype(low) for w in (self_output, cross_query, cross_key, cross_value, cross_output)])
    gain_columns = jnp.pad(gains.astype(low).T, ((0, 0), (0, spare - 3)))
    pieces = []
    for s in range(seq):
        for n, w in enumerate((self_query, self_key, self_value)):
            pieces.append(w[:, s * group_width : (s + 1) * group_width].astype(low))
            pieces.append(gain_columns if n == 0 else jnp.zeros((share, spare), low))
    own = jnp.concatenate(pieces, axis=1).reshape(share, seq, 3 * padded).transpose(1, 0, 2)
    if aligned:
        everyone, encoded, w_qkv = gather(nz, tokens[0], encoder[0], own.reshape(2, 2, share, 3 * padded))
    else:
        everyone = lax.all_gather(tokens[0], "seq", axis=0)
        encoded = lax.all_gather(encoder[0], "seq", axis=0)
        w_qkv = lax.all_to_all(own, "seq", split_axis=0, concat_axis=0, tiled=True)
        w_qkv = lax.all_gather(w_qkv, "fsdp", axis=1)
    everyone = everyone.reshape(seq * rows, width)
    encoded = encoded.reshape(-1, width)
    w_qkv = w_qkv.reshape(width, 3 * padded)
    gain_rows = w_qkv[:, group_width : group_width + 3].astype(jnp.float32).T

    length = lengths[0]
    values_in = tokens[0].astype(jnp.float32)
    normed_all = rms_norm(everyone.astype(jnp.float32), gain_rows[0]).astype(low)
    qkv = nn(normed_all, w_qkv).astype(low)
    bias = bias_rows(rel_bias)
    plan = GatherPlan(nz, 5, share, width) if aligned else None
    own_mixed, own_logsum, *gathered = attend_forward(
        qkv, qkv, qkv, group, padded, bias, lengths, plan, (squares,) if aligned else ()
    )
    squares = gathered[0] if aligned else jnp.moveaxis(lax.all_gather(squares, both, axis=0), 1, 0)
    squares = squares.reshape(5, width, width)
    w_output, c_query, c_key, c_value, c_output = (squares[n] for n in range(5))
    mixed = lax.all_to_all(own_mixed[:, :group_width], "seq", split_axis=0, concat_axis=1, tiled=True)
    attended = values_in + nn(mixed, w_output)
    normed_two = rms_norm(attended, gain_rows[1]).astype(low)
    cross_queries = nn(normed_two, c_query).astype(low)
    cross_keys = nn(encoded, c_key).astype(low)
    cross_values = nn(encoded, c_value).astype(low)
    cross_mixed, cross_logsum = attend_forward(cross_queries, cross_keys, cross_values, heads)
    crossed = attended + nn(cross_mixed, c_output)
    normed_three = rms_norm(crossed, gain_rows[2]).astype(low)
    both_parts = nn(normed_three, gate_up)
    gate, upper = both_parts[:, :inner], both_parts[:, inner:]
    hidden = activate(gate, upper).astype(low)
    result = crossed + nn(hidden, w_down)

    positions = place * rows + jnp.arange(rows, dtype=jnp.int32)
    grad_out = cotangent[0].astype(jnp.float32) * (positions < length).astype(jnp.float32)[:, None]
    grad_ffn = grad_out.astype(low)
    grad_hidden = nt(grad_ffn, w_down)
    _, pullback = jax.vjp(activate, gate, upper)
    grad_gate, grad_upper = pullback(grad_hidden)
    grad_both = jnp.concatenate([grad_gate.astype(low), grad_upper.astype(low)], axis=1)
    slabs = -(-hidden_share // share)
    grad_down = tn(hidden, grad_ffn).astype(low).reshape(world, hidden_share, width)
    grad_down = jnp.pad(grad_down, ((0, 0), (0, slabs * share - hidden_share), (0, 0)))
    grad_down = grad_down.reshape(world, slabs, share, width).transpose(0, 2, 1, 3).reshape(world * share, slabs * width)
    packed = jnp.concatenate([tn(normed_three, grad_both).astype(low), grad_down], axis=1)
    share_ffn = lax.psum_scatter(packed, both, scatter_dimension=0, tiled=True)

    grad_normed_three = nt(grad_both, gate_up)
    norm_part, grad_gain_two = rms_back(crossed, gain_rows[2], grad_normed_three)
    grad_crossed = grad_out + norm_part
    grad_branch = grad_crossed.astype(low)
    grad_coutput = tn(cross_mixed, grad_branch).astype(low)
    grad_cmixed = nt(grad_branch, c_output).astype(low)
    grad_cq, grad_ck, grad_cv = attend_backward(
        cross_queries, cross_keys, cross_values, grad_cmixed, cross_mixed, cross_logsum, heads
    )
    grad_cquery = tn(normed_two, grad_cq).astype(low)
    grad_ckey = tn(encoded, grad_ck).astype(low)
    grad_cvalue = tn(encoded, grad_cv).astype(low)
    grad_encoded = (nt(grad_ck, c_key) + nt(grad_cv, c_value)).astype(low)
    norm_part, grad_gain_one = rms_back(attended, gain_rows[1], nt(grad_cq, c_query))
    grad_attended = grad_crossed + norm_part
    grad_self_branch = grad_attended.astype(low)
    grad_output = tn(mixed, grad_self_branch).astype(low)
    grad_mixed = nt(grad_self_branch, w_output).astype(low)
    own_grad_mixed = lax.all_to_all(grad_mixed, "seq", split_axis=1, concat_axis=0, tiled=True)
    own_grad_mixed = jnp.pad(own_grad_mixed, ((0, 0), (0, padded - group_width)))
    slab = 64
    chunked = lambda g: g.reshape(2, 2, nz, 2, share, g.shape[-1])
    by_place = lambda g: g.reshape(2, 2, -1, slab, width)
    early = [grad_cquery, grad_ckey, grad_cvalue, grad_coutput]
    plan, extra = None, ()
    if aligned:
        extra = (*[chunked(g) for g in early], by_place(grad_encoded))
        plan = ReducePlan(nz, len(early), share, width, extra[-1].shape[2:])
    own_dq, own_dk, own_dv, by_distance, *sums = attend_backward(
        qkv, qkv, qkv, own_grad_mixed, own_mixed, own_logsum, group, padded, bias, lengths, plan, extra
    )
    own_qkv = jnp.concatenate([own_dq, own_dk, own_dv], axis=1)
    grad_normed_part = nt(own_qkv, w_qkv)
    values_all = everyone.astype(jnp.float32)
    units_all = values_all * lax.rsqrt(jnp.mean(values_all * values_all, axis=-1, keepdims=True) + epsilon)
    grad_gain_zero = jnp.sum(grad_normed_part * units_all, axis=0)
    grad_normed_part = grad_normed_part.astype(low)
    grad_own = tn(normed_all, own_qkv).astype(low)
    grad_gains = jnp.stack([grad_gain_zero, grad_gain_one, grad_gain_two])
    grad_gains = grad_gains.reshape(3, world, share).transpose(1, 0, 2).reshape(world, 1, 3 * share)
    grad_gains = jnp.pad(grad_gains, ((0, 0), (0, 7), (0, LANES - 3 * share)))
    wide = jnp.float32
    if aligned:
        share_output, *share_own, grad_normed, share_gains, by_distance = reduce(
            nz, group_width, chunked(grad_output), chunked(grad_own), by_place(grad_normed_part), grad_gains, by_distance
        )
        share_early, grad_encoded = sums
        share_squares = [share_output, *(share_early[n] for n in range(4))]
        grad_normed, grad_encoded = grad_normed.reshape(rows, width), grad_encoded.reshape(-1, width)
    else:
        scatter = lambda g, axes: lax.psum_scatter(g, axes, scatter_dimension=0, tiled=True)
        share_squares = scatter(jnp.concatenate([grad_output, *early], axis=1), both).astype(wide)
        share_squares = [share_squares[:, n * width : (n + 1) * width] for n in range(5)]
        grad_own = scatter(grad_own.reshape(seq, fsdp, share, 3 * padded).transpose(1, 0, 2, 3), "fsdp")[0]
        grad_own = lax.all_to_all(grad_own, "seq", split_axis=0, concat_axis=0, tiled=True).astype(wide)
        grad_own = grad_own.reshape(seq, share, 3, padded)[:, :, :, :group_width].transpose(2, 1, 0, 3).reshape(3, share, width)
        share_own = [grad_own[n] for n in range(3)]
        grad_normed = scatter(grad_normed_part, "seq").astype(wide)
        grad_encoded = scatter(grad_encoded, "seq").astype(wide)
        share_gains = scatter(grad_gains, both)[0]
        by_distance = lax.psum(by_distance, "fsdp")
    share_gains = share_gains[0, : 3 * share].reshape(3, share)
    norm_part, _ = rms_back(values_in, gain_rows[0], grad_normed)
    grad_input = grad_attended + norm_part
    bins = rel_bias.shape[0]
    near_map = (buckets(jnp.arange(LANES, dtype=jnp.int32))[:, None] == jnp.arange(bins - 1, dtype=jnp.int32)[None]).astype(wide)
    near_sums = jnp.dot(near_map.T, by_distance[:group].T, precision=highest)
    table_grad = jnp.concatenate([near_sums, -jnp.sum(near_sums, axis=0, keepdims=True)], axis=0)
    share_ffn = share_ffn.astype(wide)
    share_down = share_ffn[:, 2 * inner :].reshape(share, slabs, width).transpose(1, 0, 2).reshape(slabs * share, width)
    return (
        result.astype(low)[None], grad_input[None], grad_encoded[None], share_gains, *share_own, *share_squares,
        share_ffn[:, :inner], share_ffn[:, inner : 2 * inner], share_down[:hidden_share], table_grad,
    )


def solution(mesh):
    split = P(("seq", "fsdp"), None)
    rows = P("fsdp", "seq", None)
    gains = P(None, ("seq", "fsdp"))
    return jax.shard_map(
        per_device,
        mesh=mesh,
        in_specs=(rows, rows, rows, P("fsdp"), gains, *([split] * 11), P(None, "seq")),
        out_specs=(rows, rows, rows, gains, *([split] * 11), P(None, "seq")),
        check_vma=False,
    )
```

time: 854 us -> 428 us (0.50)
  waiting for transfers between devices: 503 us -> 5.56 us
  Pallas kernels: 77.8 us -> 235 us
  blocking collectives: 74.8 us -> 0 us
    reduce_scatter x5 -> x1, waiting for transfers between devices: 266 us -> 0.01 us  [per_device(): share_ffn = lax.psum_scatter(packed, both, scatter_dimension=0, tiled=True)]
    all_gather x2 -> x0, waiting for transfers between devices: 94 us -> none  [the longest x1 83.5 us: per_device(): packed = lax.all_gather(pack, both, axis=0)]
    pallas_call x0 -> x2, Pallas kernels: none -> 79.6 us  [the longest x1 46.2 us: reduce(): pl.pallas_call(functools.partial(reduce_kernel, nz, group_width), in_spec...]
    unnamed x11 -> x3, waiting for transfers between devices: 76 us -> 0.05 us
    pallas_call x2, Pallas kernels: 40.6 us -> 89.5 us  [attend_backward(): pl.pallas_call(functools.partial(attend_backward_kernel, causal=causal, h...]
    all_gather x1, waiting for transfers between devices: 45.9 us -> 2.11 us  [per_device(): w_down = lax.all_gather(ffn_down.astype(low), both, axis=0, tiled=True)]
    unnamed x1 -> x0, blocking collectives: 39.5 us -> none
    pallas_call x2, Pallas kernels: 37.3 us -> 65.7 us  [attend_forward(): pl.pallas_call(functools.partial(attend_forward_kernel, causal=causal, he...]
  transfers between devices with their start and end apart: 13 -> 5, of which waited for: 10 -> 2; matrix products, arithmetic and copies ran while one was open for 14% -> 27% of each run, Pallas kernels for 4% -> 56%
where the time goes in v3:
time: 428 us; the launch traced here: 420 us
  Pallas kernels  235 us (55%)
  matrix products  88.8 us (21%)
  local copies, waits for them, and re-layouts  38.8 us (9%)
  other arithmetic  26.9 us (6%)
  between operations  15.5 us (4%)
  starting transfers between devices  9.09 us (2%)
  waiting for transfers between devices  5.56 us (1%)
    pallas_call x2, Pallas kernels, attend_backward(): pl.pallas_call(functools.partial(attend_backward_kernel, causal=causal, h...  89.5 us
    pallas_call x2, Pallas kernels, attend_forward(): pl.pallas_call(functools.partial(attend_forward_kernel, causal=causal, he...  65.7 us
    pallas_call x1, Pallas kernels, reduce(): pl.pallas_call(functools.partial(reduce_kernel, nz, group_width), in_spec...  46.2 us
    pallas_call x1, Pallas kernels, gather(): pl.pallas_call(functools.partial(gather_kernel, nz), in_specs=[whole()] *...  33.4 us
    dot_general x8, matrix products, nn(): return jnp.dot(left, right, preferred_element_type=jnp.float32)  31.8 us
    dot_general x8, matrix products, nt(): lax.dot_general(left, right, (((1,), (1,)), ((), ())), preferred_element_...  31 us
    dot_general x8, matrix products, tn(): lax.dot_general(left, right, (((0,), (0,)), ((), ())), preferred_element_...  24.9 us
    unnamed x118, local copies, waits for them, and re-layouts  15.6 us
  transfers between devices with their start and end apart: 5, of which 2 were waited for; matrix products, arithmetic and copies ran while one was open for 27% of the time, Pallas kernels for 56%

profile of v3, /device:TPU:0, one launch (start us, length us, event | category | flops | bytes accessed | tf_op | source)
XLA Modules:
  0.0 419.6 jit_solution(2539999360633977921)
XLA Ops:
  13.4 33.4 %gather.1 = (bf16[2,2,512,768]{3,2,1,0:T(8,128)(2,1)S(1)}, bf16[2,2,128,768]{3,2,1,0:T(8,128)(2,1)S(1)}, bf16[2,2,4,2,24,768]{5,4,3,2,1,0:T(8,128)(2,1)S(1)}) custom-call(bf16[512,768]{1,0:T(8,128)(2,1)S(1)} %bitcast.136, bf16[128,768]{1,0:T(8,128)(2,1)S(1)} %bitcast.139, bf16[2,2,24,768]{3,2,1,0:T(8,128)(2,1)S(1)} %bitcast.138), custom_call_target="tpu_custom_call" | custom-call | tf_op jit(solution)/shard_map/gather/pallas_call | solution.py:646
  58.2 4.0 convolution_convert_fusion.2.refs_1_.refs_2_.refs_3_
  62.1 53.5 %self_forward.1 = (bf16[2048,256]{1,0:T(8,128)(2,1)}, f32[3,8,2048]{2,1,0:T(8,128)}, bf16[5,2,2,4,2,24,768]{6,5,4,3,2,1,0:T(8,128)(2,1)}) custom-call(s32[1]{0:T(128)} %copy.92.refs_0_, bf16[2048,768]{1,0:T(8,128)(2,1)} %convolution_convert_fusion.2.refs_1_.refs_2_.refs_3_, bf16[2048,768]{1,0:T(8,128)(2,1)} %convolution_convert_fusion.2.refs_1_.refs_2_.refs_3_, ...), custom_call_target="tpu_custom_call" | custom-call | flops 3221225472 | bytes 4194304 | tf_op jit(solution)/shard_map/self_forward/pallas_call | solution.py:188
  115.6 2.2 copy.66
  117.8 4.2 all-to-all-start
  122.2 4.7 %fusion.34 = (bf16[1,2,2,4,2,24,768]{6,5,4,3,2,1,0:T(8,128)(2,1)}, bf16[1,2,2,4,2,24,768]{6,5,4,3,2,1,0:T(8,128)(2,1)S(1)}, bf16[1,2,2,4,2,24,768]{6,5,4,3,2,1,0...) fusion(bf16[5,2,2,4,2,24,768]{6,5,4,3,2,1,0:T(8,128)(2,1)} %get-tuple-element.43), kind=kLoop, calls=%fused_computation.119 | loop fusion | bytes 11796480 | tf_op jit(solution)/shard_map/slice | solution.py:869
  130.3 3.4 all-to-all-done
  133.7 2.8 multiply_reduce_fusion.7
  139.3 12.3 %cross_forward.1 = (bf16[512,768]{1,0:T(8,128)(2,1)}, f32[12,8,512]{2,1,0:T(8,128)}) custom-call(bf16[512,768]{1,0:T(8,128)(2,1)} %convolution_convert_fusion.13.refs_0_, bf16[512,768]{1,0:T(8,128)(2,1)} %convolution_convert_fusion.12.refs_1_, bf16[512,768]{1,0:T(8,128)(2,1)} %convolution_convert_fusion.11.refs_2_), custom_call_target="tpu_custom_call" | custom-call | flops 1610612736 | bytes 3145728 | tf_op jit(solution)/shard_map/cross_forward/pallas_call | solution.py:188
  151.6 4.0 multiply_reduce_fusion.6
  155.6 10.0 %fusion.33 = f32[512,4096]{1,0:T(8,128)} fusion(bf16[768,4096]{1,0:T(8,128)(2,1)} %all-gather.3.cloned.1.call-done, f32[512,768]{1,0:T(8,128)} %get-tuple-element.105, f32[768]{0:T(1024)S(1)} %get-tuple-element.68, f32[512]{0:T(512)S(1)} %add_rsqrt_fusion.2), kind=kOutput, calls=%fused_computation.118 | convolution fusion | flops 3222405120 | bytes 16258048 | tf_op jit(solution)/shard_map/dot_general | solution.py:27
  165.7 2.1 all-gather.5.cloned.1.call-done
  167.8 8.4 %fusion.6 = (bf16[512,2048]{1,0:T(8,128)(2,1)S(1)}, bf16[512,2048]{1,0:T(8,128)(2,1)S(1)}, bf16[512,2048]{1,0:T(8,128)(2,1)S(1)}) fusion(f32[512,4096]{1,0:T(8,128)} %fusion.33, bf16[2048,768]{1,0:T(8,128)(2,1)} %all-gather.5.cloned.1.call-done, bf16[1,512,768]{2,1,0:T(8,128)(2,1)} %param.20, f32[512]{0:T(512)S(1)} %fusion.29), kind=kOutput, calls=%fused_computation.15 | convolution fusion | flops 1639055360 | bytes 18614272 | tf_op jit(solution)/shard_map/dot_general | solution.py:23
  176.3 1.9 convolution_convert_fusion.1
  178.5 2.3 copy.71
  182.3 4.3 %convolution_convert_fusion = bf16[768,4096]{1,0:T(8,128)(2,1)S(1)} fusion(bf16[512,2048]{1,0:T(8,128)(2,1)S(1)} %get-tuple-element.72, bf16[512,2048]{1,0:T(8,128)(2,1)S(1)} %get-tuple-element.71, f32[512,768]{1,0:T(8,128)S(1)} %copy-done.9, f32[768]{0:T(1024)S(1)} %get-tuple-element.68, f32[512]{0:T(512)S(1)} %add_rsqrt_fusion.2), kind=kOutput, calls=%fused_computation.1 | convolution fusion | flops 3233939456 | bytes 12063744 | tf_op jit(solution)/shard_map/dot_general | solution.py:31
  186.5 6.4 %pad_maximum_fusion = bf16[768,6400]{1,0:T(8,128)(2,1)} fusion(bf16[768,2304]{1,0:T(8,128)(2,1)S(1)} %bitcast.148, bf16[768,4096]{1,0:T(8,128)(2,1)S(1)} %convolution_convert_fusion), kind=kLoop, calls=%fused_computation | loop fusion | flops 19660800 | bytes 19660800 | tf_op jit(solution)/shard_map/concatenate | solution.py:895
  195.2 8.2 %multiply_reduce_fusion.2 = (f32[768]{0:T(1024)S(1)}, f32[512]{0:T(512)S(1)}, f32[512,768]{1,0:T(8,128)S(1)}) fusion(f32[512,768]{1,0:T(8,128)} %get-tuple-element.105, f32[512]{0:T(512)S(1)} %add_rsqrt_fusion.2, f32[768]{0:T(1024)S(1)} %get-tuple-element.68, bf16[768,4096]{1,0:T(8,128)(2,1)} %all-gather.3.cloned.1.call-done, ...), kind=kOutput, calls=%fused_computation.39 | convolution fusion | flops 3231972096 | bytes 13641728 | tf_op jit(solution)/shard_map/dot_general | solution.py:23
  206.5 14.5 %cross_backward.1 = (bf16[512,768]{1,0:T(8,128)(2,1)}, bf16[512,768]{1,0:T(8,128)(2,1)}, bf16[512,768]{1,0:T(8,128)(2,1)}) custom-call(bf16[512,768]{1,0:T(8,128)(2,1)} %convolution_convert_fusion.13.refs_0_, bf16[512,768]{1,0:T(8,128)(2,1)} %convolution_convert_fusion.12.refs_1_, bf16[512,768]{1,0:T(8,128)(2,1)} %convolution_convert_fusion.11.refs_2_, ...), custom_call_target="tpu_custom_call" | custom-call | flops 4026531840 | bytes 6291456 | tf_op jit(solution)/shard_map/cross_backward/pallas_call | solution.py:325
  221.0 3.3 multiply_reduce_fusion.3
  227.7 2.4 copy.67
  230.1 4.6 %all-to-all-start.1 = ((bf16[512,4,192]{0,2,1:T(8,128)(2,1)}), bf16[512,4,192]{0,2,1:T(8,128)(2,1)}, u32[]{:S(2)}, u32[]{:S(2)}) async-start(bf16[512,4,192]{0,2,1:T(8,128)(2,1)} %bitcast.156), calls=%async_computation.1 | async-start | bytes 1572864 | tf_op jit(solution)/shard_map/all_to_all | solution.py:916
  234.7 3.4 convolution_convert_fusion.6
  241.7 3.2 convolution_convert_fusion.8
  250.5 5.9 %fusion.18 = bf16[1,512,768]{2,1,0:T(8,128)(2,1)} fusion(f32[512,768]{1,0:T(8,128)} %get-tuple-element.105, bf16[512,2048]{1,0:T(8,128)(2,1)} %copy-done.53, bf16[2048,768]{1,0:T(8,128)(2,1)} %all-gather.5.cloned.1.call-done), kind=kOutput, calls=%fused_computation.62 | convolution fusion | flops 1611399168 | bytes 7602176 | tf_op jit(solution)/shard_map/dot_general | solution.py:27
  256.4 2.3 copy.68
  258.7 2.4 pad.17.refs_4_
  261.1 75.0 %self_backward.1 = (bf16[2048,256]{1,0:T(8,128)(2,1)}, bf16[2048,256]{1,0:T(8,128)(2,1)}, bf16[2048,256]{1,0:T(8,128)(2,1)}, f32[8,128]{1,0:T(8,128)}, f32[4,24,768]{2,1,0:T(8,128)}, /*index=5*/f32[2,64,768]{2,1,0:T(8,128)}) custom-call(s32[1]{0:T(128)} %copy.92.refs_0_, bf16[2048,768]{1,0:T(8,128)(2,1)} %convolution_convert_fusion.2.refs_1_.refs_2_.refs_3_, ...), custom_call_target="tpu_custom_call" | custom-call | flops 8053063680 | bytes 8388608 | tf_op jit(solution)/shard_map/self_backward/pallas_call | solution.py:325
  339.1 5.1 %multiply_reduce_fusion = (f32[768]{0:T(1024)S(1)}, bf16[2048,768]{1,0:T(8,128)(2,1)}, bf16[2048,768]{1,0:T(8,128)(2,1)}) fusion(bf16[2,2,512,768]{3,2,1,0:T(8,128)(2,1)S(1)} %get-tuple-element.40, f32[2048]{0:T(1024)S(1)} %bitcast.176, f32[768]{0:T(1024)S(1)} %get-tuple-element.70, bf16[2048,768]{1,0:T(8,128)(2,1)S(1)} %constant_dynamic-update-slice_fusion, ...), kind=kOutput, calls=%fused_computation.3 | convolution fusion | flops 2426928384 | bytes 13776896 | tf_op jit(solution)/shard_map/dot_general | solution.py:23
  345.2 6.6 %convolution_convert_fusion.3 = bf16[768,768]{1,0:T(8,128)(2,1)} fusion(bf16[2048,768]{1,0:T(8,128)(2,1)} %get-tuple-element.81, bf16[2048,768]{1,0:T(8,128)(2,1)} %copy-done.36), kind=kOutput, calls=%fused_computation.50 | convolution fusion | flops 2416508928 | bytes 7471104 | tf_op jit(solution)/shard_map/dot_general | solution.py:31
  351.7 46.2 %reduce.15 = (f32[24,768]{1,0:T(8,128)}, f32[24,768]{1,0:T(8,128)}, f32[24,768]{1,0:T(8,128)}, f32[24,768]{1,0:T(8,128)}, f32[8,64,768]{2,1,0:T(8,128)}, /*index=5*/f32[8,128]{1,0:T(8,128)}, f32[8,128]{1,0:T(8,128)}) custom-call(bf16[2,2,4,2,24,768]{5,4,3,2,1,0:T(8,128)(2,1)} %bitcast.152, bf16[2,2,4,2,24,768]{5,4,3,2,1,0:T(8,128)(2,1)} %bitcast.168, ...), custom_call_target="tpu_custom_call" | custom-call | tf_op jit(solution)/shard_map/reduce/pallas_call | solution.py:778
  403.9 3.0 fusion.13
  (207 shorter events, 58.2 us)
Async XLA Ops:
  7.2 4.5 %copy-start.38 = (f32[24,768]{1,0:T(8,128)S(1)}, f32[24,768]{1,0:T(8,128)}, u32[]{:S(2)}) copy-start(f32[24,768]{1,0:T(8,128)} %param.24) | copy-start | bytes 221188
  7.2 4.5 %copy-start.39 = (f32[24,768]{1,0:T(8,128)S(1)}, f32[24,768]{1,0:T(8,128)}, u32[]{:S(2)}) copy-start(f32[24,768]{1,0:T(8,128)} %param.25) | copy-start | bytes 221188
  7.2 4.5 %copy-start.40 = (f32[24,768]{1,0:T(8,128)S(1)}, f32[24,768]{1,0:T(8,128)}, u32[]{:S(2)}) copy-start(f32[24,768]{1,0:T(8,128)} %param.23) | copy-start | bytes 221188
  7.2 4.6 %copy-start.48 = (f32[3,24]{1,0:T(4,128)S(1)}, f32[3,24]{1,0:T(4,128)}, u32[]{:S(2)}) copy-start(f32[3,24]{1,0:T(4,128)} %param.22) | copy-start | bytes 868
  7.2 5.0 %copy-start.2 = (bf16[1,128,768]{2,1,0:T(8,128)(2,1)S(1)}, bf16[1,128,768]{2,1,0:T(8,128)(2,1)}, u32[]{:S(2)}) copy-start(bf16[1,128,768]{2,1,0:T(8,128)(2,1)} %param.19) | copy-start | bytes 589828
  7.2 148.4 %all-gather.3.cloned.1.call-start = ((), (), s32[]{:S(2)}) async-start(), calls=%async_computation.3 | async-start | bytes 6488064 | tf_op jit(solution)/shard_map/all_gather | solution.py:836
  10.0 157.8 %all-gather.5.cloned.1.call-start = ((), (), s32[]{:S(2)}) async-start(), calls=%async_computation.4 | async-start | bytes 3244032 | tf_op jit(solution)/shard_map/all_gather | solution.py:837
  117.8 15.9 %all-to-all-start = ((bf16[4,512,192]{1,2,0:T(8,128)(2,1)}), bf16[4,512,192]{1,2,0:T(8,128)(2,1)}, u32[]{:S(2)}, u32[]{:S(2)}) async-start(bf16[4,512,192]{1,2,0:T(8,128)(2,1)} %copy.66), calls=%async_computation | async-start | bytes 1572864 | tf_op jit(solution)/shard_map/all_to_all | solution.py:870
  122.0 284.8 %reduce-scatter.2.cloned.1.call-start = ((), (), s32[]{:S(2)}) async-start(), calls=%async_computation.5 | async-start | bytes 10137600 | tf_op jit(solution)/shard_map/reduce_scatter | solution.py:896
  122.2 4.7 %copy-start.7 = (bf16[2,2,128,768]{3,2,1,0:T(8,128)(2,1)S(1)}, bf16[2,2,128,768]{3,2,1,0:T(8,128)(2,1)}, u32[]{:S(2)}) copy-start(bf16[2,2,128,768]{3,2,1,0:T(8,128)(2,1)} %copy-done.6) | copy-start | bytes 2359300
  133.7 3.9 copy-start.30
  167.8 8.5 %copy-start.33 = (bf16[1,512,768]{2,1,0:T(8,128)(2,1)S(1)}, bf16[1,512,768]{2,1,0:T(8,128)(2,1)}, u32[]{:S(2)}) copy-start(bf16[1,512,768]{2,1,0:T(8,128)(2,1)} %param.20) | copy-start | bytes 2359300
  176.2 5.4 %copy-start.22 = (bf16[512,2048]{1,0:T(8,128)(2,1)}, bf16[512,2048]{1,0:T(8,128)(2,1)S(1)}, u32[]{:S(2)}) copy-start(bf16[512,2048]{1,0:T(8,128)(2,1)S(1)} %get-tuple-element.71) | copy-start | bytes 6291460
  176.3 5.4 %copy-start.23 = (bf16[512,2048]{1,0:T(8,128)(2,1)}, bf16[512,2048]{1,0:T(8,128)(2,1)S(1)}, u32[]{:S(2)}) copy-start(bf16[512,2048]{1,0:T(8,128)(2,1)S(1)} %get-tuple-element.72) | copy-start | bytes 6291460
  195.2 8.3 %copy-start.10 = (f32[512,768]{1,0:T(8,128)S(1)}, f32[512,768]{1,0:T(8,128)}, u32[]{:S(2)}) copy-start(f32[512,768]{1,0:T(8,128)} %get-tuple-element.105) | copy-start | bytes 4718596
  195.2 8.3 %copy-start.34 = (bf16[1,512,768]{2,1,0:T(8,128)(2,1)S(1)}, bf16[1,512,768]{2,1,0:T(8,128)(2,1)}, u32[]{:S(2)}) copy-start(bf16[1,512,768]{2,1,0:T(8,128)(2,1)} %param.20) | copy-start | bytes 2359300
  221.0 3.3 copy-start.15
  221.0 3.3 copy-start.18
  230.1 26.3 %all-to-all-start.1 = ((bf16[512,4,192]{0,2,1:T(8,128)(2,1)}), bf16[512,4,192]{0,2,1:T(8,128)(2,1)}, u32[]{:S(2)}, u32[]{:S(2)}) async-start(bf16[512,4,192]{0,2,1:T(8,128)(2,1)} %bitcast.156), calls=%async_computation.1 | async-start | bytes 1572864 | tf_op jit(solution)/shard_map/all_to_all | solution.py:916
  234.7 3.4 copy-start.28
  234.7 3.4 copy-start.52
  241.7 3.2 copy-start.19
  241.7 3.2 copy-start.50
  338.8 5.4 %copy-start.36 = (bf16[2048,768]{1,0:T(8,128)(2,1)}, bf16[2048,768]{1,0:T(8,128)(2,1)S(1)}, u32[]{:S(2)}) copy-start(bf16[2048,768]{1,0:T(8,128)(2,1)S(1)} %constant_dynamic-update-slice_fusion) | copy-start | bytes 9437188
  351.7 47.5 %copy-start.1 = (bf16[1,512,768]{2,1,0:T(8,128)(2,1)S(1)}, bf16[1,512,768]{2,1,0:T(8,128)(2,1)}, u32[]{:S(2)}) copy-start(bf16[1,512,768]{2,1,0:T(8,128)(2,1)} %param.18) | copy-start | bytes 2359300
  397.9 5.2 %copy-start.37 = (f32[4,24,768]{2,1,0:T(8,128)S(1)}, f32[4,24,768]{2,1,0:T(8,128)}, u32[]{:S(2)}) copy-start(f32[4,24,768]{2,1,0:T(8,128)} %get-tuple-element.62) | copy-start | bytes 884740
  398.0 5.9 %copy-start.13 = (f32[512,768]{1,0:T(8,128)S(1)}, f32[512,768]{1,0:T(8,128)}, u32[]{:S(2)}) copy-start(f32[512,768]{1,0:T(8,128)} %copy-done.11) | copy-start | bytes 4718596
  406.8 2.7 copy-start.35
  407.8 2.4 copy-start.44
  407.8 3.1 copy-start.43
  407.9 3.7 copy-start.42
  408.0 4.2 copy-start.41
  (27 other events, 40.3 us)
Sparse Core Ops, SparseCore 0:
  11.5 91.8 all-gather.2
  106.9 60.8 all-gather.4
  193.1 162.0 reduce-scatter.1

commit v4 on v3

--- a/solution.py
+++ b/solution.py
@@ -266,6 +266,7 @@
 
     point = 0
     if not causal:
+        at_step(head, stages, 0, 1)
         for start in range(0, keys, key_block):
             for at in range(0, rows, block):
                 piece(slice(start, start + key_block), slice(at, at + block))
@@ -339,6 +340,223 @@
     )(*args, *extra)
 
 
+def scale_of(values):
+    return lax.rsqrt(jnp.mean(values * values, axis=-1, keepdims=True) + epsilon)
+
+
+def project_kernel(gain_lane, x_ref, w_ref, qkv_ref, normed_ref, gains_ref):
+    @pl.when(pl.program_id(0) == 0)
+    def _():
+        tile = gain_lane // LANES * LANES
+        turned = w_ref[:, tile : tile + LANES].astype(jnp.float32).T
+        first = gain_lane - tile
+        gains_ref[...] = turned[first : first + 8]
+
+    values = x_ref[...].astype(jnp.float32)
+    normed = (values * scale_of(values) * gains_ref[0:1, :]).astype(low)
+    normed_ref[...] = normed
+    qkv_ref[...] = nn(normed, w_ref[...]).astype(low)
+
+
+def project(everyone, w_qkv, gain_lane):
+    count, width = everyone.shape
+    wide = w_qkv.shape[1]
+    block = min(BLOCK, count)
+    rows = lambda n: pl.BlockSpec((block, n), lambda i: (i, 0))
+    return pl.pallas_call(
+        functools.partial(project_kernel, gain_lane),
+        grid=(count // block,),
+        in_specs=[rows(width), pl.BlockSpec((width, wide), lambda i: (0, 0))],
+        out_specs=[rows(wide), rows(width), pl.BlockSpec((8, width), lambda i: (0, 0))],
+        out_shape=[
+            jax.ShapeDtypeStruct((count, wide), low), jax.ShapeDtypeStruct((count, width), low),
+            jax.ShapeDtypeStruct((8, width), jnp.float32),
+        ],
+        compiler_params=pltpu.CompilerParams(vmem_limit_bytes=40 * 2**20),
+        name="project",
+    )(everyone, w_qkv)
+
+
+def unproject_kernel(x_ref, normed_ref, w_ref, dq_ref, dk_ref, dv_ref, part_ref, own_ref, gain_ref, own_scr):
+    step = pl.program_id(0)
+    padded = dq_ref.shape[1]
+    grads = [r[...] for r in (dq_ref, dk_ref, dv_ref)]
+    part = sum(nt(g, w_ref[:, n * padded : (n + 1) * padded]) for n, g in enumerate(grads))
+    values = x_ref[...].astype(jnp.float32)
+    share = jnp.sum(part * (values * scale_of(values)), axis=0, keepdims=True)
+    part_ref[...] = part.astype(low)
+    turned = normed_ref[...].T
+
+    @pl.when(step == 0)
+    def _():
+        gain_ref[...] = jnp.zeros_like(gain_ref)
+        own_scr[...] = jnp.zeros_like(own_scr)
+
+    gain_ref[...] += jnp.broadcast_to(share, gain_ref.shape)
+    for n, g in enumerate(grads):
+        own_scr[:, n * padded : (n + 1) * padded] += nn(turned, g)
+
+    @pl.when(step == pl.num_programs(0) - 1)
+    def _():
+        own_ref[...] = own_scr[...].astype(low)
+
+
+def unproject(everyone, normed, w_qkv, dq, dk, dv):
+    count, width = everyone.shape
+    wide, padded = w_qkv.shape[1], dq.shape[1]
+    block = min(BLOCK, count)
+    rows = lambda n: pl.BlockSpec((block, n), lambda i: (i, 0))
+    fixed = lambda a, b: pl.BlockSpec((a, b), lambda i: (0, 0))
+    return pl.pallas_call(
+        unproject_kernel,
+        grid=(count // block,),
+        in_specs=[rows(width), rows(width), fixed(width, wide), rows(padded), rows(padded), rows(padded)],
+        out_specs=[rows(width), fixed(width, wide), fixed(8, width)],
+        out_shape=[
+            jax.ShapeDtypeStruct((count, width), low), jax.ShapeDtypeStruct((width, wide), low),
+            jax.ShapeDtypeStruct((8, width), jnp.float32),
+        ],
+        scratch_shapes=[pltpu.VMEM((width, wide), jnp.float32)],
+        compiler_params=pltpu.CompilerParams(vmem_limit_bytes=50 * 2**20),
+        name="unproject",
+    )(everyone, normed, w_qkv, dq, dk, dv)
+
+
+slope = float(np.sqrt(2.0 / np.pi))
+cubic = 0.044715
+
+
+def middle_kernel(
+    slabs, scalars, x1_ref, mixed_ref, co_ref, gains_ref, cot_ref, gate_ref, up_ref, down_ref,
+    out_ref, dx_ref, dm_ref, co_grad_ref, gain_ref, packed,
+    x2_scr, n3_scr, n3t_scr, df_scr, result_scr, dn_scr, gate_buf, up_buf, down_buf, sem,
+):
+    step, steps = pl.program_id(0), pl.num_programs(0)
+    rows, width = x1_ref.shape
+    block = gate_ref.shape[1]
+    world, share = packed.shape[:2]
+    inner = block * steps
+    owners = down_buf.shape[1]
+    hidden_share = block // owners
+
+    @pl.when(step == 0)
+    def _():
+        x2 = x1_ref[...] + nn(mixed_ref[...], co_ref[...])
+        x2_scr[...] = x2
+        normed = (x2 * scale_of(x2) * gains_ref[2:3, :]).astype(low)
+        n3_scr[...] = normed
+        n3t_scr[...] = normed.T
+        place = scalars[1] + lax.broadcasted_iota(jnp.int32, (rows, 1), 0)
+        df_scr[...] = jnp.where(place < scalars[0], cot_ref[...], 0)
+        result_scr[...] = x2
+        dn_scr[...] = jnp.zeros_like(dn_scr)
+        down_buf[...] = jnp.zeros_like(down_buf)
+
+    normed, df = n3_scr[...], df_scr[...]
+    gate, upper = nn(normed, gate_ref[...]), nn(normed, up_ref[...])
+    bent = jnp.tanh(slope * (gate + cubic * (gate * gate * gate)))
+    half = 0.5 * (1.0 + bent)
+    active = gate * half
+    hidden = (active * upper).astype(low)
+    result_scr[...] += nn(hidden, down_ref[...])
+    grad_hidden = nt(df, down_ref[...])
+    rise = half + (0.5 * gate) * ((1.0 - bent * bent) * (slope + (3.0 * cubic * slope) * (gate * gate)))
+    grad_gate = (grad_hidden * upper * rise).astype(low)
+    grad_upper = (grad_hidden * active).astype(low)
+    dn_scr[...] += nt(grad_gate, gate_ref[...]) + nt(grad_upper, up_ref[...])
+    slot = lax.rem(step, 2)
+
+    def sends(at, which):
+        first = pl.multiple_of(at * block, LANES)
+        yield pltpu.make_async_copy(gate_buf.at[which], packed.at[:, :, pl.ds(first, block)], sem.at[which, 0])
+        yield pltpu.make_async_copy(up_buf.at[which], packed.at[:, :, pl.ds(pl.multiple_of(inner + at * block, LANES), block)], sem.at[which, 1])
+        for k in range(slabs):
+            column = 2 * inner + k * width
+            yield pltpu.make_async_copy(
+                down_buf.at[which, :, k], packed.at[pl.ds(at * owners, owners), :, column : column + width], sem.at[which, 2 + k]
+            )
+
+    @pl.when(step >= 2)
+    def _():
+        for copy in sends(step - 2, slot):
+            copy.wait()
+
+    turned = n3t_scr[...]
+    gate_buf[slot] = nn(turned, grad_gate).reshape(world, share, block).astype(low)
+    up_buf[slot] = nn(turned, grad_upper).reshape(world, share, block).astype(low)
+    grad_down = tn(hidden, df)
+    for o in range(owners):
+        for k in range(slabs):
+            size = min(share, hidden_share - k * share)
+            start = o * hidden_share + k * share
+            down_buf[slot, o, k, :size] = grad_down[start : start + size].astype(low)
+    for copy in sends(step, slot):
+        copy.start()
+
+    @pl.when(step == steps - 1)
+    def _():
+        out_ref[...] = result_scr[...].astype(low)
+        x2, grad_normed = x2_scr[...], dn_scr[...]
+        scale = scale_of(x2)
+        unit = x2 * scale
+        grad_unit = grad_normed * gains_ref[2:3, :]
+        gain_ref[...] = jnp.broadcast_to(jnp.sum(grad_normed * unit, axis=0, keepdims=True), gain_ref.shape)
+        back = scale * (grad_unit - unit * jnp.mean(grad_unit * unit, axis=-1, keepdims=True))
+        dx = df.astype(jnp.float32) + back
+        dx_ref[...] = dx
+        branch = dx.astype(low)
+        dm_ref[...] = nt(branch, co_ref[...]).astype(low)
+        co_grad_ref[...] = tn(mixed_ref[...], branch).astype(low)
+        if steps > 1:
+            for copy in sends(step - 1, 1 - slot):
+                copy.wait()
+        for copy in sends(step, slot):
+            copy.wait()
+
+
+def middle(scalars, x1, mixed, c_output, gains, cotangent, gate_up, w_down, world):
+    rows, width = x1.shape
+    inner = w_down.shape[0]
+    block = min(BLOCK, inner)
+    steps = inner // block
+    share, hidden_share = width // world, inner // world
+    slabs = -(-hidden_share // share)
+    owners = block // hidden_share
+    fixed = lambda *shape: pl.BlockSpec(shape, lambda j: (0,) * len(shape))
+    f32 = jnp.float32
+    return pl.pallas_call(
+        functools.partial(middle_kernel, slabs),
+        grid=(steps,),
+        in_specs=[
+            pl.BlockSpec(memory_space=pltpu.SMEM), fixed(rows, width), fixed(rows, width), fixed(width, width),
+            fixed(8, width), fixed(rows, width),
+            pl.BlockSpec((width, block), lambda j: (0, j)), pl.BlockSpec((width, block), lambda j: (0, steps + j)),
+            pl.BlockSpec((block, width), lambda j: (j, 0)),
+        ],
+        out_specs=[
+            fixed(rows, width), fixed(rows, width), fixed(rows, width), fixed(width, width), fixed(8, width),
+            pl.BlockSpec(memory_space=pl.ANY),
+        ],
+        out_shape=[
+            jax.ShapeDtypeStruct((rows, width), low), jax.ShapeDtypeStruct((rows, width), f32),
+            jax.ShapeDtypeStruct((rows, width), low), jax.ShapeDtypeStruct((width, width), low),
+            jax.ShapeDtypeStruct((8, width), f32),
+            jax.ShapeDtypeStruct((world, share, 2 * inner + slabs * width), low),
+        ],
+        scratch_shapes=[
+            pltpu.VMEM((rows, width), f32), pltpu.VMEM((rows, width), low), pltpu.VMEM((width, rows), low),
+            pltpu.VMEM((rows, width), low), pltpu.VMEM((rows, width), f32), pltpu.VMEM((rows, width), f32),
+            pltpu.VMEM((2, world, share, block), low), pltpu.VMEM((2, world, share, block), low),
+            pltpu.VMEM((2, owners, slabs, share, width), low), pltpu.SemaphoreType.DMA((2, 2 + slabs)),
+        ],
+        compiler_params=pltpu.CompilerParams(vmem_limit_bytes=62 * 2**20),
+        cost_estimate=pl.CostEstimate(
+            flops=2 * rows * width * (9 * inner + 3 * width), transcendentals=rows * inner, bytes_accessed=26 * width * inner // 4
+        ),
+        name="middle",
+    )(scalars, x1, mixed, c_output, gains, cotangent, gate_up, gate_up, w_down)
+
+
 def coordinates():
     place, slot = lax.axis_index("seq"), lax.axis_index("fsdp")
     return place // 2, lax.rem(place, 2), slot // 2, lax.rem(slot, 2)
@@ -395,9 +613,17 @@
 
 
 def add_low(target, left, right):
-    @pl.loop(0, left.shape[0])
+    count = left.shape[0]
+    unroll = 4 if count % 4 == 0 else 1
+
+    @pl.loop(0, count // unroll)
     def _(n):
-        target[n] = (left[n].astype(jnp.float32) + right[n].astype(jnp.float32)).astype(target.dtype)
+        for k in range(unroll):
+            at = n * unroll + k
+            if target.dtype == low:
+                target[at] = left[at] + right[at]
+            else:
+                target[at] = left[at].astype(target.dtype) + right[at].astype(target.dtype)
 
 
 def whole(space=pltpu.VMEM):
@@ -486,45 +712,46 @@
 
 
 class ReducePlan:
-    outputs = 2
-
-    def __init__(self, nz, count, share, width, slabs):
+    def __init__(self, nz, count, share, width, number, points, slabs=None):
         self.nz, self.count, self.share, self.width, self.slabs = nz, count, share, width, slabs
-        self.inputs = count + 1
-        self.total = count * (nz + 2) + 2
+        self.number, self.points = number, points
+        self.inputs = count + (slabs is not None)
+        self.outputs = 1 + (slabs is not None)
+        self.total = count * (nz + 1) + count + 2 * (slabs is not None)
 
     def in_specs(self):
         return [whole()] * self.inputs
 
     def out_specs(self):
-        return [whole(), whole()]
+        return [whole()] * self.outputs
 
     def out_shape(self):
-        return [
-            jax.ShapeDtypeStruct((self.count, self.share, self.width), jnp.float32),
-            jax.ShapeDtypeStruct(self.slabs, jnp.float32),
-        ]
+        shapes = [jax.ShapeDtypeStruct((self.count, self.share, self.width), jnp.float32)]
+        return shapes + ([jax.ShapeDtypeStruct(self.slabs, jnp.float32)] if self.slabs else [])
 
     def scratch(self):
         nz, tail = self.nz, (self.share, self.width)
         vmem = lambda *shape: pltpu.VMEM((self.count, *shape, *tail), low)
-        slabs = [pltpu.VMEM((*lead, *self.slabs), low) for lead in ((2,), (2,), ())]
+        slabs = [pltpu.VMEM((*lead, *self.slabs), low) for lead in ((2,), (2,), ())] if self.slabs else []
         sems = [pltpu.SemaphoreType.DMA((self.total,)), pltpu.SemaphoreType.DMA((self.total,))]
         return [vmem(2, 2, nz), vmem(2, nz, 2), vmem(2, nz), vmem(2, nz), vmem(nz), vmem(nz), vmem(nz - 1), *slabs, *sems]
 
     def params(self):
-        return pltpu.CompilerParams(collective_id=3, has_side_effects=True, vmem_limit_bytes=60 * 2**20)
+        return pltpu.CompilerParams(collective_id=self.number, has_side_effects=True, vmem_limit_bytes=60 * 2**20)
 
     def stages(self, given, made, scratch):
-        squares, enc = given[:-1], given[-1]
-        out, out_enc = made
-        a, ra, b, rb, d, rd, re, enc_r, enc_a, enc_rx, send_sem, recv_sem = scratch
+        squares, out, beside = given[: self.count], made[0], self.slabs is not None
+        a, ra, b, rb, d, rd, re = scratch[:7]
+        send_sem, recv_sem = scratch[-2:]
+        if beside:
+            enc, out_enc, (enc_r, enc_a, enc_rx) = given[-1], made[1], scratch[7:10]
         nz, my, count = self.nz, Near(self.nz), self.count
         x, c, z, y = my.x, my.c, my.z, my.y
         copies = Copies(send_sem, recv_sem)
-        enc_core = copies.add(lambda: enc.at[:, 1 - c], lambda: enc_r, my.by_core)
+        if beside:
+            enc_core = copies.add(lambda: enc.at[:, 1 - c], lambda: enc_r, my.by_core)
+            enc_x = copies.add(lambda: enc_a.at[1 - x], lambda: enc_rx, my.by_x)
         core = [copies.add(lambda n=n: squares[n].at[:, 1 - c], lambda n=n: ra.at[n], my.by_core) for n in range(count)]
-        enc_x = copies.add(lambda: enc_a.at[1 - x], lambda: enc_rx, my.by_x)
         one, two, three = [], [], []
         for n in range(count):
             y_first = n % 2 == 0
@@ -541,7 +768,7 @@
 
         def begin():
             greet([my.by_x, my.by_core, my.by_y, *my.by_z[1:]])
-            copies.start(*core, enc_core)
+            copies.start(*core, *([enc_core] if beside else []))
 
         def after_core(n):
             copies.arrive(core[n])
@@ -578,19 +805,20 @@
             copies.start(enc_x)
 
         def end():
-            copies.arrive(enc_x)
-            add_low(out_enc, enc_a.at[x], enc_rx)
+            if beside:
+                copies.arrive(enc_x)
+                add_low(out_enc, enc_a.at[x], enc_rx)
             for n in range(count):
                 after_three(n)
             copies.finish()
 
         part = functools.partial
-        work = [part(after_core, n) for n in range(count)] + [encoder]
+        work = [part(after_core, n) for n in range(count)] + ([encoder] if beside else [])
         work += [part(after_one, n) for n in range(count)] + [part(after_two, n) for n in range(count)]
-        points = 3 * BACKWARD_POINTS - 2
+        first, last = self.points // 12, self.points - 1 - self.points // 12
         stages = [(0, begin)]
         for number, stage in enumerate(work):
-            stages.append((2 + number * (points - 2) // len(work), stage))
+            stages.append((first + number * (last - first) // max(len(work) - 1, 1), stage))
         return stages + [(-1, end)]
 
 
@@ -674,22 +902,32 @@
     pl.semaphore_wait(barrier, world - 1)
     copies = Copies(send_sem, recv_sem)
     add = copies.add
-    tok_core = [add(lambda h=h: tok.at[h, 1 - c], lambda h=h: tok_r.at[h], my.by_core) for h in (1 - x, x)]
-    own_y = add(lambda: own.at[:, :, :, 1 - y], lambda: own_r, my.by_y)
+    half = tok.shape[2] // 2
+    padded = own.shape[-1] // 3
+    cut = lambda p: slice(p * half, (p + 1) * half)
+    own_cut = lambda n: slice(n * padded, (n + 1) * padded)
+    tok_core = [
+        add(lambda h=h, p=p: tok.at[h, 1 - c, cut(p)], lambda h=h, p=p: tok_r.at[h, cut(p)], my.by_core)
+        for h in (1 - x, x) for p in range(2)
+    ]
+    own_y = [
+        add(lambda n=n: own.at[:, :, :, 1 - y, :, own_cut(n)], lambda n=n: own_r.at[n], my.by_y) for n in range(3)
+    ]
     core = add(lambda: square.at[:, 1 - c], lambda: ra, my.by_core)
     near_all = [add(lambda: near, lambda t=t: near_r.at[t - 1], (place, lax.rem(slot + t, slots))) for t in range(1, slots)]
-    tok_x = add(lambda: tok_a.at[1 - x], lambda: tok_rx, my.by_x)
+    tok_x = [add(lambda p=p: tok_a.at[1 - x, cut(p)], lambda p=p: tok_rx.at[cut(p)], my.by_x) for p in range(2)]
     one = add(lambda: a.at[:, 1 - y], lambda: rb, my.by_y)
     two = add(lambda: b.at[1 - x], lambda: rd, my.by_x)
     three = [add(lambda t=t: d.at[my.steps[t]], lambda t=t: re.at[t - 1], my.by_z[t]) for t in range(1, nz)]
     own_z = [
-        add(lambda t=t: own_a.at[:, :, my.steps[t]], lambda t=t: own_rz.at[t - 1], my.by_z[t]) for t in range(1, nz)
+        [add(lambda n=n, t=t: own_a.at[n, :, :, my.steps[t]], lambda n=n, t=t: own_rz.at[n, t - 1], my.by_z[t]) for t in range(1, nz)]
+        for n in range(3)
     ]
-    landing = lambda: own_in.at[x, c]
+    landing = lambda: own_in.at[:, x, c]
     own_seq = [
-        add(lambda: own_f.at[1 - x, c], landing, my.by_x),
-        add(lambda: own_f.at[x, 1 - c], landing, my.by_core),
-        add(lambda: own_f.at[1 - x, 1 - c], landing, my.diagonal),
+        add(lambda: own_f.at[:, 1 - x, c], landing, my.by_x),
+        add(lambda: own_f.at[:, x, 1 - c], landing, my.by_core),
+        add(lambda: own_f.at[:, 1 - x, 1 - c], landing, my.diagonal),
     ]
 
     def gain_copy(t):
@@ -699,40 +937,56 @@
             device_id=(other // slots, lax.rem(other, slots)), device_id_type=MESH,
         )
 
-    copies.start(own_y, tok_core[0], core, tok_core[1], *near_all)
+    copies.start(own_y[0], *tok_core[:2], own_y[1], core, *tok_core[2:], own_y[2], *near_all)
 
     @pl.loop(1, world)
     def _(t):
         gain_copy(t).start()
 
-    copies.arrive(tok_core[0])
-    add_low(tok_a.at[1 - x], tok.at[1 - x, c], tok_r.at[1 - x])
-    copies.start(tok_x)
+    def tok_sum(h, p):
+        add_low(tok_a.at[h, cut(p)], tok.at[h, c, cut(p)], tok_r.at[h, cut(p)])
+
+    for p in range(2):
+        copies.arrive(tok_core[p])
+        tok_sum(1 - x, p)
+        copies.start(tok_x[p])
     copies.arrive(core)
-    for half in range(2):
+    for h in range(2):
         for side in range(2):
-            add_low(a.at[half, side], square.at[half, c, :, side], ra.at[half, :, side])
+            add_low(a.at[h, side], square.at[h, c, :, side], ra.at[h, :, side])
     copies.start(one)
-    copies.arrive(tok_core[1])
-    add_low(tok_a.at[x], tok.at[x, c], tok_r.at[x])
-    copies.arrive(own_y)
-    for half in range(2):
-        for side in range(2):
-            add_low(own_a.at[half, side], own.at[half, side, :, y], own_r.at[half, side])
-    copies.start(*own_z)
+
+    def own_sum(n):
+        copies.arrive(own_y[n])
+        for h in range(2):
+            for side in range(2):
+                for k in range(nz):
+                    own_a[n, h, side, k] = own[h, side, k, y, :, own_cut(n)] + own_r[n, h, side, k]
+        copies.start(*own_z[n])
+
+    own_sum(0)
+    for p in range(2):
+        copies.arrive(tok_core[2 + p])
+        tok_sum(x, p)
+    own_sum(1)
+    own_sum(2)
     copies.arrive(one)
     for side in range(2):
         add_low(b.at[side], a.at[side, y], rb.at[side])
     copies.start(two)
-    copies.arrive(*own_z)
-    for half in range(2):
-        for side in range(2):
-            total = own_a[half, side, z].astype(jnp.float32)
-            for t in range(nz - 1):
-                total += own_rz[t, half, side].astype(jnp.float32)
-            own_f[half, side] = total.astype(low)
+    for n in range(3):
+        copies.arrive(*own_z[n])
+        for h in range(2):
+            for side in range(2):
+                total = own_a[n, h, side, z].astype(jnp.float32)
+                for t in range(nz - 1):
+                    total += own_rz[n, t, h, side].astype(jnp.float32)
+                own_f[n, h, side] = total.astype(low)
     copies.start(*own_seq)
-    own_in[x, c] = own_f[x, c]
+    own_in[:, x, c] = own_f[:, x, c]
+    copies.arrive(two)
+    add_low(d, b.at[x], rd)
+    copies.start(*three)
     copies.arrive(*near_all)
     total = near[...]
     for t in range(slots - 1):
@@ -745,16 +999,13 @@
         gain_copy(t).wait_recv()
         out_gain[...] += gain_r[t - 1]
 
+    for p in range(2):
+        copies.arrive(tok_x[p])
+        add_low(out_tok.at[cut(p)], tok_a.at[x, cut(p)], tok_rx.at[cut(p)])
     copies.arrive(*own_seq)
-    padded = own_in.shape[-1] // 3
     for n, out in enumerate((out_q, out_k, out_v)):
-        parts = [own_in[s // 2, s % 2, :, n * padded : n * padded + group_width].astype(jnp.float32) for s in range(4)]
+        parts = [own_in[n, s // 2, s % 2, :, :group_width].astype(jnp.float32) for s in range(4)]
         out[...] = jnp.concatenate(parts, axis=1)
-    copies.arrive(two)
-    add_low(d, b.at[x], rd)
-    copies.start(*three)
-    copies.arrive(tok_x)
-    add_low(out_tok, tok_a.at[x], tok_rx)
     copies.arrive(*three)
     total = d[z].astype(jnp.float32)
     for t in range(nz - 1):
@@ -773,7 +1024,8 @@
     vmem = lambda *shape: pltpu.VMEM(shape, low)
     slabs = tok.shape[2:]
     world = 8 * nz
-    total = 4 + 2 * nz - 1 + 3 + 2 * (nz - 1) + 3
+    padded = wide // 3
+    total = 4 + 3 + 1 + 2 * nz - 1 + 2 + 2 + nz - 1 + 3 * (nz - 1) + 3
     f32 = lambda *shape: jax.ShapeDtypeStruct(shape, jnp.float32)
     return pl.pallas_call(
         functools.partial(reduce_kernel, nz, group_width),
@@ -783,8 +1035,8 @@
         scratch_shapes=[
             vmem(2, 2, nz, share, width), vmem(2, nz, 2, share, width), vmem(2, nz, share, width), vmem(2, nz, share, width),
             vmem(nz, share, width), vmem(nz, share, width), vmem(nz - 1, share, width),
-            vmem(2, 2, nz, share, wide), vmem(2, 2, nz, share, wide), vmem(nz - 1, 2, 2, share, wide), vmem(2, 2, share, wide),
-            vmem(2, 2, share, wide),
+            vmem(3, 2, 2, nz, share, padded), vmem(3, 2, 2, nz, share, padded), vmem(3, nz - 1, 2, 2, share, padded),
+            vmem(3, 2, 2, share, padded), vmem(3, 2, 2, share, padded),
             vmem(2, *slabs), vmem(2, *slabs), vmem(*slabs),
             pltpu.VMEM((world - 1, *gain.shape[1:]), jnp.float32), pltpu.VMEM((2 * nz - 1, *near.shape), jnp.float32),
             pltpu.SemaphoreType.DMA((total,)), pltpu.SemaphoreType.DMA((total,)),
@@ -853,12 +1105,9 @@
     everyone = everyone.reshape(seq * rows, width)
     encoded = encoded.reshape(-1, width)
     w_qkv = w_qkv.reshape(width, 3 * padded)
-    gain_rows = w_qkv[:, group_width : group_width + 3].astype(jnp.float32).T
-
     length = lengths[0]
     values_in = tokens[0].astype(jnp.float32)
-    normed_all = rms_norm(everyone.astype(jnp.float32), gain_rows[0]).astype(low)
-    qkv = nn(normed_all, w_qkv).astype(low)
+    qkv, normed_all, gain_rows = project(everyone, w_qkv, group_width)
     bias = bias_rows(rel_bias)
     plan = GatherPlan(nz, 5, share, width) if aligned else None
     own_mixed, own_logsum, *gathered = attend_forward(
@@ -874,35 +1123,48 @@
     cross_keys = nn(encoded, c_key).astype(low)
     cross_values = nn(encoded, c_value).astype(low)
     cross_mixed, cross_logsum = attend_forward(cross_queries, cross_keys, cross_values, heads)
-    crossed = attended + nn(cross_mixed, c_output)
-    normed_three = rms_norm(crossed, gain_rows[2]).astype(low)
-    both_parts = nn(normed_three, gate_up)
-    gate, upper = both_parts[:, :inner], both_parts[:, inner:]
-    hidden = activate(gate, upper).astype(low)
-    result = crossed + nn(hidden, w_down)
-
-    positions = place * rows + jnp.arange(rows, dtype=jnp.int32)
-    grad_out = cotangent[0].astype(jnp.float32) * (positions < length).astype(jnp.float32)[:, None]
-    grad_ffn = grad_out.astype(low)
-    grad_hidden = nt(grad_ffn, w_down)
-    _, pullback = jax.vjp(activate, gate, upper)
-    grad_gate, grad_upper = pullback(grad_hidden)
-    grad_both = jnp.concatenate([grad_gate.astype(low), grad_upper.astype(low)], axis=1)
     slabs = -(-hidden_share // share)
-    grad_down = tn(hidden, grad_ffn).astype(low).reshape(world, hidden_share, width)
-    grad_down = jnp.pad(grad_down, ((0, 0), (0, slabs * share - hidden_share), (0, 0)))
-    grad_down = grad_down.reshape(world, slabs, share, width).transpose(0, 2, 1, 3).reshape(world * share, slabs * width)
-    packed = jnp.concatenate([tn(normed_three, grad_both).astype(low), grad_down], axis=1)
+    if aligned:
+        scalars = jnp.stack([length, place * rows])
+        result, grad_crossed, grad_cmixed, grad_coutput, gain_two, packed = middle(
+            scalars, attended, cross_mixed, c_output, gain_rows, cotangent[0], gate_up, w_down, world
+        )
+        grad_gain_two = gain_two[0]
+        packed = packed.reshape(width, -1)
+    else:
+        crossed = attended + nn(cross_mixed, c_output)
+        normed_three = rms_norm(crossed, gain_rows[2]).astype(low)
+        both_parts = nn(normed_three, gate_up)
+        gate, upper = both_parts[:, :inner], both_parts[:, inner:]
+        hidden = activate(gate, upper).astype(low)
+        result = (crossed + nn(hidden, w_down)).astype(low)
+
+        positions = place * rows + jnp.arange(rows, dtype=jnp.int32)
+        grad_out = cotangent[0].astype(jnp.float32) * (positions < length).astype(jnp.float32)[:, None]
+        grad_ffn = grad_out.astype(low)
+        grad_hidden = nt(grad_ffn, w_down)
+        _, pullback = jax.vjp(activate, gate, upper)
+        grad_gate, grad_upper = pullback(grad_hidden)
+        grad_both = jnp.concatenate([grad_gate.astype(low), grad_upper.astype(low)], axis=1)
+        grad_down = tn(hidden, grad_ffn).astype(low).reshape(world, hidden_share, width)
+        grad_down = jnp.pad(grad_down, ((0, 0), (0, slabs * share - hidden_share), (0, 0)))
+        grad_down = grad_down.reshape(world, slabs, share, width).transpose(0, 2, 1, 3).reshape(world * share, slabs * width)
+        packed = jnp.concatenate([tn(normed_three, grad_both).astype(low), grad_down], axis=1)
+
+        grad_normed_three = nt(grad_both, gate_up)
+        norm_part, grad_gain_two = rms_back(crossed, gain_rows[2], grad_normed_three)
+        grad_crossed = grad_out + norm_part
+        grad_branch = grad_crossed.astype(low)
+        grad_coutput = tn(cross_mixed, grad_branch).astype(low)
+        grad_cmixed = nt(grad_branch, c_output).astype(low)
     share_ffn = lax.psum_scatter(packed, both, scatter_dimension=0, tiled=True)
-
-    grad_normed_three = nt(grad_both, gate_up)
-    norm_part, grad_gain_two = rms_back(crossed, gain_rows[2], grad_normed_three)
-    grad_crossed = grad_out + norm_part
-    grad_branch = grad_crossed.astype(low)
-    grad_coutput = tn(cross_mixed, grad_branch).astype(low)
-    grad_cmixed = nt(grad_branch, c_output).astype(low)
-    grad_cq, grad_ck, grad_cv = attend_backward(
-        cross_queries, cross_keys, cross_values, grad_cmixed, cross_mixed, cross_logsum, heads
+    slab = 64
+    chunked = lambda g: g.reshape(2, 2, nz, 2, share, g.shape[-1])
+    by_place = lambda g: g.reshape(2, 2, -1, slab, width)
+    plan = ReducePlan(nz, 1, share, width, 4, heads) if aligned else None
+    grad_cq, grad_ck, grad_cv, *first_sums = attend_backward(
+        cross_queries, cross_keys, cross_values, grad_cmixed, cross_mixed, cross_logsum, heads,
+        plan=plan, extra=(chunked(grad_coutput),) if aligned else (),
     )
     grad_cquery = tn(normed_two, grad_cq).astype(low)
     grad_ckey = tn(encoded, grad_ck).astype(low)
@@ -915,24 +1177,16 @@
     grad_mixed = nt(grad_self_branch, w_output).astype(low)
     own_grad_mixed = lax.all_to_all(grad_mixed, "seq", split_axis=1, concat_axis=0, tiled=True)
     own_grad_mixed = jnp.pad(own_grad_mixed, ((0, 0), (0, padded - group_width)))
-    slab = 64
-    chunked = lambda g: g.reshape(2, 2, nz, 2, share, g.shape[-1])
-    by_place = lambda g: g.reshape(2, 2, -1, slab, width)
-    early = [grad_cquery, grad_ckey, grad_cvalue, grad_coutput]
+    early = [grad_cquery, grad_ckey, grad_cvalue]
     plan, extra = None, ()
     if aligned:
         extra = (*[chunked(g) for g in early], by_place(grad_encoded))
-        plan = ReducePlan(nz, len(early), share, width, extra[-1].shape[2:])
+        plan = ReducePlan(nz, len(early), share, width, 3, 3 * BACKWARD_POINTS, extra[-1].shape[2:])
     own_dq, own_dk, own_dv, by_distance, *sums = attend_backward(
         qkv, qkv, qkv, own_grad_mixed, own_mixed, own_logsum, group, padded, bias, lengths, plan, extra
     )
-    own_qkv = jnp.concatenate([own_dq, own_dk, own_dv], axis=1)
-    grad_normed_part = nt(own_qkv, w_qkv)
-    values_all = everyone.astype(jnp.float32)
-    units_all = values_all * lax.rsqrt(jnp.mean(values_all * values_all, axis=-1, keepdims=True) + epsilon)
-    grad_gain_zero = jnp.sum(grad_normed_part * units_all, axis=0)
-    grad_normed_part = grad_normed_part.astype(low)
-    grad_own = tn(normed_all, own_qkv).astype(low)
+    grad_normed_part, grad_own, gain_zero = unproject(everyone, normed_all, w_qkv, own_dq, own_dk, own_dv)
+    grad_gain_zero = gain_zero[0]
     grad_gains = jnp.stack([grad_gain_zero, grad_gain_one, grad_gain_two])
     grad_gains = grad_gains.reshape(3, world, share).transpose(1, 0, 2).reshape(world, 1, 3 * share)
     grad_gains = jnp.pad(grad_gains, ((0, 0), (0, 7), (0, LANES - 3 * share)))
@@ -942,11 +1196,11 @@
             nz, group_width, chunked(grad_output), chunked(grad_own), by_place(grad_normed_part), grad_gains, by_distance
         )
         share_early, grad_encoded = sums
-        share_squares = [share_output, *(share_early[n] for n in range(4))]
+        share_squares = [share_output, *(share_early[n] for n in range(3)), first_sums[0][0]]
         grad_normed, grad_encoded = grad_normed.reshape(rows, width), grad_encoded.reshape(-1, width)
     else:
         scatter = lambda g, axes: lax.psum_scatter(g, axes, scatter_dimension=0, tiled=True)
-        share_squares = scatter(jnp.concatenate([grad_output, *early], axis=1), both).astype(wide)
+        share_squares = scatter(jnp.concatenate([grad_output, *early, grad_coutput], axis=1), both).astype(wide)
         share_squares = [share_squares[:, n * width : (n + 1) * width] for n in range(5)]
         grad_own = scatter(grad_own.reshape(seq, fsdp, share, 3 * padded).transpose(1, 0, 2, 3), "fsdp")[0]
         grad_own = lax.all_to_all(grad_own, "seq", split_axis=0, concat_axis=0, tiled=True).astype(wide)
@@ -966,7 +1220,7 @@
     share_ffn = share_ffn.astype(wide)
     share_down = share_ffn[:, 2 * inner :].reshape(share, slabs, width).transpose(1, 0, 2).reshape(slabs * share, width)
     return (
-        result.astype(low)[None], grad_input[None], grad_encoded[None], share_gains, *share_own, *share_squares,
+        result[None], grad_input[None], grad_encoded[None], share_gains, *share_own, *share_squares,
         share_ffn[:, :inner], share_ffn[:, inner : 2 * inner], share_down[:hidden_share], table_grad,
     )
 

time: 428 us -> 387 us (0.904); the launches traced: 420 us -> 388 us
  matrix products: 88.8 us -> 24 us
  Pallas kernels: 235 us -> 267 us
  waiting for transfers between devices: 5.56 us -> 27.9 us
  other arithmetic: 26.9 us -> 12.1 us
  local copies, waits for them, and re-layouts: 38.8 us -> 33.4 us
    pallas_call x0 -> x3, Pallas kernels: none -> 42.4 us  [the longest x1 27 us: middle(): pl.pallas_call(functools.partial(middle_kernel, slabs), grid=(steps,), in...]
    dot_general x8 -> x4, matrix products: 31 us -> 6.51 us  [nt(): lax.dot_general(left, right, (((1,), (1,)), ((), ())), preferred_element_...]
    dot_general x8 -> x4, matrix products: 31.8 us -> 7.69 us  [nn(): return jnp.dot(left, right, preferred_element_type=jnp.float32)]
    all_gather x1, waiting for transfers between devices: 0.01 us -> 22 us  [per_device(): lax.all_gather(jnp.concatenate([ffn_gate.astype(low), ffn_up.astype(low)]...]
    dot_general x8 -> x4, matrix products: 24.9 us -> 8.73 us  [tn(): lax.dot_general(left, right, (((0,), (0,)), ((), ())), preferred_element_...]
    concatenate x1 -> x0, other arithmetic: 6.41 us -> none  [per_device(): jnp.concatenate([tn(normed_three, grad_both).astype(low), grad_down], axi...]
    pallas_call x2, Pallas kernels: 65.7 us -> 60.7 us  [attend_forward(): pl.pallas_call(functools.partial(attend_forward_kernel, causal=causal, he...]
    unnamed x118 -> x104, local copies, waits for them, and re-layouts: 15.6 us -> 14.2 us
  transfers between devices with their start and end apart: 5 -> 5, of which waited for: 2 -> 2; matrix products, arithmetic and copies ran while one was open for 27% -> 13% of each run, Pallas kernels for 56% -> 62%
where the time goes in v4:
time: 387 us; the launch traced here: 388 us
  Pallas kernels  267 us (69%)
  local copies, waits for them, and re-layouts  33.4 us (9%)
  waiting for transfers between devices  27.9 us (7%)
  matrix products  24 us (6%)
  between operations  15.4 us (4%)
  other arithmetic  12.1 us (3%)
  starting transfers between devices  7.82 us (2%)
    pallas_call x2, Pallas kernels, attend_backward(): pl.pallas_call(functools.partial(attend_backward_kernel, causal=causal, h...  87.5 us
    pallas_call x2, Pallas kernels, attend_forward(): pl.pallas_call(functools.partial(attend_forward_kernel, causal=causal, he...  60.7 us
    pallas_call x1, Pallas kernels, reduce(): pl.pallas_call(functools.partial(reduce_kernel, nz, group_width), in_spec...  44.2 us
    pallas_call x1, Pallas kernels, gather(): pl.pallas_call(functools.partial(gather_kernel, nz), in_specs=[whole()] *...  32.2 us
    pallas_call x1, Pallas kernels, middle(): pl.pallas_call(functools.partial(middle_kernel, slabs), grid=(steps,), in...  27 us
    all_gather x1, waiting for transfers between devices, per_device(): lax.all_gather(jnp.concatenate([ffn_gate.astype(low), ffn_up.astype(low)]...  22 us
    unnamed x104, local copies, waits for them, and re-layouts  14.2 us
    pallas_call x1, Pallas kernels, unproject(): pl.pallas_call(unproject_kernel, grid=(count // block,), in_specs=[rows(w...  11.6 us
  transfers between devices with their start and end apart: 5, of which 2 were waited for; matrix products, arithmetic and copies ran while one was open for 13% of the time, Pallas kernels for 62%

profile of v4, /device:TPU:0, one launch (start us, length us, event | category | flops | bytes accessed | tf_op | source)
XLA Modules:
  0.0 387.5 jit_solution(14024822036966943994)
XLA Ops:
  7.3 1.7 convert_element_type.111
  12.8 32.2 %gather.1 = (bf16[2,2,512,768]{3,2,1,0:T(8,128)(2,1)S(1)}, bf16[2,2,128,768]{3,2,1,0:T(8,128)(2,1)S(1)}, bf16[2,2,4,2,24,768]{5,4,3,2,1,0:T(8,128)(2,1)S(1)}) custom-call(bf16[512,768]{1,0:T(8,128)(2,1)S(1)} %bitcast.94, bf16[128,768]{1,0:T(8,128)(2,1)S(1)} %bitcast.101, bf16[2,2,24,768]{3,2,1,0:T(8,128)(2,1)S(1)} %bitcast.100), custom_call_target="tpu_custom_call" | custom-call | tf_op jit(solution)/shard_map/gather/pallas_call | solution.py:874
  45.2 3.8 project.1
  49.0 1.7 copy-done.3
  50.7 1.7 copy-done.9
  54.2 48.2 %self_forward.1 = (bf16[2048,256]{1,0:T(8,128)(2,1)}, f32[3,8,2048]{2,1,0:T(8,128)}, bf16[5,2,2,4,2,24,768]{6,5,4,3,2,1,0:T(8,128)(2,1)}) custom-call(s32[1]{0:T(128)S(6)} %copy.83.refs_0_, bf16[2048,768]{1,0:T(8,128)(2,1)} %copy-done.9, bf16[2048,768]{1,0:T(8,128)(2,1)} %copy-done.9, bf16[2048,768]{1,0:T(8,128)(2,1)} %copy-done.9, ...), custom_call_target="tpu_custom_call" | custom-call | flops 3221225472 | bytes 4194304 | tf_op jit(solution)/shard_map/self_forward/pallas_call | solution.py:188
  102.4 2.2 copy.63
  104.6 3.5 all-to-all-start
  108.2 4.6 %fusion.13 = (bf16[1,2,2,4,2,24,768]{6,5,4,3,2,1,0:T(8,128)(2,1)}, bf16[1,2,2,4,2,24,768]{6,5,4,3,2,1,0:T(8,128)(2,1)S(1)}, bf16[1,2,2,4,2,24,768]{6,5,4,3,2,1,0...) fusion(bf16[5,2,2,4,2,24,768]{6,5,4,3,2,1,0:T(8,128)(2,1)} %get-tuple-element.57), kind=kLoop, calls=%fused_computation.68 | loop fusion | bytes 11796480 | tf_op jit(solution)/shard_map/slice | solution.py:1118
  113.6 1.7 convolution_convert_fusion.5.refs_2_
  115.2 1.7 convolution_convert_fusion.6.refs_1_
  117.0 5.8 %all-to-all-done = bf16[4,512,192]{1,2,0:T(8,128)(2,1)S(1)} async-done(((bf16[4,512,192]{1,2,0:T(8,128)(2,1)}), bf16[4,512,192]{1,2,0:T(8,128)(2,1)S(1)}, u32[]{:S(2)}, u32[]{:S(2)}) %all-to-all-start) | async-done | bytes 786464 | tf_op jit(solution)/shard_map/all_to_all | solution.py:1119
  122.8 2.5 multiply_reduce_fusion.2
  126.5 1.8 convolution_convert_fusion.7.refs_0_
  128.3 12.5 %cross_forward.1 = (bf16[512,768]{1,0:T(8,128)(2,1)}, f32[12,8,512]{2,1,0:T(8,128)}) custom-call(bf16[512,768]{1,0:T(8,128)(2,1)} %convolution_convert_fusion.7.refs_0_, bf16[512,768]{1,0:T(8,128)(2,1)} %convolution_convert_fusion.6.refs_1_, bf16[512,768]{1,0:T(8,128)(2,1)} %convolution_convert_fusion.5.refs_2_), custom_call_target="tpu_custom_call" | custom-call | flops 1610612736 | bytes 3145728 | tf_op jit(solution)/shard_map/cross_forward/pallas_call | solution.py:188
  140.8 22.0 %all-gather.3.cloned.1.call-done.gate_ref.up_ref = bf16[768,4096]{1,0:T(8,128)(2,1)} async-done(((bf16[24,4096]{1,0:T(8,128)(2,1)}), bf16[768,4096]{1,0:T(8,128)(2,1)}) %all-gather.3.cloned.1.call-update) | async-done | bytes 6291472 | tf_op jit(solution)/shard_map/all_gather | solution.py:1088
  162.7 27.0 %middle.1 = (bf16[512,768]{1,0:T(8,128)(2,1)}, f32[512,768]{1,0:T(8,128)}, bf16[512,768]{1,0:T(8,128)(2,1)}, bf16[768,768]{1,0:T(8,128)(2,1)}, f32[8,768]{1,0:T(8,128)}, /*index=5*/bf16[32,24,6400]{2,1,0:T(8,128)(2,1)}) custom-call(s32[2]{0:T(128)} %pad_add_fusion.scalars, f32[512,768]{1,0:T(8,128)} %copy-done.14, ...), custom_call_target="tpu_custom_call" | custom-call | flops 16307453952 | bytes 10223616 | tf_op jit(solution)/shard_map/middle/pallas_call | solution.py:527
  190.2 26.7 %cross_backward.1 = (bf16[512,768]{1,0:T(8,128)(2,1)}, bf16[512,768]{1,0:T(8,128)(2,1)}, bf16[512,768]{1,0:T(8,128)(2,1)}, f32[1,24,768]{2,1,0:T(8,128)}) custom-call(bf16[512,768]{1,0:T(8,128)(2,1)} %convolution_convert_fusion.7.refs_0_, bf16[512,768]{1,0:T(8,128)(2,1)} %convolution_convert_fusion.6.refs_1_, ...), custom_call_target="tpu_custom_call" | custom-call | flops 4026531840 | bytes 6291456 | tf_op jit(solution)/shard_map/cross_backward/pallas_call | solution.py:326
  217.0 2.3 multiply_reduce_fusion
  220.6 1.7 convolution_convert_fusion.4
  222.3 2.4 copy.64
  224.7 4.2 %all-to-all-start.1 = ((bf16[512,4,192]{0,2,1:T(8,128)(2,1)}), bf16[512,4,192]{0,2,1:T(8,128)(2,1)}, u32[]{:S(2)}, u32[]{:S(2)}) async-start(bf16[512,4,192]{0,2,1:T(8,128)(2,1)} %bitcast.112), calls=%async_computation.1 | async-start | bytes 1572864 | tf_op jit(solution)/shard_map/all_to_all | solution.py:1178
  229.9 3.1 convolution_convert_fusion.1
  234.2 1.8 convolution_convert_fusion.3
  236.0 1.9 convolution_convert_fusion.2
  237.9 1.9 convolution_convert_fusion
  239.8 1.7 add_convert_fusion
  244.1 60.8 %self_backward.1 = (bf16[2048,256]{1,0:T(8,128)(2,1)}, bf16[2048,256]{1,0:T(8,128)(2,1)}, bf16[2048,256]{1,0:T(8,128)(2,1)}, f32[8,128]{1,0:T(8,128)}, f32[3,24,768]{2,1,0:T(8,128)}, /*index=5*/f32[2,64,768]{2,1,0:T(8,128)}) custom-call(s32[1]{0:T(128)S(6)} %copy.83.refs_0_, bf16[2048,768]{1,0:T(8,128)(2,1)} %copy-done.9, bf16[2048,768]{1,0:T(8,128)(2,1)} %copy-done.9, ...), custom_call_target="tpu_custom_call" | custom-call | flops 8053063680 | bytes 8388608 | tf_op jit(solution)/shard_map/self_backward/pallas_call | solution.py:326
  308.7 11.6 %unproject.1 = (bf16[2048,768]{1,0:T(8,128)(2,1)}, bf16[768,768]{1,0:T(8,128)(2,1)}, f32[8,768]{1,0:T(8,128)S(1)}) custom-call(bf16[2048,768]{1,0:T(8,128)(2,1)} %bitcast.97, bf16[2048,768]{1,0:T(8,128)(2,1)} %copy-done.3, bf16[768,768]{1,0:T(8,128)(2,1)} %bitcast.99, bf16[2048,256]{1,0:T(8,128)(2,1)S(1)} %copy-done.4, bf16[2048,256]{1,0:T(8,128)(2,1)S(1)} %copy-done.5, ...), custom_call_target="tpu_custom_call" | custom-call | tf_op jit(solution)/shard_map/unproject/pallas_call | solution.py:410
  321.2 44.2 %reduce.16 = (f32[24,768]{1,0:T(8,128)}, f32[24,768]{1,0:T(8,128)}, f32[24,768]{1,0:T(8,128)}, f32[24,768]{1,0:T(8,128)}, f32[8,64,768]{2,1,0:T(8,128)}, /*index=5*/f32[8,128]{1,0:T(8,128)}, f32[8,128]{1,0:T(8,128)}) custom-call(bf16[2,2,4,2,24,768]{5,4,3,2,1,0:T(8,128)(2,1)} %bitcast.107, bf16[2,2,4,2,24,768]{5,4,3,2,1,0:T(8,128)(2,1)} %bitcast.123, ...), custom_call_target="tpu_custom_call" | custom-call | tf_op jit(solution)/shard_map/reduce/pallas_call | solution.py:1030
  366.6 1.8 fusion.7
  371.2 3.0 fusion.5
  (175 shorter events, 28.4 us)
Async XLA Ops:
  7.2 4.5 %copy-start.29 = (f32[24,768]{1,0:T(8,128)S(1)}, f32[24,768]{1,0:T(8,128)}, u32[]{:S(2)}) copy-start(f32[24,768]{1,0:T(8,128)} %param.24) | copy-start | bytes 221188
  7.2 4.5 %copy-start.30 = (f32[24,768]{1,0:T(8,128)S(1)}, f32[24,768]{1,0:T(8,128)}, u32[]{:S(2)}) copy-start(f32[24,768]{1,0:T(8,128)} %param.25) | copy-start | bytes 221188
  7.2 4.5 %copy-start.31 = (f32[24,768]{1,0:T(8,128)S(1)}, f32[24,768]{1,0:T(8,128)}, u32[]{:S(2)}) copy-start(f32[24,768]{1,0:T(8,128)} %param.23) | copy-start | bytes 221188
  7.2 4.5 %copy-start.44 = (f32[3,24]{1,0:T(4,128)S(1)}, f32[3,24]{1,0:T(4,128)}, u32[]{:S(2)}) copy-start(f32[3,24]{1,0:T(4,128)} %param.22) | copy-start | bytes 868
  7.2 5.6 %copy-start = (bf16[1,512,768]{2,1,0:T(8,128)(2,1)S(1)}, bf16[1,512,768]{2,1,0:T(8,128)(2,1)}, u32[]{:S(2)}) copy-start(bf16[1,512,768]{2,1,0:T(8,128)(2,1)} %param.18) | copy-start | bytes 2359300
  7.2 5.6 %copy-start.7 = (bf16[1,128,768]{2,1,0:T(8,128)(2,1)S(1)}, bf16[1,128,768]{2,1,0:T(8,128)(2,1)}, u32[]{:S(2)}) copy-start(bf16[1,128,768]{2,1,0:T(8,128)(2,1)} %param.19) | copy-start | bytes 589828
  7.2 133.6 %all-gather.5.cloned.1.call-start = ((), (), s32[]{:S(2)}) async-start(), calls=%async_computation.4 | async-start | bytes 3244032 | tf_op jit(solution)/shard_map/all_gather | solution.py:1089
  9.0 153.7 %all-gather.3.cloned.1.call-start = ((), (), s32[]{:S(2)}) async-start(), calls=%async_computation.3 | async-start | bytes 6488064 | tf_op jit(solution)/shard_map/all_gather | solution.py:1088
  45.0 3.9 %copy-start.1 = (bf16[2,2,512,768]{3,2,1,0:T(8,128)(2,1)}, bf16[2,2,512,768]{3,2,1,0:T(8,128)(2,1)S(1)}, u32[]{:S(2)}) copy-start(bf16[2,2,512,768]{3,2,1,0:T(8,128)(2,1)S(1)} %get-tuple-element.53) | copy-start | bytes 9437188
  45.0 3.9 %copy-start.2 = (bf16[2,2,4,2,24,768]{5,4,3,2,1,0:T(8,128)(2,1)}, bf16[2,2,4,2,24,768]{5,4,3,2,1,0:T(8,128)(2,1)S(1)}, u32[]{:S(2)}) copy-start(bf16[2,2,4,2,24,768]{5,4,3,2,1,0:T(8,128)(2,1)S(1)} %get-tuple-element.54) | copy-start | bytes 3538948
  45.1 70.2 %copy-start.10 = (bf16[2,2,128,768]{3,2,1,0:T(8,128)(2,1)}, bf16[2,2,128,768]{3,2,1,0:T(8,128)(2,1)S(1)}, u32[]{:S(2)}) copy-start(bf16[2,2,128,768]{3,2,1,0:T(8,128)(2,1)S(1)} %get-tuple-element.59) | copy-start | bytes 2359300
  45.1 7.3 %copy-start.42 = (f32[32,3]{0,1:T(4,128)S(1)}, f32[32,3]{0,1:T(4,128)}, u32[]{:S(2)}) copy-start(f32[32,3]{0,1:T(4,128)} %param.34) | copy-start | bytes 1156
  45.1 7.5 %copy-start.45 = (s32[15]{0:T(128)S(1)}, s32[15]{0:T(128)}, u32[]{:S(2)}) copy-start(s32[15]{0:T(128)} %constant.33.clone) | copy-start | bytes 184
  45.1 8.4 %copy-start.32 = (f32[24,768]{1,0:T(8,128)S(1)}, f32[24,768]{1,0:T(8,128)}, u32[]{:S(2)}) copy-start(f32[24,768]{1,0:T(8,128)} %param.26) | copy-start | bytes 221188
  45.1 8.4 %copy-start.33 = (f32[24,768]{1,0:T(8,128)S(1)}, f32[24,768]{1,0:T(8,128)}, u32[]{:S(2)}) copy-start(f32[24,768]{1,0:T(8,128)} %param.27) | copy-start | bytes 221188
  45.1 8.4 %copy-start.34 = (f32[24,768]{1,0:T(8,128)S(1)}, f32[24,768]{1,0:T(8,128)}, u32[]{:S(2)}) copy-start(f32[24,768]{1,0:T(8,128)} %param.28) | copy-start | bytes 221188
  45.1 8.4 %copy-start.35 = (f32[24,768]{1,0:T(8,128)S(1)}, f32[24,768]{1,0:T(8,128)}, u32[]{:S(2)}) copy-start(f32[24,768]{1,0:T(8,128)} %param.29) | copy-start | bytes 221188
  45.1 8.4 %copy-start.36 = (f32[24,768]{1,0:T(8,128)S(1)}, f32[24,768]{1,0:T(8,128)}, u32[]{:S(2)}) copy-start(f32[24,768]{1,0:T(8,128)} %param.30) | copy-start | bytes 221188
  52.4 55.8 %copy-start.8 = (f32[8,768]{1,0:T(8,128)}, f32[8,768]{1,0:T(8,128)S(1)}, u32[]{:S(2)}) copy-start(f32[8,768]{1,0:T(8,128)S(1)} %get-tuple-element.58.gains_ref) | copy-start | bytes 73732
  104.6 18.2 %all-to-all-start = ((bf16[4,512,192]{1,2,0:T(8,128)(2,1)}), bf16[4,512,192]{1,2,0:T(8,128)(2,1)S(1)}, u32[]{:S(2)}, u32[]{:S(2)}) async-start(bf16[4,512,192]{1,2,0:T(8,128)(2,1)} %copy.63), calls=%async_computation | async-start | bytes 1572864 | tf_op jit(solution)/shard_map/all_to_all | solution.py:1119
  108.1 266.1 %reduce-scatter.2.cloned.1.call-start = ((), (), s32[]{:S(2)}) async-start(), calls=%async_computation.5 | async-start | bytes 10137600 | tf_op jit(solution)/shard_map/reduce_scatter | solution.py:1160
  122.8 3.7 copy-start.25
  190.2 26.8 %copy-start.15 = (f32[512,768]{1,0:T(8,128)S(1)}, f32[512,768]{1,0:T(8,128)}, u32[]{:S(2)}) copy-start(f32[512,768]{1,0:T(8,128)} %copy-done.14) | copy-start | bytes 4718596
  190.2 26.8 %copy-start.26 = (bf16[1,2,2,4,2,24,768]{6,5,4,3,2,1,0:T(8,128)(2,1)S(1)}, bf16[1,2,2,4,2,24,768]{6,5,4,3,2,1,0:T(8,128)(2,1)}, u32[]{:S(2)}) copy-start(bf16[1,2,2,4,2,24,768]{6,5,4,3,2,1,0:T(8,128)(2,1)} %get-tuple-element.97) | copy-start | bytes 3538948
  222.3 7.6 %copy-start.11 = (bf16[2,2,128,768]{3,2,1,0:T(8,128)(2,1)S(1)}, bf16[2,2,128,768]{3,2,1,0:T(8,128)(2,1)}, u32[]{:S(2)}) copy-start(bf16[2,2,128,768]{3,2,1,0:T(8,128)(2,1)} %copy-done.10) | copy-start | bytes 2359300
  224.7 16.7 %all-to-all-start.1 = ((bf16[512,4,192]{0,2,1:T(8,128)(2,1)}), bf16[512,4,192]{0,2,1:T(8,128)(2,1)}, u32[]{:S(2)}, u32[]{:S(2)}) async-start(bf16[512,4,192]{0,2,1:T(8,128)(2,1)} %bitcast.112), calls=%async_computation.1 | async-start | bytes 1572864 | tf_op jit(solution)/shard_map/all_to_all | solution.py:1178
  229.9 3.1 copy-start.23
  229.9 3.1 copy-start.48
  365.5 5.1 %copy-start.28 = (f32[3,24,768]{2,1,0:T(8,128)S(1)}, f32[3,24,768]{2,1,0:T(8,128)}, u32[]{:S(2)}) copy-start(f32[3,24,768]{2,1,0:T(8,128)} %get-tuple-element.86) | copy-start | bytes 663556
  375.2 3.7 copy-start.39
  375.4 4.2 %copy-start.38 = (f32[24,768]{1,0:T(8,128)S(1)}, f32[24,768]{1,0:T(8,128)}, u32[]{:S(2)}) copy-start(f32[24,768]{1,0:T(8,128)} %get-tuple-element.148) | copy-start | bytes 221188
  375.4 4.8 %copy-start.37 = (f32[1,24,768]{2,1,0:T(8,128)S(1)}, f32[1,24,768]{2,1,0:T(8,128)}, u32[]{:S(2)}) copy-start(f32[1,24,768]{2,1,0:T(8,128)} %get-tuple-element.87) | copy-start | bytes 221188
  (22 other events, 40.8 us)
Sparse Core Ops, SparseCore 0:
  11.5 74.5 all-gather.4
  89.6 73.0 all-gather.2
  189.9 147.2 reduce-scatter.1

commit v5 on v4

--- a/solution.py
+++ b/solution.py
@@ -195,7 +195,7 @@
             jax.ShapeDtypeStruct((heads, 8, rows), jnp.float32),
         ] + (plan.out_shape() if plan else []),
         scratch_shapes=scratch + (plan.scratch() if plan else []),
-        compiler_params=plan.params() if plan else pltpu.CompilerParams(vmem_limit_bytes=60 * 2**20),
+        compiler_params=plan.params() if plan else pltpu.CompilerParams(vmem_limit_bytes=62 * 2**20),
         cost_estimate=pl.CostEstimate(
             flops=4 * heads * LANES * rows * count // (2 if causal else 1),
             bytes_accessed=4 * (rows + count) * width,
@@ -330,7 +330,7 @@
         out_specs=out_specs + (plan.out_specs() if plan else []),
         out_shape=out_shape + (plan.out_shape() if plan else []),
         scratch_shapes=scratch + (plan.scratch() if plan else []),
-        compiler_params=plan.params() if plan else pltpu.CompilerParams(vmem_limit_bytes=60 * 2**20),
+        compiler_params=plan.params() if plan else pltpu.CompilerParams(vmem_limit_bytes=62 * 2**20),
         cost_estimate=pl.CostEstimate(
             flops=10 * heads * LANES * rows * count // (2 if causal else 1),
             bytes_accessed=8 * (rows + count) * width,
@@ -372,7 +372,7 @@
             jax.ShapeDtypeStruct((count, wide), low), jax.ShapeDtypeStruct((count, width), low),
             jax.ShapeDtypeStruct((8, width), jnp.float32),
         ],
-        compiler_params=pltpu.CompilerParams(vmem_limit_bytes=40 * 2**20),
+        compiler_params=pltpu.CompilerParams(vmem_limit_bytes=62 * 2**20),
         name="project",
     )(everyone, w_qkv)
 
@@ -417,7 +417,7 @@
             jax.ShapeDtypeStruct((8, width), jnp.float32),
         ],
         scratch_shapes=[pltpu.VMEM((width, wide), jnp.float32)],
-        compiler_params=pltpu.CompilerParams(vmem_limit_bytes=50 * 2**20),
+        compiler_params=pltpu.CompilerParams(vmem_limit_bytes=62 * 2**20),
         name="unproject",
     )(everyone, normed, w_qkv, dq, dk, dv)
 
@@ -427,10 +427,11 @@
 
 
 def middle_kernel(
-    slabs, scalars, x1_ref, mixed_ref, co_ref, gains_ref, cot_ref, gate_ref, up_ref, down_ref,
-    out_ref, dx_ref, dm_ref, co_grad_ref, gain_ref, packed,
-    x2_scr, n3_scr, n3t_scr, df_scr, result_scr, dn_scr, gate_buf, up_buf, down_buf, sem,
+    slabs, scalars, x1_ref, mixed_ref, co_ref, gains_ref, cot_ref, gate_ref, up_ref, *refs
 ):
+    slab_refs, refs = refs[:slabs], refs[slabs:]
+    out_ref, dx_ref, dm_ref, co_grad_ref, gain_ref, packed = refs[:6]
+    x2_scr, n3_scr, n3t_scr, df_scr, result_scr, dn_scr, down_ref, gate_buf, up_buf, down_buf, sem = refs[6:]
     step, steps = pl.program_id(0), pl.num_programs(0)
     rows, width = x1_ref.shape
     block = gate_ref.shape[1]
@@ -451,6 +452,12 @@
         result_scr[...] = x2
         dn_scr[...] = jnp.zeros_like(dn_scr)
         down_buf[...] = jnp.zeros_like(down_buf)
+
+    for o in range(owners):
+        for k in range(slabs):
+            size = min(share, hidden_share - k * share)
+            start = o * hidden_share + k * share
+            down_ref[start : start + size] = slab_refs[k][o, :size]
 
     normed, df = n3_scr[...], df_scr[...]
     gate, upper = nn(normed, gate_ref[...]), nn(normed, up_ref[...])
@@ -514,14 +521,14 @@
             copy.wait()
 
 
-def middle(scalars, x1, mixed, c_output, gains, cotangent, gate_up, w_down, world):
+def middle(scalars, x1, mixed, gains, cotangent, weights, inner, world):
     rows, width = x1.shape
-    inner = w_down.shape[0]
     block = min(BLOCK, inner)
     steps = inner // block
     share, hidden_share = width // world, inner // world
     slabs = -(-hidden_share // share)
     owners = block // hidden_share
+    ahead = (1 + slabs) * width // block
     fixed = lambda *shape: pl.BlockSpec(shape, lambda j: (0,) * len(shape))
     f32 = jnp.float32
     return pl.pallas_call(
@@ -530,8 +537,8 @@
         in_specs=[
             pl.BlockSpec(memory_space=pltpu.SMEM), fixed(rows, width), fixed(rows, width), fixed(width, width),
             fixed(8, width), fixed(rows, width),
-            pl.BlockSpec((width, block), lambda j: (0, j)), pl.BlockSpec((width, block), lambda j: (0, steps + j)),
-            pl.BlockSpec((block, width), lambda j: (j, 0)),
+            pl.BlockSpec((width, block), lambda j: (0, ahead + j)), pl.BlockSpec((width, block), lambda j: (0, ahead + steps + j)),
+            *[pl.BlockSpec((owners, share, width), lambda j, k=k: (j, 0, 1 + k)) for k in range(slabs)],
         ],
         out_specs=[
             fixed(rows, width), fixed(rows, width), fixed(rows, width), fixed(width, width), fixed(8, width),
@@ -546,6 +553,7 @@
         scratch_shapes=[
             pltpu.VMEM((rows, width), f32), pltpu.VMEM((rows, width), low), pltpu.VMEM((width, rows), low),
             pltpu.VMEM((rows, width), low), pltpu.VMEM((rows, width), f32), pltpu.VMEM((rows, width), f32),
+            pltpu.VMEM((block, width), low),
             pltpu.VMEM((2, world, share, block), low), pltpu.VMEM((2, world, share, block), low),
             pltpu.VMEM((2, owners, slabs, share, width), low), pltpu.SemaphoreType.DMA((2, 2 + slabs)),
         ],
@@ -554,7 +562,147 @@
             flops=2 * rows * width * (9 * inner + 3 * width), transcendentals=rows * inner, bytes_accessed=26 * width * inner // 4
         ),
         name="middle",
-    )(scalars, x1, mixed, c_output, gains, cotangent, gate_up, gate_up, w_down)
+    )(scalars, x1, mixed, weights, gains, cotangent, weights, weights, *[weights.reshape(world, share, -1)] * slabs)
+
+
+def encode_kernel(enc_ref, w_ref, key_ref, value_ref):
+    for n, out in enumerate((key_ref, value_ref)):
+        out[...] = nn(enc_ref[...], w_ref[n]).astype(low)
+
+
+def encode(encoded, squares):
+    count, width = encoded.shape
+    part = width // 3
+    columns = pl.BlockSpec((count, part), lambda j: (0, j))
+    return pl.pallas_call(
+        encode_kernel,
+        grid=(3,),
+        in_specs=[pl.BlockSpec((count, width), lambda j: (0, 0)), pl.BlockSpec((2, width, part), lambda j: (1, 0, j))],
+        out_specs=[columns] * 2,
+        out_shape=[jax.ShapeDtypeStruct((count, width), low)] * 2,
+        compiler_params=pltpu.CompilerParams(vmem_limit_bytes=62 * 2**20),
+        cost_estimate=pl.CostEstimate(flops=4 * count * width * width, transcendentals=0, bytes_accessed=8 * width * width),
+        name="encode",
+    )(encoded, squares)
+
+
+def enter_kernel(group_width, x_ref, mixed_ref, w_ref, gains_ref, attended_ref, normed_ref, query_ref):
+    total = x_ref[...].astype(jnp.float32)
+    for s in range(mixed_ref.shape[0]):
+        total += nn(mixed_ref[s, :, :group_width], w_ref[0, s * group_width : (s + 1) * group_width])
+    attended_ref[...] = total
+    normed = (total * scale_of(total) * gains_ref[1:2, :]).astype(low)
+    normed_ref[...] = normed
+    query_ref[...] = nn(normed, w_ref[1]).astype(low)
+
+
+def enter(tokens, mixed, squares, gains, group_width):
+    rows, width = tokens.shape
+    seq, _, padded = mixed.shape
+    block = min(256, rows)
+    by_rows = pl.BlockSpec((block, width), lambda i: (i, 0))
+    return pl.pallas_call(
+        functools.partial(enter_kernel, group_width),
+        grid=(rows // block,),
+        in_specs=[
+            by_rows, pl.BlockSpec((seq, block, padded), lambda i: (0, i, 0)), pl.BlockSpec((2, width, width), lambda i: (0, 0, 0)),
+            pl.BlockSpec((8, width), lambda i: (0, 0)),
+        ],
+        out_specs=[by_rows] * 3,
+        out_shape=[jax.ShapeDtypeStruct((rows, width), t) for t in (jnp.float32, low, low)],
+        compiler_params=pltpu.CompilerParams(vmem_limit_bytes=62 * 2**20),
+        cost_estimate=pl.CostEstimate(flops=4 * rows * width * width, transcendentals=0, bytes_accessed=12 * width * width),
+        name="enter",
+    )(tokens, mixed, squares, gains)
+
+
+def leave_kernel(group_width, grad_ref, w_ref, attended_ref, gains_ref, dx_ref, total_ref, branch_ref, dm_ref, gain_ref):
+    @pl.when(pl.program_id(0) == 0)
+    def _():
+        gain_ref[...] = jnp.zeros_like(gain_ref)
+
+    grad_normed = nt(grad_ref[...], w_ref[1])
+    values = attended_ref[...]
+    scale = scale_of(values)
+    unit = values * scale
+    grad_unit = grad_normed * gains_ref[1:2, :]
+    gain_ref[...] += jnp.broadcast_to(jnp.sum(grad_normed * unit, axis=0, keepdims=True), gain_ref.shape)
+    total = dx_ref[...] + scale * (grad_unit - unit * jnp.mean(grad_unit * unit, axis=-1, keepdims=True))
+    total_ref[...] = total
+    branch = total.astype(low)
+    branch_ref[...] = branch
+    for s in range(dm_ref.shape[0]):
+        dm_ref[s, :, :group_width] = nt(branch, w_ref[0, s * group_width : (s + 1) * group_width]).astype(low)
+        if dm_ref.shape[2] > group_width:
+            dm_ref[s, :, group_width:] = jnp.zeros((branch.shape[0], dm_ref.shape[2] - group_width), low)
+
+
+def leave(grad_queries, squares, attended, gains, grad_crossed, seq, group_width, padded):
+    rows, width = grad_queries.shape
+    block = min(256, rows)
+    by_rows = pl.BlockSpec((block, width), lambda i: (i, 0))
+    fixed = pl.BlockSpec((8, width), lambda i: (0, 0))
+    return pl.pallas_call(
+        functools.partial(leave_kernel, group_width),
+        grid=(rows // block,),
+        in_specs=[by_rows, pl.BlockSpec((2, width, width), lambda i: (0, 0, 0)), by_rows, fixed, by_rows],
+        out_specs=[by_rows, by_rows, pl.BlockSpec((seq, block, padded), lambda i: (0, i, 0)), fixed],
+        out_shape=[
+            jax.ShapeDtypeStruct((rows, width), jnp.float32), jax.ShapeDtypeStruct((rows, width), low),
+            jax.ShapeDtypeStruct((seq, rows, padded), low), jax.ShapeDtypeStruct((8, width), jnp.float32),
+        ],
+        compiler_params=pltpu.CompilerParams(vmem_limit_bytes=62 * 2**20),
+        cost_estimate=pl.CostEstimate(flops=4 * rows * width * width, transcendentals=0, bytes_accessed=16 * width * width),
+        name="leave",
+    )(grad_queries, squares, attended, gains, grad_crossed)
+
+
+def square_terms_kernel(group_width, normed, grad_q, encoded, grad_k, grad_v, w_ref, mixed, branch, q_out, k_out, v_out, o_out, e_out, *scratch):
+    normed_t, encoded_t, mixed_t, total = scratch
+    step = pl.program_id(0)
+
+    @pl.when(step == 0)
+    def _():
+        normed_t[...] = normed[...].T
+        encoded_t[...] = encoded[...].T
+        for s in range(mixed.shape[0]):
+            mixed_t[s * group_width : (s + 1) * group_width] = mixed[s].T[:group_width]
+        total[...] = jnp.zeros_like(total)
+
+    q_out[...] = nn(normed_t[...], grad_q[...]).astype(low)
+    k_out[...] = nn(encoded_t[...], grad_k[...]).astype(low)
+    v_out[...] = nn(encoded_t[...], grad_v[...]).astype(low)
+    o_out[...] = nn(mixed_t[...], branch[...]).astype(low)
+    total[...] += nt(grad_k[...], w_ref[0]) + nt(grad_v[...], w_ref[1])
+
+    @pl.when(step == pl.num_programs(0) - 1)
+    def _():
+        e_out[...] = total[...].astype(low)
+
+
+def square_terms(normed, grad_q, encoded, grad_k, grad_v, squares, mixed, branch, group_width):
+    rows, width = normed.shape
+    count = encoded.shape[0]
+    part = width // 3
+    fixed = lambda v: pl.BlockSpec(v.shape, lambda j: (0,) * v.ndim)
+    columns = lambda n: pl.BlockSpec((n, part), lambda j: (0, j))
+    return pl.pallas_call(
+        functools.partial(square_terms_kernel, group_width),
+        grid=(3,),
+        in_specs=[
+            fixed(normed), columns(rows), fixed(encoded), columns(count), columns(count),
+            pl.BlockSpec((2, width, part), lambda j: (1, 0, j)), fixed(mixed), columns(rows),
+        ],
+        out_specs=[columns(width)] * 4 + [fixed(encoded)],
+        out_shape=[jax.ShapeDtypeStruct((width, width), low)] * 4 + [jax.ShapeDtypeStruct((count, width), low)],
+        scratch_shapes=[
+            pltpu.VMEM((width, rows), low), pltpu.VMEM((width, count), low), pltpu.VMEM((width, rows), low),
+            pltpu.VMEM((count, width), jnp.float32),
+        ],
+        compiler_params=pltpu.CompilerParams(vmem_limit_bytes=62 * 2**20),
+        cost_estimate=pl.CostEstimate(flops=12 * rows * width * width, transcendentals=0, bytes_accessed=24 * width * width),
+        name="square_terms",
+    )(normed, grad_q, encoded, grad_k, grad_v, squares, mixed, branch)
 
 
 def coordinates():
@@ -650,7 +798,7 @@
         return [pltpu.SemaphoreType.DMA((self.total,)), pltpu.SemaphoreType.DMA((self.total,)), pltpu.SemaphoreType.DMA((1,))]
 
     def params(self):
-        return pltpu.CompilerParams(collective_id=2, has_side_effects=True, vmem_limit_bytes=60 * 2**20)
+        return pltpu.CompilerParams(collective_id=2, has_side_effects=True, vmem_limit_bytes=62 * 2**20)
 
     def stages(self, given, made, scratch):
         (src,), (out,), (send_sem, recv_sem, local_sem) = given, made, scratch
@@ -737,7 +885,7 @@
         return [vmem(2, 2, nz), vmem(2, nz, 2), vmem(2, nz), vmem(2, nz), vmem(nz), vmem(nz), vmem(nz - 1), *slabs, *sems]
 
     def params(self):
-        return pltpu.CompilerParams(collective_id=self.number, has_side_effects=True, vmem_limit_bytes=60 * 2**20)
+        return pltpu.CompilerParams(collective_id=self.number, has_side_effects=True, vmem_limit_bytes=62 * 2**20)
 
     def stages(self, given, made, scratch):
         squares, out, beside = given[: self.count], made[0], self.slabs is not None
@@ -879,7 +1027,7 @@
         scratch_shapes=[
             pltpu.SemaphoreType.DMA((total,)), pltpu.SemaphoreType.DMA((total,)), pltpu.SemaphoreType.DMA((3,)),
         ],
-        compiler_params=pltpu.CompilerParams(collective_id=0, has_side_effects=True, vmem_limit_bytes=8 * 2**20),
+        compiler_params=pltpu.CompilerParams(collective_id=0, has_side_effects=True, vmem_limit_bytes=62 * 2**20),
         name="gather",
     )(tok, enc, own)
 
@@ -1042,7 +1190,7 @@
             pltpu.SemaphoreType.DMA((total,)), pltpu.SemaphoreType.DMA((total,)),
             pltpu.SemaphoreType.DMA((world - 1,)), pltpu.SemaphoreType.DMA((world - 1,)),
         ],
-        compiler_params=pltpu.CompilerParams(collective_id=1, has_side_effects=True, vmem_limit_bytes=60 * 2**20),
+        compiler_params=pltpu.CompilerParams(collective_id=1, has_side_effects=True, vmem_limit_bytes=62 * 2**20),
         name="reduce",
     )(square, own, tok, gain, near)
 
@@ -1085,9 +1233,16 @@
     place = lax.axis_index("seq")
     aligned = share % 8 == 0
 
-    gate_up = lax.all_gather(jnp.concatenate([ffn_gate.astype(low), ffn_up.astype(low)], axis=1), both, axis=0, tiled=True)
-    w_down = lax.all_gather(ffn_down.astype(low), both, axis=0, tiled=True)
-    squares = jnp.stack([w.astype(low) for w in (self_output, cross_query, cross_key, cross_value, cross_output)])
+    slabs = -(-hidden_share // share)
+    squares = jnp.stack([w.astype(low) for w in (self_output, cross_query, cross_key, cross_value)])
+    if aligned:
+        down = jnp.pad(ffn_down.astype(low), ((0, slabs * share - hidden_share), (0, 0))).reshape(slabs, share, width)
+        wide_share = [cross_output.astype(low), *[down[k] for k in range(slabs)], ffn_gate.astype(low), ffn_up.astype(low)]
+        wide_weights = lax.all_gather(jnp.concatenate(wide_share, axis=1), both, axis=0, tiled=True)
+    else:
+        gate_up = lax.all_gather(jnp.concatenate([ffn_gate.astype(low), ffn_up.astype(low)], axis=1), both, axis=0, tiled=True)
+        w_down = lax.all_gather(ffn_down.astype(low), both, axis=0, tiled=True)
+        c_output = lax.all_gather(cross_output.astype(low), both, axis=0, tiled=True)
     gain_columns = jnp.pad(gains.astype(low).T, ((0, 0), (0, spare - 3)))
     pieces = []
     for s in range(seq):
@@ -1109,25 +1264,20 @@
     values_in = tokens[0].astype(jnp.float32)
     qkv, normed_all, gain_rows = project(everyone, w_qkv, group_width)
     bias = bias_rows(rel_bias)
-    plan = GatherPlan(nz, 5, share, width) if aligned else None
+    plan = GatherPlan(nz, 4, share, width) if aligned else None
     own_mixed, own_logsum, *gathered = attend_forward(
         qkv, qkv, qkv, group, padded, bias, lengths, plan, (squares,) if aligned else ()
     )
     squares = gathered[0] if aligned else jnp.moveaxis(lax.all_gather(squares, both, axis=0), 1, 0)
-    squares = squares.reshape(5, width, width)
-    w_output, c_query, c_key, c_value, c_output = (squares[n] for n in range(5))
-    mixed = lax.all_to_all(own_mixed[:, :group_width], "seq", split_axis=0, concat_axis=1, tiled=True)
-    attended = values_in + nn(mixed, w_output)
-    normed_two = rms_norm(attended, gain_rows[1]).astype(low)
-    cross_queries = nn(normed_two, c_query).astype(low)
-    cross_keys = nn(encoded, c_key).astype(low)
-    cross_values = nn(encoded, c_value).astype(low)
+    squares = squares.reshape(4, width, width)
+    mixed = lax.all_to_all(own_mixed.reshape(seq, rows, padded), "seq", split_axis=0, concat_axis=0, tiled=True)
+    cross_keys, cross_values = encode(encoded, squares)
+    attended, normed_two, cross_queries = enter(tokens[0], mixed, squares, gain_rows, group_width)
     cross_mixed, cross_logsum = attend_forward(cross_queries, cross_keys, cross_values, heads)
-    slabs = -(-hidden_share // share)
     if aligned:
         scalars = jnp.stack([length, place * rows])
         result, grad_crossed, grad_cmixed, grad_coutput, gain_two, packed = middle(
-            scalars, attended, cross_mixed, c_output, gain_rows, cotangent[0], gate_up, w_down, world
+            scalars, attended, cross_mixed, gain_rows, cotangent[0], wide_weights, inner, world
         )
         grad_gain_two = gain_two[0]
         packed = packed.reshape(width, -1)
@@ -1166,17 +1316,14 @@
         cross_queries, cross_keys, cross_values, grad_cmixed, cross_mixed, cross_logsum, heads,
         plan=plan, extra=(chunked(grad_coutput),) if aligned else (),
     )
-    grad_cquery = tn(normed_two, grad_cq).astype(low)
-    grad_ckey = tn(encoded, grad_ck).astype(low)
-    grad_cvalue = tn(encoded, grad_cv).astype(low)
-    grad_encoded = (nt(grad_ck, c_key) + nt(grad_cv, c_value)).astype(low)
-    norm_part, grad_gain_one = rms_back(attended, gain_rows[1], nt(grad_cq, c_query))
-    grad_attended = grad_crossed + norm_part
-    grad_self_branch = grad_attended.astype(low)
-    grad_output = tn(mixed, grad_self_branch).astype(low)
-    grad_mixed = nt(grad_self_branch, w_output).astype(low)
-    own_grad_mixed = lax.all_to_all(grad_mixed, "seq", split_axis=1, concat_axis=0, tiled=True)
-    own_grad_mixed = jnp.pad(own_grad_mixed, ((0, 0), (0, padded - group_width)))
+    grad_attended, branch, grad_mixed, gain_one = leave(
+        grad_cq, squares, attended, gain_rows, grad_crossed, seq, group_width, padded
+    )
+    grad_gain_one = gain_one[0]
+    own_grad_mixed = lax.all_to_all(grad_mixed, "seq", split_axis=0, concat_axis=0, tiled=True).reshape(seq * rows, padded)
+    grad_cquery, grad_ckey, grad_cvalue, grad_output, grad_encoded = square_terms(
+        normed_two, grad_cq, encoded, grad_ck, grad_cv, squares, mixed, branch, group_width
+    )
     early = [grad_cquery, grad_ckey, grad_cvalue]
     plan, extra = None, ()
     if aligned:

time: 387 us -> 358 us (0.925)
  Pallas kernels: 267 us -> 292 us
  matrix products: 24 us -> 1.04 us
  waiting for transfers between devices: 27.9 us -> 10.8 us
  local copies, waits for them, and re-layouts: 33.4 us -> 17.8 us
    pallas_call x0 -> x4, Pallas kernels: none -> 26.1 us  [the longest x1 9.92 us: square_terms(): pl.pallas_call(functools.partial(square_terms_kernel, group_width), grid=...]
    dot_general x12 -> x0, matrix products: 22.9 us -> none  [the longest x4 8.73 us: tn(): lax.dot_general(left, right, (((0,), (0,)), ((), ())), preferred_element_...]
    all_gather x2 -> x1, waiting for transfers between devices: 22 us -> 0.01 us  [per_device(): lax.all_gather(jnp.concatenate(wide_share, axis=1), both, axis=0, tiled=T...]
    pallas_call x2, Pallas kernels: 87.5 us -> 67.4 us  [attend_backward(): pl.pallas_call(functools.partial(attend_backward_kernel, causal=causal, h...]
    pallas_call x2, Pallas kernels: 60.7 us -> 68.8 us  [attend_forward(): pl.pallas_call(functools.partial(attend_forward_kernel, causal=causal, he...]
    unnamed x104 -> x53, local copies, waits for them, and re-layouts: 14.2 us -> 7.78 us
    pallas_call x1, Pallas kernels: 32.2 us -> 37.9 us  [gather(): pl.pallas_call(functools.partial(gather_kernel, nz), in_specs=[whole()] *...]
    all_to_all x2, waiting for transfers between devices: 5.85 us -> 10.8 us  [the longest x1 8.85 us: per_device(): lax.all_to_all(own_mixed.reshape(seq, rows, padded), 'seq', split_axis=0,...]
  transfers between devices with their start and end apart: 5 -> 4, of which waited for: 2 -> 2; matrix products, arithmetic and copies ran while one was open for 13% -> 5% of each run, Pallas kernels for 62% -> 74%
where the time goes in v5:
time: 358 us; the launch traced here: 357 us
  Pallas kernels  292 us (82%)
  local copies, waits for them, and re-layouts  17.8 us (5%)
  between operations  15.2 us (4%)
  other arithmetic  12.2 us (3%)
  waiting for transfers between devices  10.8 us (3%)
  starting transfers between devices  7.6 us (2%)
    pallas_call x2, Pallas kernels, attend_forward(): pl.pallas_call(functools.partial(attend_forward_kernel, causal=causal, he...  68.8 us
    pallas_call x2, Pallas kernels, attend_backward(): pl.pallas_call(functools.partial(attend_backward_kernel, causal=causal, h...  67.4 us
    pallas_call x1, Pallas kernels, reduce(): pl.pallas_call(functools.partial(reduce_kernel, nz, group_width), in_spec...  44.6 us
    pallas_call x1, Pallas kernels, gather(): pl.pallas_call(functools.partial(gather_kernel, nz), in_specs=[whole()] *...  37.9 us
    pallas_call x1, Pallas kernels, middle(): pl.pallas_call(functools.partial(middle_kernel, slabs), grid=(steps,), in...  27.2 us
    pallas_call x1, Pallas kernels, unproject(): pl.pallas_call(unproject_kernel, grid=(count // block,), in_specs=[rows(w...  12.6 us
    pallas_call x1, Pallas kernels, square_terms(): pl.pallas_call(functools.partial(square_terms_kernel, group_width), grid=...  9.92 us
    all_to_all x1, waiting for transfers between devices, per_device(): lax.all_to_all(own_mixed.reshape(seq, rows, padded), 'seq', split_axis=0,...  8.85 us
  transfers between devices with their start and end apart: 4, of which 2 were waited for; matrix products, arithmetic and copies ran while one was open for 5% of the time, Pallas kernels for 74%

profile of v5, /device:TPU:0, one launch (start us, length us, event | category | flops | bytes accessed | tf_op | source)
XLA Modules:
  0.0 356.6 jit_solution(3022290903391749944)
XLA Ops:
  7.3 1.0 convert_element_type.71
  8.2 0.9 convert_dynamic-update-slice_fusion.2
  9.2 0.9 convert_dynamic-update-slice_fusion.1
  10.1 0.9 convert_dynamic-update-slice_fusion
  13.7 37.9 %gather.1 = (bf16[2,2,512,768]{3,2,1,0:T(8,128)(2,1)}, bf16[2,2,128,768]{3,2,1,0:T(8,128)(2,1)}, bf16[2,2,4,2,24,768]{5,4,3,2,1,0:T(8,128)(2,1)}) custom-call(bf16[512,768]{1,0:T(8,128)(2,1)} %bitcast.68, bf16[128,768]{1,0:T(8,128)(2,1)} %bitcast.90, bf16[2,2,24,768]{3,2,1,0:T(8,128)(2,1)} %bitcast.86), custom_call_target="tpu_custom_call" | custom-call | tf_op jit(solution)/shard_map/gather/pallas_call | solution.py:1022
  51.7 7.1 %project.1 = (bf16[2048,768]{1,0:T(8,128)(2,1)}, bf16[2048,768]{1,0:T(8,128)(2,1)}, f32[8,768]{1,0:T(8,128)}) custom-call(bf16[2048,768]{1,0:T(8,128)(2,1)} %bitcast.71, bf16[768,768]{1,0:T(8,128)(2,1)} %bitcast.74), custom_call_target="tpu_custom_call" | custom-call | tf_op jit(solution)/shard_map/project/pallas_call | solution.py:366
  60.6 56.5 %self_forward.1 = (bf16[2048,256]{1,0:T(8,128)(2,1)}, f32[3,8,2048]{2,1,0:T(8,128)}, bf16[4,2,2,4,2,24,768]{6,5,4,3,2,1,0:T(8,128)(2,1)}) custom-call(s32[1]{0:T(128)S(6)} %copy.73.refs_0_, bf16[2048,768]{1,0:T(8,128)(2,1)} %get-tuple-element.69.refs_1_.refs_2_.refs_3_, bf16[2048,768]{1,0:T(8,128)(2,1)} %get-tuple-element.69.refs_1_.refs_2_.refs_3_, ...), custom_call_target="tpu_custom_call" | custom-call | flops 3221225472 | bytes 4194304 | tf_op jit(solution)/shard_map/self_forward/pallas_call | solution.py:188
  117.2 3.6 %all-to-all-start = ((bf16[4,512,256]{2,1,0:T(8,128)(2,1)}), bf16[4,512,256]{2,1,0:T(8,128)(2,1)S(1)}, u32[]{:S(2)}, u32[]{:S(2)}) async-start(bf16[4,512,256]{2,1,0:T(8,128)(2,1)} %bitcast.80), calls=%async_computation | async-start | bytes 2097152 | tf_op jit(solution)/shard_map/all_to_all | solution.py:1273
  121.6 4.7 %encode.1 = (bf16[512,768]{1,0:T(8,128)(2,1)}, bf16[512,768]{1,0:T(8,128)(2,1)}) custom-call(bf16[512,768]{1,0:T(8,128)(2,1)} %bitcast.84, bf16[4,768,768]{2,1,0:T(8,128)(2,1)} %bitcast.64), custom_call_target="tpu_custom_call" | custom-call | flops 1207959552 | bytes 4718592 | tf_op jit(solution)/shard_map/encode/pallas_call | solution.py:577
  126.3 8.8 %all-to-all-done.mixed_ref.mixed = bf16[4,512,256]{2,1,0:T(8,128)(2,1)S(1)} async-done(((bf16[4,512,256]{2,1,0:T(8,128)(2,1)}), bf16[4,512,256]{2,1,0:T(8,128)(2,1)S(1)}, u32[]{:S(2)}, u32[]{:S(2)}) %all-to-all-start) | async-done | bytes 1048608 | tf_op jit(solution)/shard_map/all_to_all | solution.py:1273
  135.2 1.0 copy-done.1
  136.2 5.3 %enter.1 = (f32[512,768]{1,0:T(8,128)}, bf16[512,768]{1,0:T(8,128)(2,1)}, bf16[512,768]{1,0:T(8,128)(2,1)}) custom-call(bf16[512,768]{1,0:T(8,128)(2,1)} %bitcast.69, bf16[4,512,256]{2,1,0:T(8,128)(2,1)} %copy-done.1, bf16[4,768,768]{2,1,0:T(8,128)(2,1)} %bitcast.65, f32[8,768]{1,0:T(8,128)} %get-tuple-element.72.gains_ref), custom_call_target="tpu_custom_call" | custom-call | flops 1207959552 | bytes 7077888 | tf_op jit(solution)/shard_map/enter/pallas_call | solution.py:604
  141.4 12.3 %cross_forward.1 = (bf16[512,768]{1,0:T(8,128)(2,1)}, f32[12,8,512]{2,1,0:T(8,128)}) custom-call(bf16[512,768]{1,0:T(8,128)(2,1)} %get-tuple-element.74.refs_0_, bf16[512,768]{1,0:T(8,128)(2,1)} %get-tuple-element.76.refs_1_, bf16[512,768]{1,0:T(8,128)(2,1)} %get-tuple-element.77.refs_2_), custom_call_target="tpu_custom_call" | custom-call | flops 1610612736 | bytes 3145728 | tf_op jit(solution)/shard_map/cross_forward/pallas_call | solution.py:188
  153.7 27.2 %middle.1 = (bf16[512,768]{1,0:T(8,128)(2,1)}, f32[512,768]{1,0:T(8,128)}, bf16[512,768]{1,0:T(8,128)(2,1)}, bf16[768,768]{1,0:T(8,128)(2,1)}, f32[8,768]{1,0:T(8,128)}, /*index=5*/bf16[32,24,6400]{2,1,0:T(8,128)(2,1)}) custom-call(s32[2]{0:T(128)} %pad_add_fusion.scalars, f32[512,768]{1,0:T(8,128)} %get-tuple-element.73.x1_ref.attended_ref, ...), custom_call_target="tpu_custom_call" | custom-call | flops 16307453952 | bytes 10223616 | tf_op jit(solution)/shard_map/middle/pallas_call | solution.py:534
  181.0 1.1 copy-done
  182.4 26.6 %cross_backward.1 = (bf16[512,768]{1,0:T(8,128)(2,1)}, bf16[512,768]{1,0:T(8,128)(2,1)}, bf16[512,768]{1,0:T(8,128)(2,1)}, f32[1,24,768]{2,1,0:T(8,128)}) custom-call(bf16[512,768]{1,0:T(8,128)(2,1)} %get-tuple-element.74.refs_0_, bf16[512,768]{1,0:T(8,128)(2,1)} %get-tuple-element.76.refs_1_, bf16[512,768]{1,0:T(8,128)(2,1)} %get-tuple-element.77.refs_2_, ...), custom_call_target="tpu_custom_call" | custom-call | flops 4026531840 | bytes 6291456 | tf_op jit(solution)/shard_map/cross_backward/pallas_call | solution.py:326
  209.0 6.2 %leave.1 = (f32[512,768]{1,0:T(8,128)}, bf16[512,768]{1,0:T(8,128)(2,1)}, bf16[4,512,256]{2,1,0:T(8,128)(2,1)}, f32[8,768]{1,0:T(8,128)}) custom-call(bf16[512,768]{1,0:T(8,128)(2,1)} %get-tuple-element.83.grad_ref.grad_q, bf16[4,768,768]{2,1,0:T(8,128)(2,1)} %bitcast.66, f32[512,768]{1,0:T(8,128)} %get-tuple-element.73.x1_ref.attended_ref, ...), custom_call_target="tpu_custom_call" | custom-call | flops 1207959552 | bytes 9437184 | tf_op jit(solution)/shard_map/leave/pallas_call | solution.py:645
  215.3 3.7 %all-to-all-start.1 = ((bf16[4,512,256]{2,1,0:T(8,128)(2,1)}), bf16[4,512,256]{2,1,0:T(8,128)(2,1)S(1)}, u32[]{:S(2)}, u32[]{:S(2)}) async-start(bf16[4,512,256]{2,1,0:T(8,128)(2,1)} %get-tuple-element.92), calls=%async_computation.1 | async-start | bytes 2097152 | tf_op jit(solution)/shard_map/all_to_all | solution.py:1323
  219.0 0.8 slice_reduce_fusion
  221.4 9.9 %square_terms.1 = (bf16[768,768]{1,0:T(8,128)(2,1)}, bf16[768,768]{1,0:T(8,128)(2,1)}, bf16[768,768]{1,0:T(8,128)(2,1)}, bf16[768,768]{1,0:T(8,128)(2,1)}, bf16[512,768]{1,0:T(8,128)(2,1)}) custom-call(bf16[512,768]{1,0:T(8,128)(2,1)} %get-tuple-element.86.normed, bf16[512,768]{1,0:T(8,128)(2,1)} %get-tuple-element.83.grad_ref.grad_q, ...), custom_call_target="tpu_custom_call" | custom-call | flops 3623878656 | bytes 14155776 | tf_op jit(solution)/shard_map/square_terms/pallas_call | solution.py:689
  231.3 1.9 all-to-all-done.1
  233.2 1.0 copy-done.3
  234.2 40.8 %self_backward.1 = (bf16[2048,256]{1,0:T(8,128)(2,1)}, bf16[2048,256]{1,0:T(8,128)(2,1)}, bf16[2048,256]{1,0:T(8,128)(2,1)}, f32[8,128]{1,0:T(8,128)}, f32[3,24,768]{2,1,0:T(8,128)}, /*index=5*/f32[2,64,768]{2,1,0:T(8,128)}) custom-call(s32[1]{0:T(128)S(6)} %copy.73.refs_0_, bf16[2048,768]{1,0:T(8,128)(2,1)} %get-tuple-element.69.refs_1_.refs_2_.refs_3_, ...), custom_call_target="tpu_custom_call" | custom-call | flops 8053063680 | bytes 8388608 | tf_op jit(solution)/shard_map/self_backward/pallas_call | solution.py:326
  275.0 12.6 %unproject.1 = (bf16[2048,768]{1,0:T(8,128)(2,1)}, bf16[768,768]{1,0:T(8,128)(2,1)}, f32[8,768]{1,0:T(8,128)}) custom-call(bf16[2048,768]{1,0:T(8,128)(2,1)} %bitcast.72, bf16[2048,768]{1,0:T(8,128)(2,1)} %get-tuple-element.91.normed_ref, bf16[768,768]{1,0:T(8,128)(2,1)} %bitcast.75, bf16[2048,256]{1,0:T(8,128)(2,1)} %get-tuple-element.98.dq_ref, ...), custom_call_target="tpu_custom_call" | custom-call | tf_op jit(solution)/shard_map/unproject/pallas_call | solution.py:410
  287.6 0.7 slice.120
  289.3 44.6 %reduce.10 = (f32[24,768]{1,0:T(8,128)}, f32[24,768]{1,0:T(8,128)}, f32[24,768]{1,0:T(8,128)}, f32[24,768]{1,0:T(8,128)}, f32[8,64,768]{2,1,0:T(8,128)}, /*index=5*/f32[8,128]{1,0:T(8,128)}, f32[8,128]{1,0:T(8,128)}) custom-call(bf16[2,2,4,2,24,768]{5,4,3,2,1,0:T(8,128)(2,1)} %bitcast.78, bf16[2,2,4,2,24,768]{5,4,3,2,1,0:T(8,128)(2,1)} %bitcast.79, ...), custom_call_target="tpu_custom_call" | custom-call | tf_op jit(solution)/shard_map/reduce/pallas_call | solution.py:1178
  333.9 1.0 fusion.16
  335.1 1.8 fusion.7
  339.7 3.4 fusion.5
  343.1 1.0 slice.149
  345.1 0.8 fusion.12
  345.8 0.7 copy.74
  (102 shorter events, 14.3 us)
Async XLA Ops:
  7.2 4.6 %copy-start.11 = (f32[24,768]{1,0:T(8,128)S(1)}, f32[24,768]{1,0:T(8,128)}, u32[]{:S(2)}) copy-start(f32[24,768]{1,0:T(8,128)} %param.24) | copy-start | bytes 221188
  7.2 4.7 %copy-start.12 = (f32[24,768]{1,0:T(8,128)S(1)}, f32[24,768]{1,0:T(8,128)}, u32[]{:S(2)}) copy-start(f32[24,768]{1,0:T(8,128)} %param.25) | copy-start | bytes 221188
  7.2 4.7 %copy-start.13 = (f32[24,768]{1,0:T(8,128)S(1)}, f32[24,768]{1,0:T(8,128)}, u32[]{:S(2)}) copy-start(f32[24,768]{1,0:T(8,128)} %param.23) | copy-start | bytes 221188
  7.2 4.7 %copy-start.20 = (f32[3,24]{1,0:T(4,128)S(1)}, f32[3,24]{1,0:T(4,128)}, u32[]{:S(2)}) copy-start(f32[3,24]{1,0:T(4,128)} %param.22) | copy-start | bytes 868
  7.2 146.5 %all-gather.2.cloned.1.call-start = ((), (), s32[]{:S(2)}) async-start(), calls=%async_computation.3 | async-start | bytes 11354112 | tf_op jit(solution)/shard_map/all_gather | solution.py:1241
  11.1 0.7 copy-start.4
  51.6 7.2 %copy-start.19 = (f32[32,3]{0,1:T(4,128)S(1)}, f32[32,3]{0,1:T(4,128)}, u32[]{:S(2)}) copy-start(f32[32,3]{0,1:T(4,128)} %param.34) | copy-start | bytes 1156
  51.6 7.4 %copy-start.21 = (s32[15]{0:T(128)S(1)}, s32[15]{0:T(128)}, u32[]{:S(2)}) copy-start(s32[15]{0:T(128)} %constant.31.clone) | copy-start | bytes 184
  51.6 7.4 %copy-start.7 = (f32[24,768]{1,0:T(8,128)S(1)}, f32[24,768]{1,0:T(8,128)}, u32[]{:S(2)}) copy-start(f32[24,768]{1,0:T(8,128)} %param.29) | copy-start | bytes 221188
  51.6 7.4 %copy-start.8 = (f32[24,768]{1,0:T(8,128)S(1)}, f32[24,768]{1,0:T(8,128)}, u32[]{:S(2)}) copy-start(f32[24,768]{1,0:T(8,128)} %param.28) | copy-start | bytes 221188
  51.7 7.5 %copy-start.9 = (f32[24,768]{1,0:T(8,128)S(1)}, f32[24,768]{1,0:T(8,128)}, u32[]{:S(2)}) copy-start(f32[24,768]{1,0:T(8,128)} %param.27) | copy-start | bytes 221188
  51.7 7.5 %copy-start.10 = (f32[24,768]{1,0:T(8,128)S(1)}, f32[24,768]{1,0:T(8,128)}, u32[]{:S(2)}) copy-start(f32[24,768]{1,0:T(8,128)} %param.26) | copy-start | bytes 221188
  117.2 18.0 %all-to-all-start = ((bf16[4,512,256]{2,1,0:T(8,128)(2,1)}), bf16[4,512,256]{2,1,0:T(8,128)(2,1)S(1)}, u32[]{:S(2)}, u32[]{:S(2)}) async-start(bf16[4,512,256]{2,1,0:T(8,128)(2,1)} %bitcast.80), calls=%async_computation | async-start | bytes 2097152 | tf_op jit(solution)/shard_map/all_to_all | solution.py:1273
  120.8 222.4 %reduce-scatter.2.cloned.1.call-start = ((), (), s32[]{:S(2)}) async-start(), calls=%async_computation.4 | async-start | bytes 10137600 | tf_op jit(solution)/shard_map/reduce_scatter | solution.py:1310
  135.2 1.0 copy-start.1
  180.9 1.1 copy-start
  215.3 17.9 %all-to-all-start.1 = ((bf16[4,512,256]{2,1,0:T(8,128)(2,1)}), bf16[4,512,256]{2,1,0:T(8,128)(2,1)S(1)}, u32[]{:S(2)}, u32[]{:S(2)}) async-start(bf16[4,512,256]{2,1,0:T(8,128)(2,1)} %get-tuple-element.92), calls=%async_computation.1 | async-start | bytes 2097152 | tf_op jit(solution)/shard_map/all_to_all | solution.py:1323
  233.2 1.0 copy-start.3
  333.9 5.1 %copy-start.6 = (f32[3,24,768]{2,1,0:T(8,128)S(1)}, f32[3,24,768]{2,1,0:T(8,128)}, u32[]{:S(2)}) copy-start(f32[3,24,768]{2,1,0:T(8,128)} %get-tuple-element.114) | copy-start | bytes 663556
  343.1 2.7 copy-start.5
  343.1 1.9 copy-start.2
  344.1 2.4 copy-start.18
  344.1 3.1 copy-start.17
  344.1 3.7 %copy-start.16 = (f32[24,768]{1,0:T(8,128)S(1)}, f32[24,768]{1,0:T(8,128)}, u32[]{:S(2)}) copy-start(f32[24,768]{1,0:T(8,128)} %get-tuple-element.167) | copy-start | bytes 221188
  344.3 4.2 %copy-start.15 = (f32[24,768]{1,0:T(8,128)S(1)}, f32[24,768]{1,0:T(8,128)}, u32[]{:S(2)}) copy-start(f32[24,768]{1,0:T(8,128)} %get-tuple-element.168) | copy-start | bytes 221188
  344.3 4.8 %copy-start.14 = (f32[1,24,768]{2,1,0:T(8,128)S(1)}, f32[1,24,768]{2,1,0:T(8,128)}, u32[]{:S(2)}) copy-start(f32[1,24,768]{2,1,0:T(8,128)} %get-tuple-element.115) | copy-start | bytes 221188
Sparse Core Ops, SparseCore 0:
  11.9 112.0 all-gather.1
  181.1 151.9 reduce-scatter.1

commit v6 on v5

--- a/solution.py
+++ b/solution.py
@@ -1193,6 +1193,70 @@
         compiler_params=pltpu.CompilerParams(collective_id=1, has_side_effects=True, vmem_limit_bytes=62 * 2**20),
         name="reduce",
     )(square, own, tok, gain, near)
+
+
+def finish_kernel(
+    slabs, x_ref, attended_ref, normed_ref, rows_ref, share_gain_ref, near_ref, map_ref, ffn_ref, enc_ref, early_ref, last_ref, *refs
+):
+    squares, refs = refs[:4], refs[4:]
+    dx_ref, gain_ref, table_ref, gate_ref, up_ref, down_ref, enc_out = refs[:7]
+    outs = refs[7:]
+    values = x_ref[...].astype(jnp.float32)
+    scale = scale_of(values)
+    unit = values * scale
+    grad_unit = normed_ref[...] * rows_ref[0:1, :]
+    dx_ref[0] = attended_ref[...] + scale * (grad_unit - unit * jnp.mean(grad_unit * unit, axis=-1, keepdims=True))
+
+    @pl.when(pl.program_id(0) == 0)
+    def _():
+        share, inner = gate_ref.shape
+        width = down_ref.shape[1]
+        for n in range(3):
+            gain_ref[n : n + 1, :] = share_gain_ref[0:1, n * share : (n + 1) * share]
+        table = lax.dot_general(
+            map_ref[...], near_ref[...], (((1,), (1,)), ((), ())), precision=highest, preferred_element_type=jnp.float32
+        )
+        table_ref[...] = table[:, : table_ref.shape[1]]
+        gate_ref[...] = ffn_ref[:, :inner].astype(jnp.float32)
+        up_ref[...] = ffn_ref[:, inner : 2 * inner].astype(jnp.float32)
+        for k in range(slabs):
+            size = min(share, down_ref.shape[0] - k * share)
+            column = 2 * inner + k * width
+            down_ref[k * share : k * share + size] = ffn_ref[:size, column : column + width].astype(jnp.float32)
+        enc_out[0] = enc_ref[...]
+        for n, square in enumerate(squares):
+            outs[n][...] = square[...]
+        for n in range(3):
+            outs[4 + n][...] = early_ref[n]
+        outs[7][...] = last_ref[0]
+
+
+def finish(tokens, grad_attended, grad_normed, gains, share_gains, by_distance, share_ffn, grad_encoded, early, last, squares, group, bins, sizes):
+    rows, width = tokens.shape
+    share, inner, hidden_share = sizes
+    block = min(128, rows)
+    place = np.arange(LANES)
+    far = 16 + np.sum(place[:, None] >= bounds[None], axis=1)
+    bucket = np.where(place < 16, place, far)
+    table_map = (bucket[None] == np.arange(bins)[:, None]).astype(np.float32)
+    table_map[bins - 1] = -(bucket < bins - 1).astype(np.float32)
+    by_rows = pl.BlockSpec((block, width), lambda i: (i, 0))
+    fixed = lambda shape: pl.BlockSpec(shape, lambda i: (0,) * len(shape))
+    f32 = lambda *shape: jax.ShapeDtypeStruct(shape, jnp.float32)
+    given = [gains, share_gains, by_distance, jnp.asarray(table_map), share_ffn, grad_encoded, early, last, *squares]
+    made = [
+        f32(3, share), f32(bins, group), f32(share, inner), f32(share, inner), f32(hidden_share, width),
+        f32(1, *grad_encoded.shape), *[f32(share, width)] * 8,
+    ]
+    return pl.pallas_call(
+        functools.partial(finish_kernel, -(-hidden_share // share)),
+        grid=(rows // block,),
+        in_specs=[by_rows] * 3 + [fixed(v.shape) for v in given],
+        out_specs=[pl.BlockSpec((1, block, width), lambda i: (0, i, 0))] + [fixed(v.shape) for v in made],
+        out_shape=[f32(1, rows, width), *made],
+        compiler_params=pltpu.CompilerParams(vmem_limit_bytes=62 * 2**20),
+        name="finish",
+    )(tokens, grad_attended, grad_normed, *given)
 
 
 def rms_norm(values, gain):
@@ -1343,8 +1407,14 @@
             nz, group_width, chunked(grad_output), chunked(grad_own), by_place(grad_normed_part), grad_gains, by_distance
         )
         share_early, grad_encoded = sums
-        share_squares = [share_output, *(share_early[n] for n in range(3)), first_sums[0][0]]
-        grad_normed, grad_encoded = grad_normed.reshape(rows, width), grad_encoded.reshape(-1, width)
+        grad_input, share_gains, table_grad, share_gate, share_up, share_down, grad_encoded, *shares = finish(
+            tokens[0], grad_attended, grad_normed.reshape(rows, width), gain_rows, share_gains, by_distance, share_ffn,
+            grad_encoded.reshape(-1, width), share_early, first_sums[0], (*share_own, share_output),
+            group, rel_bias.shape[0], (share, inner, hidden_share),
+        )
+        return (
+            result[None], grad_input, grad_encoded, share_gains, *shares, share_gate, share_up, share_down, table_grad,
+        )
     else:
         scatter = lambda g, axes: lax.psum_scatter(g, axes, scatter_dimension=0, tiled=True)
         share_squares = scatter(jnp.concatenate([grad_output, *early, grad_coutput], axis=1), both).astype(wide)

time: 358 us -> 349 us (0.975)
  local copies, waits for them, and re-layouts: 17.8 us -> 8.51 us
  Pallas kernels: 292 us -> 299 us
  other arithmetic: 12.2 us -> 5.97 us
    pallas_call x0 -> x1, Pallas kernels: none -> 5.7 us  [finish(): pl.pallas_call(functools.partial(finish_kernel, -(-hidden_share // share)...]
    slice x5 -> x0, local copies, waits for them, and re-layouts: 3.9 us -> none  [the longest x1 0.98 us: per_device(): share_ffn[:, 2 * inner:].reshape(share, slabs, width).transpose(1, 0, 2)]
    unnamed x53 -> x30, local copies, waits for them, and re-layouts: 7.78 us -> 4.11 us
  transfers between devices with their start and end apart: 4 -> 4, of which waited for: 2 -> 2; matrix products, arithmetic and copies ran while one was open for 5% -> 2% of each run, Pallas kernels for 74% -> 77%
where the time goes in v6:
time: 349 us; the launch traced here: 347 us
  Pallas kernels  299 us (86%)
  between operations  15.1 us (4%)
  waiting for transfers between devices  11.5 us (3%)
  local copies, waits for them, and re-layouts  8.51 us (2%)
  starting transfers between devices  7.56 us (2%)
  other arithmetic  5.97 us (2%)
    pallas_call x2, Pallas kernels, attend_forward(): pl.pallas_call(functools.partial(attend_forward_kernel, causal=causal, he...  68.9 us
    pallas_call x2, Pallas kernels, attend_backward(): pl.pallas_call(functools.partial(attend_backward_kernel, causal=causal, h...  68.9 us
    pallas_call x1, Pallas kernels, reduce(): pl.pallas_call(functools.partial(reduce_kernel, nz, group_width), in_spec...  44.6 us
    pallas_call x1, Pallas kernels, gather(): pl.pallas_call(functools.partial(gather_kernel, nz), in_specs=[whole()] *...  37.9 us
    pallas_call x1, Pallas kernels, middle(): pl.pallas_call(functools.partial(middle_kernel, slabs), grid=(steps,), in...  27.2 us
    pallas_call x1, Pallas kernels, unproject(): pl.pallas_call(unproject_kernel, grid=(count // block,), in_specs=[rows(w...  12.3 us
    pallas_call x1, Pallas kernels, square_terms(): pl.pallas_call(functools.partial(square_terms_kernel, group_width), grid=...  10.1 us
    all_to_all x1, waiting for transfers between devices, per_device(): lax.all_to_all(own_mixed.reshape(seq, rows, padded), 'seq', split_axis=0,...  8.85 us
  transfers between devices with their start and end apart: 4, of which 2 were waited for; matrix products, arithmetic and copies ran while one was open for 2% of the time, Pallas kernels for 77%

profile of v6, /device:TPU:0, one launch (start us, length us, event | category | flops | bytes accessed | tf_op | source)
XLA Modules:
  0.0 347.5 jit_solution(15419608980023480247)
XLA Ops:
  7.3 1.0 convert_element_type.55
  8.2 0.9 convert_dynamic-update-slice_fusion.2
  9.2 0.9 convert_dynamic-update-slice_fusion.1
  10.1 0.9 convert_dynamic-update-slice_fusion
  11.1 0.7 copy-done.2
  13.0 0.7 copy.53
  13.6 37.9 %gather.1 = (bf16[2,2,512,768]{3,2,1,0:T(8,128)(2,1)}, bf16[2,2,128,768]{3,2,1,0:T(8,128)(2,1)}, bf16[2,2,4,2,24,768]{5,4,3,2,1,0:T(8,128)(2,1)}) custom-call(bf16[512,768]{1,0:T(8,128)(2,1)} %bitcast.51, bf16[128,768]{1,0:T(8,128)(2,1)} %bitcast.69, bf16[2,2,24,768]{3,2,1,0:T(8,128)(2,1)} %bitcast.65), custom_call_target="tpu_custom_call" | custom-call | tf_op jit(solution)/shard_map/gather/pallas_call | solution.py:1022
  51.6 7.1 %project.1 = (bf16[2048,768]{1,0:T(8,128)(2,1)}, bf16[2048,768]{1,0:T(8,128)(2,1)}, f32[8,768]{1,0:T(8,128)}) custom-call(bf16[2048,768]{1,0:T(8,128)(2,1)} %bitcast.48, bf16[768,768]{1,0:T(8,128)(2,1)} %bitcast.54), custom_call_target="tpu_custom_call" | custom-call | tf_op jit(solution)/shard_map/project/pallas_call | solution.py:366
  59.1 0.7 pad_maximum_fusion.refs_5_
  60.6 56.6 %self_forward.1 = (bf16[2048,256]{1,0:T(8,128)(2,1)}, f32[3,8,2048]{2,1,0:T(8,128)}, bf16[4,2,2,4,2,24,768]{6,5,4,3,2,1,0:T(8,128)(2,1)}) custom-call(s32[1]{0:T(128)S(6)} %copy.59.refs_0_, bf16[2048,768]{1,0:T(8,128)(2,1)} %get-tuple-element.84.refs_1_.refs_2_.refs_3_, bf16[2048,768]{1,0:T(8,128)(2,1)} %get-tuple-element.84.refs_1_.refs_2_.refs_3_, ...), custom_call_target="tpu_custom_call" | custom-call | flops 3221225472 | bytes 4194304 | tf_op jit(solution)/shard_map/self_forward/pallas_call | solution.py:188
  117.2 3.5 %all-to-all-start = ((bf16[4,512,256]{2,1,0:T(8,128)(2,1)}), bf16[4,512,256]{2,1,0:T(8,128)(2,1)S(1)}, u32[]{:S(2)}, u32[]{:S(2)}) async-start(bf16[4,512,256]{2,1,0:T(8,128)(2,1)} %bitcast.60), calls=%async_computation | async-start | bytes 2097152 | tf_op jit(solution)/shard_map/all_to_all | solution.py:1337
  121.6 4.7 %encode.1 = (bf16[512,768]{1,0:T(8,128)(2,1)}, bf16[512,768]{1,0:T(8,128)(2,1)}) custom-call(bf16[512,768]{1,0:T(8,128)(2,1)} %bitcast.63, bf16[4,768,768]{2,1,0:T(8,128)(2,1)} %bitcast.44), custom_call_target="tpu_custom_call" | custom-call | flops 1207959552 | bytes 4718592 | tf_op jit(solution)/shard_map/encode/pallas_call | solution.py:577
  126.3 8.9 %all-to-all-done.mixed_ref.mixed = bf16[4,512,256]{2,1,0:T(8,128)(2,1)S(1)} async-done(((bf16[4,512,256]{2,1,0:T(8,128)(2,1)}), bf16[4,512,256]{2,1,0:T(8,128)(2,1)S(1)}, u32[]{:S(2)}, u32[]{:S(2)}) %all-to-all-start) | async-done | bytes 1048608 | tf_op jit(solution)/shard_map/all_to_all | solution.py:1337
  135.1 1.0 copy-done
  136.1 5.3 %enter.1 = (f32[512,768]{1,0:T(8,128)}, bf16[512,768]{1,0:T(8,128)(2,1)}, bf16[512,768]{1,0:T(8,128)(2,1)}) custom-call(bf16[512,768]{1,0:T(8,128)(2,1)} %bitcast.52, bf16[4,512,256]{2,1,0:T(8,128)(2,1)} %copy-done, bf16[4,768,768]{2,1,0:T(8,128)(2,1)} %bitcast.45, f32[8,768]{1,0:T(8,128)} %get-tuple-element.87.gains_ref.rows_ref), custom_call_target="tpu_custom_call" | custom-call | flops 1207959552 | bytes 7077888 | tf_op jit(solution)/shard_map/enter/pallas_call | solution.py:604
  141.4 12.3 %cross_forward.1 = (bf16[512,768]{1,0:T(8,128)(2,1)}, f32[12,8,512]{2,1,0:T(8,128)}) custom-call(bf16[512,768]{1,0:T(8,128)(2,1)} %get-tuple-element.89.refs_0_, bf16[512,768]{1,0:T(8,128)(2,1)} %get-tuple-element.91.refs_1_, bf16[512,768]{1,0:T(8,128)(2,1)} %get-tuple-element.92.refs_2_), custom_call_target="tpu_custom_call" | custom-call | flops 1610612736 | bytes 3145728 | tf_op jit(solution)/shard_map/cross_forward/pallas_call | solution.py:188
  153.7 27.2 %middle.1 = (bf16[512,768]{1,0:T(8,128)(2,1)}, f32[512,768]{1,0:T(8,128)}, bf16[512,768]{1,0:T(8,128)(2,1)}, bf16[768,768]{1,0:T(8,128)(2,1)}, f32[8,768]{1,0:T(8,128)}, /*index=5*/bf16[32,24,6400]{2,1,0:T(8,128)(2,1)}) custom-call(s32[2]{0:T(128)} %pad_add_fusion.scalars, f32[512,768]{1,0:T(8,128)} %get-tuple-element.88.x1_ref.attended_ref, ...), custom_call_target="tpu_custom_call" | custom-call | flops 16307453952 | bytes 10223616 | tf_op jit(solution)/shard_map/middle/pallas_call | solution.py:534
  181.0 27.0 %cross_backward.1 = (bf16[512,768]{1,0:T(8,128)(2,1)}, bf16[512,768]{1,0:T(8,128)(2,1)}, bf16[512,768]{1,0:T(8,128)(2,1)}, f32[1,24,768]{2,1,0:T(8,128)}) custom-call(bf16[512,768]{1,0:T(8,128)(2,1)} %get-tuple-element.89.refs_0_, bf16[512,768]{1,0:T(8,128)(2,1)} %get-tuple-element.91.refs_1_, bf16[512,768]{1,0:T(8,128)(2,1)} %get-tuple-element.92.refs_2_, ...), custom_call_target="tpu_custom_call" | custom-call | flops 4026531840 | bytes 6291456 | tf_op jit(solution)/shard_map/cross_backward/pallas_call | solution.py:326
  208.0 6.2 %leave.1 = (f32[512,768]{1,0:T(8,128)}, bf16[512,768]{1,0:T(8,128)(2,1)}, bf16[4,512,256]{2,1,0:T(8,128)(2,1)}, f32[8,768]{1,0:T(8,128)}) custom-call(bf16[512,768]{1,0:T(8,128)(2,1)} %get-tuple-element.98.grad_ref.grad_q, bf16[4,768,768]{2,1,0:T(8,128)(2,1)} %bitcast.46, f32[512,768]{1,0:T(8,128)} %get-tuple-element.88.x1_ref.attended_ref, ...), custom_call_target="tpu_custom_call" | custom-call | flops 1207959552 | bytes 9437184 | tf_op jit(solution)/shard_map/leave/pallas_call | solution.py:645
  214.2 3.8 %all-to-all-start.1 = ((bf16[4,512,256]{2,1,0:T(8,128)(2,1)}), bf16[4,512,256]{2,1,0:T(8,128)(2,1)S(1)}, u32[]{:S(2)}, u32[]{:S(2)}) async-start(bf16[4,512,256]{2,1,0:T(8,128)(2,1)} %get-tuple-element.107), calls=%async_computation.1 | async-start | bytes 2097152 | tf_op jit(solution)/shard_map/all_to_all | solution.py:1387
  217.9 0.7 slice.92
  218.7 0.7 slice.91
  219.4 10.1 %square_terms.1 = (bf16[768,768]{1,0:T(8,128)(2,1)}, bf16[768,768]{1,0:T(8,128)(2,1)}, bf16[768,768]{1,0:T(8,128)(2,1)}, bf16[768,768]{1,0:T(8,128)(2,1)}, bf16[512,768]{1,0:T(8,128)(2,1)}) custom-call(bf16[512,768]{1,0:T(8,128)(2,1)} %get-tuple-element.101.normed, bf16[512,768]{1,0:T(8,128)(2,1)} %get-tuple-element.98.grad_ref.grad_q, ...), custom_call_target="tpu_custom_call" | custom-call | flops 3623878656 | bytes 14155776 | tf_op jit(solution)/shard_map/square_terms/pallas_call | solution.py:689
  229.5 2.6 all-to-all-done.1
  232.1 1.0 copy-done.1
  233.1 41.9 %self_backward.1 = (bf16[2048,256]{1,0:T(8,128)(2,1)}, bf16[2048,256]{1,0:T(8,128)(2,1)}, bf16[2048,256]{1,0:T(8,128)(2,1)}, f32[8,128]{1,0:T(8,128)}, f32[3,24,768]{2,1,0:T(8,128)}, /*index=5*/f32[2,64,768]{2,1,0:T(8,128)}) custom-call(s32[1]{0:T(128)S(6)} %copy.59.refs_0_, bf16[2048,768]{1,0:T(8,128)(2,1)} %get-tuple-element.84.refs_1_.refs_2_.refs_3_, ...), custom_call_target="tpu_custom_call" | custom-call | flops 8053063680 | bytes 8388608 | tf_op jit(solution)/shard_map/self_backward/pallas_call | solution.py:326
  275.0 12.3 %unproject.1 = (bf16[2048,768]{1,0:T(8,128)(2,1)}, bf16[768,768]{1,0:T(8,128)(2,1)}, f32[8,768]{1,0:T(8,128)}) custom-call(bf16[2048,768]{1,0:T(8,128)(2,1)} %bitcast.49, bf16[2048,768]{1,0:T(8,128)(2,1)} %get-tuple-element.106.normed_ref, bf16[768,768]{1,0:T(8,128)(2,1)} %bitcast.55, bf16[2048,256]{1,0:T(8,128)(2,1)} %get-tuple-element.113.dq_ref, ...), custom_call_target="tpu_custom_call" | custom-call | tf_op jit(solution)/shard_map/unproject/pallas_call | solution.py:410
  287.3 0.7 slice.90
  288.3 0.7 pad.14.gain
  289.0 44.6 %reduce.3 = (f32[24,768]{1,0:T(8,128)}, f32[24,768]{1,0:T(8,128)}, f32[24,768]{1,0:T(8,128)}, f32[24,768]{1,0:T(8,128)}, f32[8,64,768]{2,1,0:T(8,128)}, /*index=5*/f32[8,128]{1,0:T(8,128)}, f32[8,128]{1,0:T(8,128)}) custom-call(bf16[2,2,4,2,24,768]{5,4,3,2,1,0:T(8,128)(2,1)} %bitcast.58, bf16[2,2,4,2,24,768]{5,4,3,2,1,0:T(8,128)(2,1)} %bitcast.59, ...), custom_call_target="tpu_custom_call" | custom-call | tf_op jit(solution)/shard_map/reduce/pallas_call | solution.py:1178
  333.6 5.7 %finish.1 = (f32[1,512,768]{2,1,0:T(8,128)}, f32[3,24]{1,0:T(4,128)}, f32[32,3]{1,0:T(8,128)}, f32[24,2048]{1,0:T(8,128)}, f32[24,2048]{1,0:T(8,128)}, /*index=5...) custom-call(bf16[512,768]{1,0:T(8,128)(2,1)} %bitcast.53, ...), custom_call_target="tpu_custom_call" | custom-call | tf_op jit(solution)/shard_map/finish/pallas_call | solution.py:1251
  339.3 1.4 copy.50
  (58 shorter events, 2.7 us)
Async XLA Ops:
  7.2 5.3 %copy-start.11 = (f32[3,24]{1,0:T(4,128)S(1)}, f32[3,24]{1,0:T(4,128)}, u32[]{:S(2)}) copy-start(f32[3,24]{1,0:T(4,128)} %param.23) | copy-start | bytes 868
  7.2 5.4 %copy-start.7 = (f32[24,768]{1,0:T(8,128)S(1)}, f32[24,768]{1,0:T(8,128)}, u32[]{:S(2)}) copy-start(f32[24,768]{1,0:T(8,128)} %param.24) | copy-start | bytes 221188
  7.2 5.4 %copy-start.8 = (f32[24,768]{1,0:T(8,128)S(1)}, f32[24,768]{1,0:T(8,128)}, u32[]{:S(2)}) copy-start(f32[24,768]{1,0:T(8,128)} %param.25) | copy-start | bytes 221188
  7.2 5.4 %copy-start.9 = (f32[24,768]{1,0:T(8,128)S(1)}, f32[24,768]{1,0:T(8,128)}, u32[]{:S(2)}) copy-start(f32[24,768]{1,0:T(8,128)} %param.26) | copy-start | bytes 221188
  7.2 146.5 %all-gather.2.cloned.1.call-start = ((), (), s32[]{:S(2)}) async-start(), calls=%async_computation.3 | async-start | bytes 11354112 | tf_op jit(solution)/shard_map/all_gather | solution.py:1305
  11.1 0.7 copy-start.2
  51.6 7.2 %copy-start.10 = (f32[32,3]{0,1:T(4,128)S(1)}, f32[32,3]{0,1:T(4,128)}, u32[]{:S(2)}) copy-start(f32[32,3]{0,1:T(4,128)} %param.35) | copy-start | bytes 1156
  51.6 7.4 %copy-start.12 = (s32[15]{0:T(128)S(1)}, s32[15]{0:T(128)}, u32[]{:S(2)}) copy-start(s32[15]{0:T(128)} %constant.26.clone) | copy-start | bytes 184
  51.6 7.4 %copy-start.3 = (f32[24,768]{1,0:T(8,128)S(1)}, f32[24,768]{1,0:T(8,128)}, u32[]{:S(2)}) copy-start(f32[24,768]{1,0:T(8,128)} %param.28) | copy-start | bytes 221188
  51.6 7.4 %copy-start.4 = (f32[24,768]{1,0:T(8,128)S(1)}, f32[24,768]{1,0:T(8,128)}, u32[]{:S(2)}) copy-start(f32[24,768]{1,0:T(8,128)} %param.27) | copy-start | bytes 221188
  51.6 7.4 %copy-start.5 = (f32[24,768]{1,0:T(8,128)S(1)}, f32[24,768]{1,0:T(8,128)}, u32[]{:S(2)}) copy-start(f32[24,768]{1,0:T(8,128)} %param.30) | copy-start | bytes 221188
  51.6 7.4 %copy-start.6 = (f32[24,768]{1,0:T(8,128)S(1)}, f32[24,768]{1,0:T(8,128)}, u32[]{:S(2)}) copy-start(f32[24,768]{1,0:T(8,128)} %param.29) | copy-start | bytes 221188
  117.2 17.9 %all-to-all-start = ((bf16[4,512,256]{2,1,0:T(8,128)(2,1)}), bf16[4,512,256]{2,1,0:T(8,128)(2,1)S(1)}, u32[]{:S(2)}, u32[]{:S(2)}) async-start(bf16[4,512,256]{2,1,0:T(8,128)(2,1)} %bitcast.60), calls=%async_computation | async-start | bytes 2097152 | tf_op jit(solution)/shard_map/all_to_all | solution.py:1337
  120.7 212.8 %reduce-scatter.2.cloned.1.call-start = ((), (), s32[]{:S(2)}) async-start(), calls=%async_computation.4 | async-start | bytes 10137600 | tf_op jit(solution)/shard_map/reduce_scatter | solution.py:1374
  135.1 1.0 copy-start
  214.2 17.9 %all-to-all-start.1 = ((bf16[4,512,256]{2,1,0:T(8,128)(2,1)}), bf16[4,512,256]{2,1,0:T(8,128)(2,1)S(1)}, u32[]{:S(2)}, u32[]{:S(2)}) async-start(bf16[4,512,256]{2,1,0:T(8,128)(2,1)} %get-tuple-element.107), calls=%async_computation.1 | async-start | bytes 2097152 | tf_op jit(solution)/shard_map/all_to_all | solution.py:1387
  232.1 1.0 copy-start.1
Sparse Core Ops, SparseCore 0:
  11.9 112.2 all-gather.1
  181.1 151.8 reduce-scatter.1

commit v7 on v6

--- a/solution.py
+++ b/solution.py
@@ -156,6 +156,10 @@
         for at in range(0, rows, block):
             o_ref[at : at + block, :] = ot_scr[:, at : at + block].T.astype(low)
 
+    if plan:
+        per_tile = LANES // HEAD
+        for tile in range(-(-heads // per_tile)):
+            pl.when(head == min((tile + 1) * per_tile, heads) - 1)(functools.partial(plan.send, tile, o_ref))
     at_end(head, heads, stages)
 
 
@@ -779,29 +783,33 @@
 
 
 class GatherPlan:
-    inputs, outputs = 1, 1
-
-    def __init__(self, nz, count, share, width):
-        self.nz, self.count, self.share, self.width = nz, count, share, width
-        self.total = 8 * nz - 1
+    inputs, outputs = 1, 2
+
+    def __init__(self, nz, count, share, width, rows, tiles):
+        self.nz, self.count, self.share, self.width, self.rows, self.tiles = nz, count, share, width, rows, tiles
+        self.total = 8 * nz - 1 + 3 * tiles
 
     def in_specs(self):
         return [whole()]
 
     def out_specs(self):
-        return [whole(pl.ANY)]
+        return [whole(pl.ANY)] * 2
 
     def out_shape(self):
-        return [jax.ShapeDtypeStruct((self.count, 2, 2, self.nz, 2, self.share, self.width), low)]
+        return [
+            jax.ShapeDtypeStruct((self.count, 2, 2, self.nz, 2, self.share, self.width), low),
+            jax.ShapeDtypeStruct((2, 2, self.rows, self.tiles * LANES), low),
+        ]
 
     def scratch(self):
-        return [pltpu.SemaphoreType.DMA((self.total,)), pltpu.SemaphoreType.DMA((self.total,)), pltpu.SemaphoreType.DMA((1,))]
+        sems = [pltpu.SemaphoreType.DMA((n,)) for n in (self.total, self.total, 1 + self.tiles)]
+        return [pltpu.VMEM((self.tiles, 2, 2, self.rows, LANES), low), *sems]
 
     def params(self):
         return pltpu.CompilerParams(collective_id=2, has_side_effects=True, vmem_limit_bytes=62 * 2**20)
 
     def stages(self, given, made, scratch):
-        (src,), (out,), (send_sem, recv_sem, local_sem) = given, made, scratch
+        (src,), (out, got), (parts, send_sem, recv_sem, local_sem) = given, made, scratch
         nz, my = self.nz, Near(self.nz)
         x, c, z, y, backs = my.x, my.c, my.z, my.y, my.backs
         copies = Copies(send_sem, recv_sem)
@@ -825,9 +833,27 @@
         core_y = [copies.add(from_y[t], from_y[t], my.by_core) for t in range(nz)]
         core_far = [copies.add(far[t], far[t], my.by_core) for t in range(nz)]
         local = lambda: pltpu.make_async_copy(src, mine(), local_sem.at[0])
+        lands = [lambda t=t: got.at[x, c, :, t * LANES : (t + 1) * LANES] for t in range(self.tiles)]
+        exchange = [
+            [
+                copies.add(lambda t=t: parts.at[t, 1 - x, c], lands[t], my.by_x),
+                copies.add(lambda t=t: parts.at[t, x, 1 - c], lands[t], my.by_core),
+                copies.add(lambda t=t: parts.at[t, 1 - x, 1 - c], lands[t], my.diagonal),
+            ]
+            for t in range(self.tiles)
+        ]
+        keep = lambda t: pltpu.make_async_copy(parts.at[t, x, c], lands[t](), local_sem.at[1 + t])
+
+        def send(tile, mixed):
+            for s in range(4):
+                parts[tile, s // 2, s % 2] = mixed[s * self.rows : (s + 1) * self.rows, :]
+            copies.start(*exchange[tile])
+            keep(tile).start()
+
+        self.send = send
 
         def begin():
-            greet([my.by_x, my.by_core, my.by_y, *my.by_z[1:]])
+            greet([my.by_x, my.by_core, my.diagonal, my.by_y, *my.by_z[1:]])
             copies.start(*by_z[1:], by_y[0], by_x[0], by_core[0])
             local().start()
 
@@ -848,6 +874,9 @@
         def end():
             local().wait()
             copies.arrive(*by_core, *core_x, *core_y, *core_far)
+            for tile in range(self.tiles):
+                copies.arrive(*exchange[tile])
+                keep(tile).wait()
             copies.finish()
 
         work = [functools.partial(line, t) for t in range(1, nz)]
@@ -1328,13 +1357,16 @@
     values_in = tokens[0].astype(jnp.float32)
     qkv, normed_all, gain_rows = project(everyone, w_qkv, group_width)
     bias = bias_rows(rel_bias)
-    plan = GatherPlan(nz, 4, share, width) if aligned else None
+    plan = GatherPlan(nz, 4, share, width, rows, padded // LANES) if aligned else None
     own_mixed, own_logsum, *gathered = attend_forward(
         qkv, qkv, qkv, group, padded, bias, lengths, plan, (squares,) if aligned else ()
     )
     squares = gathered[0] if aligned else jnp.moveaxis(lax.all_gather(squares, both, axis=0), 1, 0)
     squares = squares.reshape(4, width, width)
-    mixed = lax.all_to_all(own_mixed.reshape(seq, rows, padded), "seq", split_axis=0, concat_axis=0, tiled=True)
+    if aligned:
+        mixed = gathered[1].reshape(seq, rows, padded)
+    else:
+        mixed = lax.all_to_all(own_mixed.reshape(seq, rows, padded), "seq", split_axis=0, concat_axis=0, tiled=True)
     cross_keys, cross_values = encode(encoded, squares)
     attended, normed_two, cross_queries = enter(tokens[0], mixed, squares, gain_rows, group_width)
     cross_mixed, cross_logsum = attend_forward(cross_queries, cross_keys, cross_values, heads)

time: 349 us -> 343 us (0.983)
  waiting for transfers between devices: 11.5 us -> 2.68 us
  Pallas kernels: 299 us -> 307 us
  starting transfers between devices: 7.56 us -> 3.82 us
    all_to_all x1 -> x0, waiting for transfers between devices: 8.85 us -> none  [per_device(): lax.all_to_all(own_mixed.reshape(seq, rows, padded), 'seq', split_axis=0,...]
    pallas_call x2, Pallas kernels: 68.9 us -> 75.5 us  [attend_forward(): pl.pallas_call(functools.partial(attend_forward_kernel, causal=causal, he...]
    all_to_all x1 -> x0, starting transfers between devices: 3.54 us -> none  [per_device(): lax.all_to_all(own_mixed.reshape(seq, rows, padded), 'seq', split_axis=0,...]
  transfers between devices with their start and end apart: 4 -> 3, of which waited for: 2 -> 1; matrix products, arithmetic and copies ran while one was open for 2% -> 2% of each run, Pallas kernels for 77% -> 80%
where the time goes in v7:
time: 343 us; the launch traced here: 342 us
  Pallas kernels  307 us (90%)
  between operations  15 us (4%)
  local copies, waits for them, and re-layouts  7.53 us (2%)
  other arithmetic  5.97 us (2%)
  starting transfers between devices  3.82 us (1%)
    pallas_call x2, Pallas kernels, attend_forward(): pl.pallas_call(functools.partial(attend_forward_kernel, causal=causal, he...  75.5 us
    pallas_call x2, Pallas kernels, attend_backward(): pl.pallas_call(functools.partial(attend_backward_kernel, causal=causal, h...  70.4 us
    pallas_call x1, Pallas kernels, reduce(): pl.pallas_call(functools.partial(reduce_kernel, nz, group_width), in_spec...  44.6 us
    pallas_call x1, Pallas kernels, gather(): pl.pallas_call(functools.partial(gather_kernel, nz), in_specs=[whole()] *...  38 us
    pallas_call x1, Pallas kernels, middle(): pl.pallas_call(functools.partial(middle_kernel, slabs), grid=(steps,), in...  27.4 us
    pallas_call x1, Pallas kernels, unproject(): pl.pallas_call(unproject_kernel, grid=(count // block,), in_specs=[rows(w...  12.3 us
    pallas_call x1, Pallas kernels, square_terms(): pl.pallas_call(functools.partial(square_terms_kernel, group_width), grid=...  10.1 us
    pallas_call x1, Pallas kernels, project(): pl.pallas_call(functools.partial(project_kernel, gain_lane), grid=(count...  7.09 us
  transfers between devices with their start and end apart: 3, of which 1 were waited for; matrix products, arithmetic and copies ran while one was open for 2% of the time, Pallas kernels for 80%

profile of v7, /device:TPU:0, one launch (start us, length us, event | category | flops | bytes accessed | tf_op | source)
XLA Modules:
  0.0 342.4 jit_solution(11221089796709976138)
XLA Ops:
  7.3 1.0 convert_element_type.55
  8.2 0.9 convert_dynamic-update-slice_fusion.2
  9.2 0.9 convert_dynamic-update-slice_fusion.1
  10.1 0.9 convert_dynamic-update-slice_fusion
  11.1 0.7 copy-done.1
  13.0 0.7 copy.53
  13.7 38.0 %gather.1 = (bf16[2,2,512,768]{3,2,1,0:T(8,128)(2,1)}, bf16[2,2,128,768]{3,2,1,0:T(8,128)(2,1)}, bf16[2,2,4,2,24,768]{5,4,3,2,1,0:T(8,128)(2,1)}) custom-call(bf16[512,768]{1,0:T(8,128)(2,1)} %bitcast.51, bf16[128,768]{1,0:T(8,128)(2,1)} %bitcast.70, bf16[2,2,24,768]{3,2,1,0:T(8,128)(2,1)} %bitcast.66), custom_call_target="tpu_custom_call" | custom-call | tf_op jit(solution)/shard_map/gather/pallas_call | solution.py:1051
  51.8 7.1 %project.1 = (bf16[2048,768]{1,0:T(8,128)(2,1)}, bf16[2048,768]{1,0:T(8,128)(2,1)}, f32[8,768]{1,0:T(8,128)}) custom-call(bf16[2048,768]{1,0:T(8,128)(2,1)} %bitcast.48, bf16[768,768]{1,0:T(8,128)(2,1)} %bitcast.54), custom_call_target="tpu_custom_call" | custom-call | tf_op jit(solution)/shard_map/project/pallas_call | solution.py:370
  58.9 0.6 pad_add_fusion.scalars
  59.4 0.2 slice_reduce_fusion
  59.8 0.7 pad_maximum_fusion.refs_5_
  60.7 0.6 broadcast_select_fusion.refs_4_.refs_7_
  61.3 63.2 %self_forward.1 = (bf16[2048,256]{1,0:T(8,128)(2,1)}, f32[3,8,2048]{2,1,0:T(8,128)}, bf16[4,2,2,4,2,24,768]{6,5,4,3,2,1,0:T(8,128)(2,1)}, bf16[2,2,512,256]{3,2,1,0:T(8,128)(2,1)}) custom-call(s32[1]{0:T(128)S(6)} %copy.59.refs_0_, bf16[2048,768]{1,0:T(8,128)(2,1)} %get-tuple-element.85.refs_1_.refs_2_.refs_3_, ...), custom_call_target="tpu_custom_call" | custom-call | flops 3221225472 | bytes 4194304 | tf_op jit(solution)/shard_map/self_forward/pallas_call | solution.py:192
  124.5 4.7 %encode.1 = (bf16[512,768]{1,0:T(8,128)(2,1)}, bf16[512,768]{1,0:T(8,128)(2,1)}) custom-call(bf16[512,768]{1,0:T(8,128)(2,1)} %bitcast.64, bf16[4,768,768]{2,1,0:T(8,128)(2,1)} %bitcast.44), custom_call_target="tpu_custom_call" | custom-call | flops 1207959552 | bytes 4718592 | tf_op jit(solution)/shard_map/encode/pallas_call | solution.py:581
  129.2 5.3 %enter.1 = (f32[512,768]{1,0:T(8,128)}, bf16[512,768]{1,0:T(8,128)(2,1)}, bf16[512,768]{1,0:T(8,128)(2,1)}) custom-call(bf16[512,768]{1,0:T(8,128)(2,1)} %bitcast.52, bf16[4,512,256]{2,1,0:T(8,128)(2,1)} %bitcast.60, bf16[4,768,768]{2,1,0:T(8,128)(2,1)} %bitcast.45, f32[8,768]{1,0:T(8,128)} %get-tuple-element.88.gains_ref.rows_ref), custom_call_target="tpu_custom_call" | custom-call | flops 1207959552 | bytes 7077888 | tf_op jit(solution)/shard_map/enter/pallas_call | solution.py:608
  134.5 12.3 %cross_forward.1 = (bf16[512,768]{1,0:T(8,128)(2,1)}, f32[12,8,512]{2,1,0:T(8,128)}) custom-call(bf16[512,768]{1,0:T(8,128)(2,1)} %get-tuple-element.90.refs_0_, bf16[512,768]{1,0:T(8,128)(2,1)} %get-tuple-element.92.refs_1_, bf16[512,768]{1,0:T(8,128)(2,1)} %get-tuple-element.93.refs_2_), custom_call_target="tpu_custom_call" | custom-call | flops 1610612736 | bytes 3145728 | tf_op jit(solution)/shard_map/cross_forward/pallas_call | solution.py:192
  146.8 27.4 %middle.1 = (bf16[512,768]{1,0:T(8,128)(2,1)}, f32[512,768]{1,0:T(8,128)}, bf16[512,768]{1,0:T(8,128)(2,1)}, bf16[768,768]{1,0:T(8,128)(2,1)}, f32[8,768]{1,0:T(8,128)}, /*index=5*/bf16[32,24,6400]{2,1,0:T(8,128)(2,1)}) custom-call(s32[2]{0:T(128)} %pad_add_fusion.scalars, f32[512,768]{1,0:T(8,128)} %get-tuple-element.89.x1_ref.attended_ref, ...), custom_call_target="tpu_custom_call" | custom-call | flops 16307453952 | bytes 10223616 | tf_op jit(solution)/shard_map/middle/pallas_call | solution.py:538
  174.2 26.6 %cross_backward.1 = (bf16[512,768]{1,0:T(8,128)(2,1)}, bf16[512,768]{1,0:T(8,128)(2,1)}, bf16[512,768]{1,0:T(8,128)(2,1)}, f32[1,24,768]{2,1,0:T(8,128)}) custom-call(bf16[512,768]{1,0:T(8,128)(2,1)} %get-tuple-element.90.refs_0_, bf16[512,768]{1,0:T(8,128)(2,1)} %get-tuple-element.92.refs_1_, bf16[512,768]{1,0:T(8,128)(2,1)} %get-tuple-element.93.refs_2_, ...), custom_call_target="tpu_custom_call" | custom-call | flops 4026531840 | bytes 6291456 | tf_op jit(solution)/shard_map/cross_backward/pallas_call | solution.py:330
  200.9 6.2 %leave.1 = (f32[512,768]{1,0:T(8,128)}, bf16[512,768]{1,0:T(8,128)(2,1)}, bf16[4,512,256]{2,1,0:T(8,128)(2,1)}, f32[8,768]{1,0:T(8,128)}) custom-call(bf16[512,768]{1,0:T(8,128)(2,1)} %get-tuple-element.99.grad_ref.grad_q, bf16[4,768,768]{2,1,0:T(8,128)(2,1)} %bitcast.46, f32[512,768]{1,0:T(8,128)} %get-tuple-element.89.x1_ref.attended_ref, ...), custom_call_target="tpu_custom_call" | custom-call | flops 1207959552 | bytes 9437184 | tf_op jit(solution)/shard_map/leave/pallas_call | solution.py:649
  207.1 3.7 %all-to-all-start = ((bf16[4,512,256]{2,1,0:T(8,128)(2,1)}), bf16[4,512,256]{2,1,0:T(8,128)(2,1)S(1)}, u32[]{:S(2)}, u32[]{:S(2)}) async-start(bf16[4,512,256]{2,1,0:T(8,128)(2,1)} %get-tuple-element.108), calls=%async_computation | async-start | bytes 2097152 | tf_op jit(solution)/shard_map/all_to_all | solution.py:1419
  210.9 0.7 slice.92
  211.6 0.7 slice.91
  212.4 10.1 %square_terms.1 = (bf16[768,768]{1,0:T(8,128)(2,1)}, bf16[768,768]{1,0:T(8,128)(2,1)}, bf16[768,768]{1,0:T(8,128)(2,1)}, bf16[768,768]{1,0:T(8,128)(2,1)}, bf16[512,768]{1,0:T(8,128)(2,1)}) custom-call(bf16[512,768]{1,0:T(8,128)(2,1)} %get-tuple-element.102.normed, bf16[512,768]{1,0:T(8,128)(2,1)} %get-tuple-element.99.grad_ref.grad_q, ...), custom_call_target="tpu_custom_call" | custom-call | flops 3623878656 | bytes 14155776 | tf_op jit(solution)/shard_map/square_terms/pallas_call | solution.py:693
  222.4 2.6 all-to-all-done
  225.0 1.0 copy-done
  226.0 43.8 %self_backward.1 = (bf16[2048,256]{1,0:T(8,128)(2,1)}, bf16[2048,256]{1,0:T(8,128)(2,1)}, bf16[2048,256]{1,0:T(8,128)(2,1)}, f32[8,128]{1,0:T(8,128)}, f32[3,24,768]{2,1,0:T(8,128)}, /*index=5*/f32[2,64,768]{2,1,0:T(8,128)}) custom-call(s32[1]{0:T(128)S(6)} %copy.59.refs_0_, bf16[2048,768]{1,0:T(8,128)(2,1)} %get-tuple-element.85.refs_1_.refs_2_.refs_3_, ...), custom_call_target="tpu_custom_call" | custom-call | flops 8053063680 | bytes 8388608 | tf_op jit(solution)/shard_map/self_backward/pallas_call | solution.py:330
  269.8 12.3 %unproject.1 = (bf16[2048,768]{1,0:T(8,128)(2,1)}, bf16[768,768]{1,0:T(8,128)(2,1)}, f32[8,768]{1,0:T(8,128)}) custom-call(bf16[2048,768]{1,0:T(8,128)(2,1)} %bitcast.49, bf16[2048,768]{1,0:T(8,128)(2,1)} %get-tuple-element.107.normed_ref, bf16[768,768]{1,0:T(8,128)(2,1)} %bitcast.55, bf16[2048,256]{1,0:T(8,128)(2,1)} %get-tuple-element.115.dq_ref, ...), custom_call_target="tpu_custom_call" | custom-call | tf_op jit(solution)/shard_map/unproject/pallas_call | solution.py:414
  282.1 0.7 slice.90
  283.1 0.7 pad.14.gain
  283.8 44.6 %reduce.3 = (f32[24,768]{1,0:T(8,128)}, f32[24,768]{1,0:T(8,128)}, f32[24,768]{1,0:T(8,128)}, f32[24,768]{1,0:T(8,128)}, f32[8,64,768]{2,1,0:T(8,128)}, /*index=5*/f32[8,128]{1,0:T(8,128)}, f32[8,128]{1,0:T(8,128)}) custom-call(bf16[2,2,4,2,24,768]{5,4,3,2,1,0:T(8,128)(2,1)} %bitcast.58, bf16[2,2,4,2,24,768]{5,4,3,2,1,0:T(8,128)(2,1)} %bitcast.59, ...), custom_call_target="tpu_custom_call" | custom-call | tf_op jit(solution)/shard_map/reduce/pallas_call | solution.py:1207
  328.5 5.7 %finish.1 = (f32[1,512,768]{2,1,0:T(8,128)}, f32[3,24]{1,0:T(4,128)}, f32[32,3]{1,0:T(8,128)}, f32[24,2048]{1,0:T(8,128)}, f32[24,2048]{1,0:T(8,128)}, /*index=5...) custom-call(bf16[512,768]{1,0:T(8,128)(2,1)} %bitcast.53, ...), custom_call_target="tpu_custom_call" | custom-call | tf_op jit(solution)/shard_map/finish/pallas_call | solution.py:1280
  334.2 1.4 copy.50
  (54 shorter events, 1.2 us)
Async XLA Ops:
  7.2 5.3 %copy-start.10 = (f32[3,24]{1,0:T(4,128)S(1)}, f32[3,24]{1,0:T(4,128)}, u32[]{:S(2)}) copy-start(f32[3,24]{1,0:T(4,128)} %param.23) | copy-start | bytes 868
  7.2 5.4 %copy-start.6 = (f32[24,768]{1,0:T(8,128)S(1)}, f32[24,768]{1,0:T(8,128)}, u32[]{:S(2)}) copy-start(f32[24,768]{1,0:T(8,128)} %param.24) | copy-start | bytes 221188
  7.2 5.5 %copy-start.7 = (f32[24,768]{1,0:T(8,128)S(1)}, f32[24,768]{1,0:T(8,128)}, u32[]{:S(2)}) copy-start(f32[24,768]{1,0:T(8,128)} %param.25) | copy-start | bytes 221188
  7.2 5.5 %copy-start.8 = (f32[24,768]{1,0:T(8,128)S(1)}, f32[24,768]{1,0:T(8,128)}, u32[]{:S(2)}) copy-start(f32[24,768]{1,0:T(8,128)} %param.26) | copy-start | bytes 221188
  7.2 139.6 %all-gather.2.cloned.1.call-start = ((), (), s32[]{:S(2)}) async-start(), calls=%async_computation.2 | async-start | bytes 11354112 | tf_op jit(solution)/shard_map/all_gather | solution.py:1334
  11.1 0.7 copy-start.1
  11.8 316.7 %reduce-scatter.2.cloned.1.call-start = ((), (), s32[]{:S(2)}) async-start(), calls=%async_computation.3 | async-start | bytes 10137600 | tf_op jit(solution)/shard_map/reduce_scatter | solution.py:1406
  51.7 7.8 %copy-start.9 = (f32[32,3]{0,1:T(4,128)S(1)}, f32[32,3]{0,1:T(4,128)}, u32[]{:S(2)}) copy-start(f32[32,3]{0,1:T(4,128)} %param.35) | copy-start | bytes 1156
  51.7 7.9 %copy-start.11 = (s32[15]{0:T(128)S(1)}, s32[15]{0:T(128)}, u32[]{:S(2)}) copy-start(s32[15]{0:T(128)} %constant.26.clone) | copy-start | bytes 184
  51.7 8.0 %copy-start.2 = (f32[24,768]{1,0:T(8,128)S(1)}, f32[24,768]{1,0:T(8,128)}, u32[]{:S(2)}) copy-start(f32[24,768]{1,0:T(8,128)} %param.28) | copy-start | bytes 221188
  51.7 8.0 %copy-start.3 = (f32[24,768]{1,0:T(8,128)S(1)}, f32[24,768]{1,0:T(8,128)}, u32[]{:S(2)}) copy-start(f32[24,768]{1,0:T(8,128)} %param.27) | copy-start | bytes 221188
  51.7 8.0 %copy-start.4 = (f32[24,768]{1,0:T(8,128)S(1)}, f32[24,768]{1,0:T(8,128)}, u32[]{:S(2)}) copy-start(f32[24,768]{1,0:T(8,128)} %param.30) | copy-start | bytes 221188
  51.7 8.0 %copy-start.5 = (f32[24,768]{1,0:T(8,128)S(1)}, f32[24,768]{1,0:T(8,128)}, u32[]{:S(2)}) copy-start(f32[24,768]{1,0:T(8,128)} %param.29) | copy-start | bytes 221188
  207.1 17.9 %all-to-all-start = ((bf16[4,512,256]{2,1,0:T(8,128)(2,1)}), bf16[4,512,256]{2,1,0:T(8,128)(2,1)S(1)}, u32[]{:S(2)}, u32[]{:S(2)}) async-start(bf16[4,512,256]{2,1,0:T(8,128)(2,1)} %get-tuple-element.108), calls=%async_computation | async-start | bytes 2097152 | tf_op jit(solution)/shard_map/all_to_all | solution.py:1419
  225.0 1.0 copy-start
Sparse Core Ops, SparseCore 0:
  11.9 113.4 all-gather.1
  174.4 153.1 reduce-scatter.1
